TPU v7x, 32 devices: a whole 2x2x4 slice. The times are simulated.
32 devices in a mesh: dp: 4 (over z), fsdp: 8 (over y, x, core).
Axes of the slice: x: 2, y: 2, z: 4, core: 2. Of those that a mesh axis runs over, the one named last changes fastest.
Arguments:
- tokens: bfloat16 [32, 512, 1024], P(('dp', 'fsdp')), may hold values from -6 to 6
- memory: bfloat16 [32, 512, 1024], P(('dp', 'fsdp')), may hold values from -6 to 6
- compressed: bfloat16 [32, 512, 1024], P(('dp', 'fsdp')), may hold values from -6 to 6
- mem_fill: int32 [32], P(('dp', 'fsdp')), may hold values from 0 to 512, as said below
- cmem_fill: int32 [32], P(('dp', 'fsdp')), may hold values from 0 to 512, as said below
- pad_mask: int32 [32, 512], P(('dp', 'fsdp')), may hold values from 0 to 1, as said below
- first_gain: bfloat16 [1024], P('fsdp'), may hold values from 0.5 to 1.5
- first_shift: bfloat16 [1024], P('fsdp'), may hold values from -1.5 to 1.5
- query_weight: bfloat16 [1024, 1024], P('fsdp'), may hold values from -0.1875 to 0.1875
- key_weight: bfloat16 [1024, 1024], P('fsdp'), may hold values from -0.1875 to 0.1875
- value_weight: bfloat16 [1024, 1024], P('fsdp'), may hold values from -0.1875 to 0.1875
- position_weight: bfloat16 [1024, 1024], P('fsdp'), may hold values from -0.1875 to 0.1875
- content_bias: bfloat16 [1024], P('fsdp'), may hold values from -3 to 3
- position_bias: bfloat16 [1024], P('fsdp'), may hold values from -3 to 3
- output_weight: bfloat16 [1024, 1024], P('fsdp'), may hold values from -0.75 to 0.75
- second_gain: bfloat16 [1024], P('fsdp'), may hold values from 0.5 to 1.5
- second_shift: bfloat16 [1024], P('fsdp'), may hold values from -1.5 to 1.5
- inner_weight: bfloat16 [1024, 4096], P('fsdp'), may hold values from -0.1875 to 0.1875
- inner_bias: bfloat16 [4096], P('fsdp'), may hold values from -3 to 3
- outer_weight: bfloat16 [4096, 1024], P('fsdp'), may hold values from -0.125 to 0.125
- outer_bias: bfloat16 [1024], P('fsdp'), may hold values from -3 to 3
- conv_weight: bfloat16 [3072, 1024], P('fsdp'), may hold values from -0.109375 to 0.109375
- conv_bias: bfloat16 [1024], P('fsdp'), may hold values from -3 to 3
- out_grad: bfloat16 [32, 512, 1024], P(('dp', 'fsdp')), may hold values from -6 to 6
- comp_grad: bfloat16 [32, 170, 1024], P(('dp', 'fsdp')), may hold values from -6 to 6
Outputs:
- out_tokens: bfloat16 [32, 512, 1024], P(('dp', 'fsdp'))
- token_gradient: float32 [32, 512, 1024], P(('dp', 'fsdp'))
- new_compressed: bfloat16 [32, 170, 1024], P(('dp', 'fsdp'))
- first_gain_gradient: float32 [1024], P('fsdp')
- first_shift_gradient: float32 [1024], P('fsdp')
- query_gradient: float32 [1024, 1024], P('fsdp')
- key_gradient: float32 [1024, 1024], P('fsdp')
- value_gradient: float32 [1024, 1024], P('fsdp')
- position_gradient: float32 [1024, 1024], P('fsdp')
- content_bias_gradient: float32 [1024], P('fsdp')
- position_bias_gradient: float32 [1024], P('fsdp')
- output_gradient: float32 [1024, 1024], P('fsdp')
- second_gain_gradient: float32 [1024], P('fsdp')
- second_shift_gradient: float32 [1024], P('fsdp')
- inner_gradient: float32 [1024, 4096], P('fsdp')
- inner_bias_gradient: float32 [4096], P('fsdp')
- outer_gradient: float32 [4096, 1024], P('fsdp')
- outer_bias_gradient: float32 [1024], P('fsdp')
- conv_gradient: float32 [3072, 1024], P('fsdp')
- conv_bias_gradient: float32 [1024], P('fsdp')
Inputs may be any that keep to these rules, and one draw needn't show every extreme that they name: The valid memory rows of a stream are its last mem_fill rows; in every draw some stream has a full memory. The valid compressed rows of a stream are its last cmem_fill rows; in every draw some stream has a full compressed memory. `pad_mask`: each stream's real tokens are a prefix of one or more tokens; in every draw some stream has no padding.
All inputs are finite; a program needn't handle non-finite values.
Results may differ from a plain program's by a relative error of at most 0.022.
Values may be sent and summed in bfloat16 or wider, within the bound.
A program may use at most 256 MiB of HBM per device.

v0:
```python
import math

import jax
import jax.numpy as jnp
from jax import lax
from jax.sharding import PartitionSpec as P

HEADS = 8
DH = 128
RATE = 3


EPSILON = 1e-05
MASKED = -1000000000.0


def smooth_gate(values):
    return jax.nn.gelu(values, approximate=True)


def norm_parts(rows, gain, shift):
    center = jnp.mean(rows, axis=-1, keepdims=True)
    centered = rows - center
    spread = lax.rsqrt(jnp.mean(centered * centered, axis=-1, keepdims=True) + EPSILON)
    scaled = centered * spread
    return (scaled * gain.astype(jnp.float32) + shift.astype(jnp.float32), scaled, spread)


def norm_back(grad, scaled, spread, gain):
    inner = grad * gain.astype(jnp.float32)
    return spread * (
        inner
        - jnp.mean(inner, axis=-1, keepdims=True)
        - scaled * jnp.mean(inner * scaled, axis=-1, keepdims=True)
    )


def positions(count, width):
    distance = (count - 1 - jnp.arange(count, dtype=jnp.int32)).astype(jnp.float32)
    rates = jnp.exp(
        jnp.arange(0, width, 2, dtype=jnp.int32).astype(jnp.float32) * (-math.log(10000.0) / width)
    )
    angle = distance[:, None] * rates[None, :]
    return jnp.concatenate([jnp.sin(angle), jnp.cos(angle)], axis=1)


def rel_shift(table):
    leading, rows, cols = table.shape
    padded = jnp.pad(table, ((0, 0), (0, 0), (1, 0)))
    folded = padded.reshape(leading, cols + 1, rows)
    return folded[:, 1:, :].reshape(leading, rows, cols)


def shift_back(grad):
    pull = jax.vjp(rel_shift, grad)[1]
    return pull(grad)[0]


def key_mask(mem_fill, cmem_fill, pad_mask, cmem_rows, mem_rows):
    seg_rows = pad_mask.shape[-1]
    comp_valid = jnp.arange(cmem_rows, dtype=jnp.int32)[None, :] >= (cmem_rows - cmem_fill)[:, None]
    mem_valid = jnp.arange(mem_rows, dtype=jnp.int32)[None, :] >= (mem_rows - mem_fill)[:, None]
    keyvalid = jnp.concatenate([comp_valid, mem_valid, pad_mask == 1], axis=1)
    column = jnp.arange(cmem_rows + mem_rows + seg_rows, dtype=jnp.int32)[None, :]
    own = (cmem_rows + mem_rows + jnp.arange(seg_rows, dtype=jnp.int32))[:, None]
    return (column <= own)[None] & (keyvalid[:, None, :] | (column == own)[None])


def to_heads(array):
    return jnp.moveaxis(array.reshape(array.shape[:-1] + (HEADS, DH)), -2, 0)


def from_heads(array):
    return jnp.moveaxis(array, 0, -2).reshape(array.shape[1:-1] + (HEADS * DH,))


def per_device(
    tokens,
    memory,
    compressed,
    mem_fill,
    cmem_fill,
    pad_mask,
    first_gain,
    first_shift,
    query_weight,
    key_weight,
    value_weight,
    position_weight,
    content_bias,
    position_bias,
    output_weight,
    second_gain,
    second_shift,
    inner_weight,
    inner_bias,
    outer_weight,
    outer_bias,
    conv_weight,
    conv_bias,
    out_grad,
    comp_grad,
):
    f32 = jnp.float32
    bf16 = jnp.bfloat16
    streams, seg_rows, width = tokens.shape
    mem_rows = memory.shape[1]
    cmem_rows = compressed.shape[1]
    total = cmem_rows + mem_rows + seg_rows
    scale = 1.0 / math.sqrt(DH)
    share = 1.0 / (streams * lax.axis_size("dp") * lax.axis_size("fsdp"))
    (
        full_first_gain,
        full_first_shift,
        full_query,
        full_keys,
        full_values,
        full_position,
        full_content,
        full_posbias,
        full_output,
    ) = (
        lax.all_gather(first_gain, "fsdp", axis=0, tiled=True),
        lax.all_gather(first_shift, "fsdp", axis=0, tiled=True),
        lax.all_gather(query_weight, "fsdp", axis=0, tiled=True),
        lax.all_gather(key_weight, "fsdp", axis=0, tiled=True),
        lax.all_gather(value_weight, "fsdp", axis=0, tiled=True),
        lax.all_gather(position_weight, "fsdp", axis=0, tiled=True),
        lax.all_gather(content_bias, "fsdp", axis=0, tiled=True),
        lax.all_gather(position_bias, "fsdp", axis=0, tiled=True),
        lax.all_gather(output_weight, "fsdp", axis=0, tiled=True),
    )
    allowed = key_mask(mem_fill, cmem_fill, pad_mask, cmem_rows, mem_rows)
    whole = jnp.concatenate([compressed, memory, tokens], axis=1).astype(f32)
    normed, scaled_one, spread_one = norm_parts(whole, full_first_gain, full_first_shift)
    normed_low = normed.astype(bf16)
    own_rows = normed_low[:, total - seg_rows :]
    query = jnp.einsum("bsd,de->bse", own_rows, full_query, preferred_element_type=f32)
    query_u = (query + full_content.astype(f32)).astype(bf16)
    query_v = (query + full_posbias.astype(f32)).astype(bf16)
    keys = jnp.einsum("bsd,de->bse", normed_low, full_keys, preferred_element_type=f32).astype(bf16)
    values = jnp.einsum("bsd,de->bse", normed_low, full_values, preferred_element_type=f32).astype(
        bf16
    )
    pos_low = positions(total, width).astype(bf16)
    relative = jnp.dot(pos_low, full_position, preferred_element_type=f32).astype(bf16)

    def head_scores(query_u_head, query_v_head, keys_head, relative_head):
        content = jnp.einsum("bid,bjd->bij", query_u_head, keys_head, preferred_element_type=f32)
        position = rel_shift(
            jnp.einsum("bid,jd->bij", query_v_head, relative_head, preferred_element_type=f32)
        )
        return jnp.where(allowed, (content + position) * scale, MASKED)

    def head_forward(packed):
        query_u_head, query_v_head, keys_head, values_head, relative_head = packed
        scores = head_scores(query_u_head, query_v_head, keys_head, relative_head)
        top = jnp.max(scores, axis=-1, keepdims=True)
        expo = jnp.exp(scores - top)
        summed = jnp.sum(expo, axis=-1, keepdims=True)
        weights = (expo / summed).astype(bf16)
        mixed_head = jnp.einsum("bij,bjd->bid", weights, values_head, preferred_element_type=f32)
        return (mixed_head, top[..., 0] + jnp.log(summed[..., 0]))

    heads_in = (
        to_heads(query_u),
        to_heads(query_v),
        to_heads(keys),
        to_heads(values),
        to_heads(relative),
    )
    mixed_heads, logsum = lax.map(head_forward, heads_in)
    mixed_low = from_heads(mixed_heads).astype(bf16)
    attended = jnp.einsum("bsd,de->bse", mixed_low, full_output, preferred_element_type=f32)
    hidden = tokens.astype(f32) + attended
    (
        full_second_gain,
        full_second_shift,
        full_inner,
        full_inner_bias,
        full_outer,
        full_outer_bias,
        full_conv,
        full_conv_bias,
    ) = (
        lax.all_gather(second_gain, "fsdp", axis=0, tiled=True),
        lax.all_gather(second_shift, "fsdp", axis=0, tiled=True),
        lax.all_gather(inner_weight, "fsdp", axis=0, tiled=True),
        lax.all_gather(inner_bias, "fsdp", axis=0, tiled=True),
        lax.all_gather(outer_weight, "fsdp", axis=0, tiled=True),
        lax.all_gather(outer_bias, "fsdp", axis=0, tiled=True),
        lax.all_gather(conv_weight, "fsdp", axis=0, tiled=True),
        lax.all_gather(conv_bias, "fsdp", axis=0, tiled=True),
    )
    inner_norm, scaled_two, spread_two = norm_parts(hidden, full_second_gain, full_second_shift)
    inner_low = inner_norm.astype(bf16)
    preact = jnp.einsum(
        "bsd,df->bsf", inner_low, full_inner, preferred_element_type=f32
    ) + full_inner_bias.astype(f32)
    active = smooth_gate(preact).astype(bf16)
    result = (
        hidden
        + jnp.einsum("bsf,fd->bsd", active, full_outer, preferred_element_type=f32)
        + full_outer_bias.astype(f32)
    )
    groups = mem_rows // RATE
    start = mem_rows - RATE * groups
    mem_valid = (
        jnp.arange(mem_rows, dtype=jnp.int32)[None, :] >= (mem_rows - mem_fill)[:, None]
    ).astype(bf16)
    taps = (memory * mem_valid[..., None])[:, start:, :].reshape(streams, groups, RATE * width)
    group_valid = (start + RATE * jnp.arange(groups, dtype=jnp.int32) + RATE - 1)[None, :] >= (
        mem_rows - mem_fill
    )[:, None]
    made = (
        jnp.einsum("bnk,kd->bnd", taps, full_conv, preferred_element_type=f32)
        + full_conv_bias.astype(f32)
    ) * group_valid[..., None].astype(f32)
    back_second_gain, back_inner, back_outer = (
        lax.all_gather(second_gain, "fsdp", axis=0, tiled=True),
        lax.all_gather(inner_weight, "fsdp", axis=0, tiled=True),
        lax.all_gather(outer_weight, "fsdp", axis=0, tiled=True),
    )
    grad_wide = out_grad.astype(f32)
    outer_grad = jnp.einsum("bsf,bsd->fd", active, out_grad, preferred_element_type=f32)
    outer_bias_grad = jnp.sum(grad_wide, axis=(0, 1))
    active_grad = jnp.einsum("bsd,fd->bsf", out_grad, back_outer, preferred_element_type=f32)
    gate_pull = jax.vjp(smooth_gate, preact)[1]
    preact_grad = gate_pull(active_grad)[0].astype(bf16)
    inner_grad = jnp.einsum("bsd,bsf->df", inner_low, preact_grad, preferred_element_type=f32)
    inner_bias_grad = jnp.sum(preact_grad.astype(f32), axis=(0, 1))
    inner_norm_grad = jnp.einsum("bsf,df->bsd", preact_grad, back_inner, preferred_element_type=f32)
    second_gain_grad = jnp.sum(inner_norm_grad * scaled_two, axis=(0, 1))
    second_shift_grad = jnp.sum(inner_norm_grad, axis=(0, 1))
    hidden_grad = grad_wide + norm_back(inner_norm_grad, scaled_two, spread_two, back_second_gain)
    made_grad = comp_grad * group_valid[..., None].astype(bf16)
    conv_grad = jnp.einsum("bnk,bnd->kd", taps, made_grad, preferred_element_type=f32)
    conv_bias_grad = jnp.sum(made_grad.astype(f32), axis=(0, 1))
    ffn_parts = (
        lax.psum_scatter(
            second_gain_grad.astype(jnp.bfloat16), "fsdp", scatter_dimension=0, tiled=True
        ).astype(jnp.float32),
        lax.psum_scatter(
            second_shift_grad.astype(jnp.bfloat16), "fsdp", scatter_dimension=0, tiled=True
        ).astype(jnp.float32),
        lax.psum_scatter(
            inner_grad.astype(jnp.bfloat16), "fsdp", scatter_dimension=0, tiled=True
        ).astype(jnp.float32),
        lax.psum_scatter(
            inner_bias_grad.astype(jnp.bfloat16), "fsdp", scatter_dimension=0, tiled=True
        ).astype(jnp.float32),
        lax.psum_scatter(
            outer_grad.astype(jnp.bfloat16), "fsdp", scatter_dimension=0, tiled=True
        ).astype(jnp.float32),
        lax.psum_scatter(
            outer_bias_grad.astype(jnp.bfloat16), "fsdp", scatter_dimension=0, tiled=True
        ).astype(jnp.float32),
        lax.psum_scatter(
            conv_grad.astype(jnp.bfloat16), "fsdp", scatter_dimension=0, tiled=True
        ).astype(jnp.float32),
        lax.psum_scatter(
            conv_bias_grad.astype(jnp.bfloat16), "fsdp", scatter_dimension=0, tiled=True
        ).astype(jnp.float32),
    )
    ffn_done = (
        lax.psum(ffn_parts[0].astype(jnp.bfloat16), "dp").astype(jnp.float32),
        lax.psum(ffn_parts[1].astype(jnp.bfloat16), "dp").astype(jnp.float32),
        lax.psum(ffn_parts[2].astype(jnp.bfloat16), "dp").astype(jnp.float32),
        lax.psum(ffn_parts[3].astype(jnp.bfloat16), "dp").astype(jnp.float32),
        lax.psum(ffn_parts[4].astype(jnp.bfloat16), "dp").astype(jnp.float32),
        lax.psum(ffn_parts[5].astype(jnp.bfloat16), "dp").astype(jnp.float32),
        lax.psum(ffn_parts[6].astype(jnp.bfloat16), "dp").astype(jnp.float32),
        lax.psum(ffn_parts[7].astype(jnp.bfloat16), "dp").astype(jnp.float32),
    )
    back_first_gain, back_query, back_keys, back_values, back_output = (
        lax.all_gather(first_gain, "fsdp", axis=0, tiled=True),
        lax.all_gather(query_weight, "fsdp", axis=0, tiled=True),
        lax.all_gather(key_weight, "fsdp", axis=0, tiled=True),
        lax.all_gather(value_weight, "fsdp", axis=0, tiled=True),
        lax.all_gather(output_weight, "fsdp", axis=0, tiled=True),
    )
    hidden_low = hidden_grad.astype(bf16)
    output_grad = jnp.einsum("bsd,bse->de", mixed_low, hidden_low, preferred_element_type=f32)
    mixed_grad = jnp.einsum(
        "bse,de->bsd", hidden_low, back_output, preferred_element_type=f32
    ).astype(bf16)

    def head_backward(packed):
        (
            query_u_head,
            query_v_head,
            keys_head,
            values_head,
            relative_head,
            mixed_grad_head,
            logsum_head,
        ) = packed
        scores = head_scores(query_u_head, query_v_head, keys_head, relative_head)
        weights = jnp.exp(scores - logsum_head[..., None])
        weights_low = weights.astype(bf16)
        weight_grad = jnp.einsum(
            "bid,bjd->bij", mixed_grad_head, values_head, preferred_element_type=f32
        )
        values_grad = jnp.einsum(
            "bij,bid->bjd", weights_low, mixed_grad_head, preferred_element_type=f32
        ).astype(bf16)
        score_grad = weights * (
            weight_grad - jnp.sum(weights * weight_grad, axis=-1, keepdims=True)
        )
        logit_grad = (score_grad * scale).astype(bf16)
        query_u_grad = jnp.einsum("bij,bjd->bid", logit_grad, keys_head, preferred_element_type=f32)
        keys_grad = jnp.einsum(
            "bij,bid->bjd", logit_grad, query_u_head, preferred_element_type=f32
        ).astype(bf16)
        raw_grad = shift_back(logit_grad.astype(f32)).astype(bf16)
        query_v_grad = jnp.einsum(
            "bij,jd->bid", raw_grad, relative_head, preferred_element_type=f32
        )
        relative_grad = jnp.einsum(
            "bij,bid->bjd", raw_grad, query_v_head, preferred_element_type=f32
        ).astype(bf16)
        return (query_u_grad, query_v_grad, keys_grad, values_grad, relative_grad)

    heads_back = heads_in + (to_heads(mixed_grad), logsum)
    query_u_heads, query_v_heads, keys_heads, values_heads, relative_heads = lax.map(
        head_backward, heads_back
    )
    query_u_grad = from_heads(query_u_heads)
    query_v_grad = from_heads(query_v_heads)
    keys_grad = from_heads(keys_heads)
    values_grad = from_heads(values_heads)
    relative_grad = from_heads(relative_heads)
    content_grad = jnp.sum(query_u_grad, axis=(0, 1))
    posbias_grad = jnp.sum(query_v_grad, axis=(0, 1))
    query_low_grad = (query_u_grad + query_v_grad).astype(bf16)
    position_grad = jnp.einsum("ld,ble->de", pos_low, relative_grad, preferred_element_type=f32)
    query_grad = jnp.einsum("bsd,bse->de", own_rows, query_low_grad, preferred_element_type=f32)
    key_grad = jnp.einsum("bsd,bse->de", normed_low, keys_grad, preferred_element_type=f32)
    value_grad = jnp.einsum("bsd,bse->de", normed_low, values_grad, preferred_element_type=f32)
    normed_grad = jnp.einsum("bse,de->bsd", keys_grad, back_keys, preferred_element_type=f32)
    normed_grad = normed_grad + jnp.einsum(
        "bse,de->bsd", values_grad, back_values, preferred_element_type=f32
    )
    own_grad = jnp.einsum("bse,de->bsd", query_low_grad, back_query, preferred_element_type=f32)
    normed_grad = normed_grad + jnp.pad(own_grad, ((0, 0), (total - seg_rows, 0), (0, 0)))
    first_gain_grad = jnp.sum(normed_grad * scaled_one, axis=(0, 1))
    first_shift_grad = jnp.sum(normed_grad, axis=(0, 1))
    whole_grad = norm_back(normed_grad, scaled_one, spread_one, back_first_gain)
    token_gradient = hidden_grad + whole_grad[:, total - seg_rows :]
    attn_parts = (
        lax.psum_scatter(
            first_gain_grad.astype(jnp.bfloat16), "fsdp", scatter_dimension=0, tiled=True
        ).astype(jnp.float32),
        lax.psum_scatter(
            first_shift_grad.astype(jnp.bfloat16), "fsdp", scatter_dimension=0, tiled=True
        ).astype(jnp.float32),
        lax.psum_scatter(
            query_grad.astype(jnp.bfloat16), "fsdp", scatter_dimension=0, tiled=True
        ).astype(jnp.float32),
        lax.psum_scatter(
            key_grad.astype(jnp.bfloat16), "fsdp", scatter_dimension=0, tiled=True
        ).astype(jnp.float32),
        lax.psum_scatter(
            value_grad.astype(jnp.bfloat16), "fsdp", scatter_dimension=0, tiled=True
        ).astype(jnp.float32),
        lax.psum_scatter(
            position_grad.astype(jnp.bfloat16), "fsdp", scatter_dimension=0, tiled=True
        ).astype(jnp.float32),
        lax.psum_scatter(
            content_grad.astype(jnp.bfloat16), "fsdp", scatter_dimension=0, tiled=True
        ).astype(jnp.float32),
        lax.psum_scatter(
            posbias_grad.astype(jnp.bfloat16), "fsdp", scatter_dimension=0, tiled=True
        ).astype(jnp.float32),
        lax.psum_scatter(
            output_grad.astype(jnp.bfloat16), "fsdp", scatter_dimension=0, tiled=True
        ).astype(jnp.float32),
    )
    attn_done = (
        lax.psum(attn_parts[0].astype(jnp.bfloat16), "dp").astype(jnp.float32),
        lax.psum(attn_parts[1].astype(jnp.bfloat16), "dp").astype(jnp.float32),
        lax.psum(attn_parts[2].astype(jnp.bfloat16), "dp").astype(jnp.float32),
        lax.psum(attn_parts[3].astype(jnp.bfloat16), "dp").astype(jnp.float32),
        lax.psum(attn_parts[4].astype(jnp.bfloat16), "dp").astype(jnp.float32),
        lax.psum(attn_parts[5].astype(jnp.bfloat16), "dp").astype(jnp.float32),
        lax.psum(attn_parts[6].astype(jnp.bfloat16), "dp").astype(jnp.float32),
        lax.psum(attn_parts[7].astype(jnp.bfloat16), "dp").astype(jnp.float32),
        lax.psum(attn_parts[8].astype(jnp.bfloat16), "dp").astype(jnp.float32),
    )
    attn_mean = tuple((item * share for item in attn_done))
    ffn_mean = tuple((item * share for item in ffn_done))
    return (
        result.astype(bf16),
        token_gradient,
        made.astype(bf16),
        attn_mean[0],
        attn_mean[1],
        attn_mean[2],
        attn_mean[3],
        attn_mean[4],
        attn_mean[5],
        attn_mean[6],
        attn_mean[7],
        attn_mean[8],
        ffn_mean[0],
        ffn_mean[1],
        ffn_mean[2],
        ffn_mean[3],
        ffn_mean[4],
        ffn_mean[5],
        ffn_mean[6],
        ffn_mean[7],
    )


def solution(mesh):
    in_specs = (
        P(("dp", "fsdp"), None, None),
        P(("dp", "fsdp"), None, None),
        P(("dp", "fsdp"), None, None),
        P(("dp", "fsdp")),
        P(("dp", "fsdp")),
        P(("dp", "fsdp"), None),
        P("fsdp"),
        P("fsdp"),
        P("fsdp", None),
        P("fsdp", None),
        P("fsdp", None),
        P("fsdp", None),
        P("fsdp"),
        P("fsdp"),
        P("fsdp", None),
        P("fsdp"),
        P("fsdp"),
        P("fsdp", None),
        P("fsdp"),
        P("fsdp", None),
        P("fsdp"),
        P("fsdp", None),
        P("fsdp"),
        P(("dp", "fsdp"), None, None),
        P(("dp", "fsdp"), None, None),
    )
    out_specs = (
        P(("dp", "fsdp"), None, None),
        P(("dp", "fsdp"), None, None),
        P(("dp", "fsdp"), None, None),
        P("fsdp"),
        P("fsdp"),
        P("fsdp", None),
        P("fsdp", None),
        P("fsdp", None),
        P("fsdp", None),
        P("fsdp"),
        P("fsdp"),
        P("fsdp", None),
        P("fsdp"),
        P("fsdp"),
        P("fsdp", None),
        P("fsdp"),
        P("fsdp", None),
        P("fsdp"),
        P("fsdp", None),
        P("fsdp"),
    )
    return jax.shard_map(
        per_device, mesh=mesh, in_specs=in_specs, out_specs=out_specs, check_vma=False
    )
```

profile of v0, /device:TPU:0, one launch (start us, length us, event | category | flops | bytes accessed | tf_op | source)
XLA Modules:
  0.0 1380.3 jit_solution(14879130544681628141)
XLA Ops:
  20.6 10.2 all-gather.3
  30.9 8.7 all-gather.2
  47.7 7.9 all-gather.1
  55.6 8.7 all-gather
  65.0 7.8 all-gather.5
  72.8 8.7 all-gather.4
  81.6 8.1 all-gather.6
  89.8 13.0 fusion.82
  111.3 7.8 convolution_convert_fusion.8
  123.8 7.7 convolution_convert_fusion.7
  136.6 7.9 convolution_convert_fusion.6
  150.9 159.4 %while.38 = (s32[]{:T(128)}, bf16[8,1,512,128]{2,3,0,1:T(8,128)(2,1)}, f32[8,1,512]{2,1,0:T(1,128)}, bf16[8,1,512,128]{3,2,1,0:T(8,128)(2,1)}, bf16[8,1,1536,128...) while((s32[]{:T(128)}, ...), condition=%wide.region_5.6_spmd.clone.clone, body=%wide.region_2.5_spmd.clone.sunk.clone | while | flops 614202880 | bytes 42631796 | solution.py:172
  153.5 5.2 reshape.1218
  173.3 5.2 reshape.1218
  193.1 5.2 reshape.1218
  213.0 5.2 reshape.1218
  233.0 5.2 reshape.1218
  252.8 5.2 reshape.1218
  272.6 5.2 reshape.1218
  314.3 11.0 fusion.125
  325.3 14.3 %fusion.132 = (bf16[4096]{0:T(1024)(128)(2,1)}, bf16[512,4096]{1,0:T(8,128)(2,1)S(1)}) fusion(f32[512,4096]{1,0:T(8,128)} %fusion.125, f32[4096]{0:T(1024)S(1)} %bitcast.375, bf16[4096,1024]{1,0:T(8,128)(2,1)} %all-gather.30.cloned.1.call-done, bf16[1,512,1024]{2,1,0:T(8,128)(2,1)S(1)} %copy-done.13), kind=kOutput, calls=%fused_computation.231 | convolution fusion | flops 4341100544 | bytes 22044672 | tf_op jit(solution)/shard_map/bsd,fd->bsf/dot_general | solution.py:227
  339.6 5.4 fusion.87
  350.8 470.6 %while.39 = (s32[]{:T(128)}, f32[8,1,512,128]{2,3,0,1:T(8,128)}, f32[8,1,512,128]{2,3,0,1:T(8,128)}, bf16[8,1,1536,128]{2,3,0,1:T(8,128)(2,1)}, bf16[8,1,1536,12...) while((s32[]{:T(128)}, f32[8,1,512,128]{2,3,0,1:T(8,128)}, ...), condition=%wide.region_12.13_spmd.clone.clone, body=%wide.region_10.12_spmd.clone.sunk.clone | while | flops 1622998528 | bytes 98858720 | solution.py:325
  387.4 5.5 reshape.1224
  446.2 5.5 reshape.1224
  504.9 5.5 reshape.1224
  563.7 5.5 reshape.1224
  622.4 5.5 reshape.1224
  681.2 5.5 reshape.1224
  739.9 5.5 reshape.1224
  798.7 5.5 reshape.1224
  830.2 6.6 convolution_convert_fusion.11
  836.8 6.8 convolution_convert_fusion.10
  843.8 7.7 fusion.95
  856.0 9.4 convolution_convert_fusion.4
  866.7 13.2 convolution_convert_fusion.3
  880.5 7.8 all-gather.7
  888.3 8.7 all-gather.8
  911.2 5.7 fusion.135
  917.0 12.4 fusion.127
  929.5 23.7 %all-reduce.13 = (bf16[1024]{0:T(1024)(128)(2,1)S(1)}, bf16[1024]{0:T(1024)(128)(2,1)S(1)}, bf16[1024]{0:T(1024)(128)(2,1)S(1)}, bf16[1024]{0:T(1024)(128)(2,1)S...) all-reduce(bf16[1024]{0:T(1024)(128)(2,1)S(1)} %get-tuple-element.3, ...), channel_id=2, replica_groups=mesh['dp'=4,'fsdp'=8] {'fsdp'}, use_global_device_ids=true, to_apply=%region_16.17.clone | all-reduce | flops 12288 | bytes 49152
  953.9 11.9 all-reduce.14
  966.9 39.1 %reduce-scatter.15.cloned.1.call-done = bf16[128,1024]{1,0:T(8,128)(2,1)} async-done(((bf16[1024,1024]{1,0:T(8,128)(2,1)}), bf16[128,1024]{1,0:T(8,128)(2,1)}) %reduce-scatter.15.cloned.1.call-update) | async-done | bytes 262160 | tf_op jit(solution)/shard_map/reduce_scatter | solution.py:366
  1005.9 44.7 %reduce-scatter.17.cloned.1.call-done = bf16[128,1024]{1,0:T(8,128)(2,1)} async-done(((bf16[1024,1024]{1,0:T(8,128)(2,1)}), bf16[128,1024]{1,0:T(8,128)(2,1)}) %reduce-scatter.17.cloned.1.call-update) | async-done | bytes 262160 | tf_op jit(solution)/shard_map/reduce_scatter | solution.py:375
  1050.7 74.6 %reduce-scatter.19.cloned.1.call-done = bf16[128,4096]{1,0:T(8,128)(2,1)} async-done(((bf16[1024,4096]{1,0:T(8,128)(2,1)}), bf16[128,4096]{1,0:T(8,128)(2,1)}) %reduce-scatter.19.cloned.1.call-update) | async-done | bytes 1048592 | tf_op jit(solution)/shard_map/reduce_scatter | solution.py:246
  1125.3 75.0 %reduce-scatter.21.cloned.1.call-done = bf16[512,1024]{1,0:T(8,128)(2,1)} async-done(((bf16[4096,1024]{1,0:T(8,128)(2,1)}), bf16[512,1024]{1,0:T(8,128)(2,1)}) %reduce-scatter.21.cloned.1.call-update) | async-done | bytes 1048592 | tf_op jit(solution)/shard_map/reduce_scatter | solution.py:252
  1208.6 12.5 fusion.93
  1221.1 139.5 %all-reduce.18.cloned.1.call-done = (bf16[128,1024]{1,0:T(8,128)(2,1)}, bf16[128,1024]{1,0:T(8,128)(2,1)}, bf16[128,1024]{1,0:T(8,128)(2,1)}, bf16[128,1024]{1,0...) async-done(((bf16[128,1024]{1,0:T(8,128)(2,1)}, bf16[128,1024]{1,0:T(8,128)(2,1)}, ...) | async-done | bytes 4194320 | tf_op jit(solution)/shard_map/psum | solution.py:382
  (546 shorter events, 655.1 us)
Async XLA Ops:
  7.2 99.9 %all-gather.18.cloned.1.call-start = ((), (), s32[]{:S(2)}) async-start(), calls=%async_computation.8 | async-start | bytes 2359296 | tf_op jit(solution)/shard_map/all_gather | solution.py:125
  7.9 103.4 %all-gather.20.cloned.1.call-start = ((), (), s32[]{:S(2)}) async-start(), calls=%async_computation.9 | async-start | bytes 2359296 | tf_op jit(solution)/shard_map/all_gather | solution.py:126
  8.7 115.1 %all-gather.22.cloned.1.call-start = ((), (), s32[]{:S(2)}) async-start(), calls=%async_computation.10 | async-start | bytes 2359296 | tf_op jit(solution)/shard_map/all_gather | solution.py:128
  9.4 127.2 %all-gather.24.cloned.1.call-start = ((), (), s32[]{:S(2)}) async-start(), calls=%async_computation.11 | async-start | bytes 2359296 | tf_op jit(solution)/shard_map/all_gather | solution.py:127
  10.0 300.3 %all-gather.26.cloned.1.call-start = ((), (), s32[]{:S(2)}) async-start(), calls=%async_computation.12 | async-start | bytes 2359296 | tf_op jit(solution)/shard_map/all_gather | solution.py:131
  10.6 303.6 %all-gather.28.cloned.1.call-start = ((), (), s32[]{:S(2)}) async-start(), calls=%async_computation.13 | async-start | bytes 9437184 | tf_op jit(solution)/shard_map/all_gather | solution.py:188
  11.2 314.1 %all-gather.30.cloned.1.call-start = ((), (), s32[]{:S(2)}) async-start(), calls=%async_computation.14 | async-start | bytes 9437184 | tf_op jit(solution)/shard_map/all_gather | solution.py:190
  11.9 891.0 %all-gather.32.cloned.1.call-start = ((), (), s32[]{:S(2)}) async-start(), calls=%async_computation.15 | async-start | bytes 7077888 | tf_op jit(solution)/shard_map/all_gather | solution.py:192
  12.7 954.2 %reduce-scatter.23.cloned.1.call-start = ((), (), s32[]{:S(2)}) async-start(), calls=%async_computation.23 | async-start | bytes 7077888 | tf_op jit(solution)/shard_map/reduce_scatter | solution.py:258
  19.4 11.5 copy-start.50
  19.4 20.2 %copy-start.2 = (bf16[1,512,1024]{2,1,0:T(8,128)(2,1)S(1)}, bf16[1,512,1024]{2,1,0:T(8,128)(2,1)}, u32[]{:S(2)}) copy-start(bf16[1,512,1024]{2,1,0:T(8,128)(2,1)} %param.29) | copy-start | bytes 3145732
  19.4 20.2 %copy-start.8 = (bf16[1,512,1024]{2,1,0:T(8,128)(2,1)S(1)}, bf16[1,512,1024]{2,1,0:T(8,128)(2,1)}, u32[]{:S(2)}) copy-start(bf16[1,512,1024]{2,1,0:T(8,128)(2,1)} %param.31) | copy-start | bytes 3145732
  19.4 947.4 %reduce-scatter.9.cloned.1.call-start = ((), (), s32[]{:S(2)}) async-start(), calls=%async_computation.16 | async-start | bytes 2359296 | tf_op jit(solution)/shard_map/reduce_scatter | solution.py:357
  40.2 62.6 %copy-start.26 = (f32[1536]{0:T(1024)}, f32[1536]{0:T(1024)S(1)}, u32[]{:S(2)}) copy-start(f32[1536]{0:T(1024)S(1)} %broadcast_multiply_fusion.3) | copy-start | bytes 18436
  43.2 59.6 %copy-start.28 = (f32[1536]{0:T(1024)}, f32[1536]{0:T(1024)S(1)}, u32[]{:S(2)}) copy-start(f32[1536]{0:T(1024)S(1)} %add_rsqrt_fusion) | copy-start | bytes 18436
  43.2 12.4 copy-start.52
  43.3 21.8 %copy-start.53 = (bf16[128]{0:T(256)(128)(2,1)S(1)}, bf16[128]{0:T(256)(128)(2,1)}, u32[]{:S(2)}) copy-start(bf16[128]{0:T(256)(128)(2,1)} %param.45) | copy-start | bytes 772
  43.3 29.6 %copy-start.54 = (bf16[128]{0:T(256)(128)(2,1)S(1)}, bf16[128]{0:T(256)(128)(2,1)}, u32[]{:S(2)}) copy-start(bf16[128]{0:T(256)(128)(2,1)} %param.44) | copy-start | bytes 772
  43.3 38.3 %copy-start.48 = (bf16[512]{0:T(512)(128)(2,1)S(1)}, bf16[512]{0:T(512)(128)(2,1)}, u32[]{:S(2)}) copy-start(bf16[512]{0:T(512)(128)(2,1)} %param.47) | copy-start | bytes 3076
  47.7 55.0 %copy-start.46 = (s32[1,512]{1,0:T(1,128)S(1)}, s32[1,512]{1,0:T(1,128)}, u32[]{:S(2)}) copy-start(s32[1,512]{1,0:T(1,128)} %param.34) | copy-start | bytes 6148
  55.6 51.4 %copy-start.32 = (f32[8,1,128]{2,1,0:T(1,128)}, f32[8,1,128]{2,1,0:T(1,128)S(1)}, u32[]{:S(2)}) copy-start(f32[8,1,128]{2,1,0:T(1,128)S(1)} %convert_element_type.476) | copy-start | bytes 12292
  64.4 42.7 %copy-start.30 = (f32[8,1,128]{2,1,0:T(1,128)}, f32[8,1,128]{2,1,0:T(1,128)S(1)}, u32[]{:S(2)}) copy-start(f32[8,1,128]{2,1,0:T(1,128)S(1)} %convert_element_type.475) | copy-start | bytes 12292
  72.8 241.4 %copy-start.43 = (f32[8,1,128]{2,1,0:T(1,128)}, f32[8,1,128]{2,1,0:T(1,128)S(1)}, u32[]{:S(2)}) copy-start(f32[8,1,128]{2,1,0:T(1,128)S(1)} %convert_element_type.480) | copy-start | bytes 12292
  89.7 235.6 %copy-start.34 = (f32[8,1,512]{2,1,0:T(1,128)}, f32[8,1,512]{2,1,0:T(1,128)S(1)}, u32[]{:S(2)}) copy-start(f32[8,1,512]{2,1,0:T(1,128)S(1)} %convert_element_type.481) | copy-start | bytes 49156
  313.8 32.0 %copy-start.6 = (f32[1,512,1024]{2,1,0:T(8,128)}, f32[1,512,1024]{2,1,0:T(8,128)S(1)}, u32[]{:S(2)}) copy-start(f32[1,512,1024]{2,1,0:T(8,128)S(1)} %get-tuple-element.478) | copy-start | bytes 6291460
  314.2 31.6 %copy-start.41 = (f32[512]{0:T(512)}, f32[512]{0:T(512)S(1)}, u32[]{:S(2)}) copy-start(f32[512]{0:T(512)S(1)} %add_rsqrt_fusion.1) | copy-start | bytes 6148
  314.3 11.1 copy-start.13
  325.3 14.3 %copy-start.57 = (bf16[1024,4096]{1,0:T(8,128)(2,1)S(1)}, bf16[1024,4096]{1,0:T(8,128)(2,1)}, u32[]{:S(2)}) copy-start(bf16[1024,4096]{1,0:T(8,128)(2,1)} %all-gather.28.cloned.1.call-done) | copy-start | bytes 25165828
  830.1 136.7 %reduce-scatter.11.cloned.1.call-start = ((), (), s32[]{:S(2)}) async-start(), calls=%async_computation.17 | async-start | bytes 2359296 | tf_op jit(solution)/shard_map/reduce_scatter | solution.py:360
  836.8 130.0 %reduce-scatter.13.cloned.1.call-start = ((), (), s32[]{:S(2)}) async-start(), calls=%async_computation.18 | async-start | bytes 2359296 | tf_op jit(solution)/shard_map/reduce_scatter | solution.py:363
  843.7 162.2 %reduce-scatter.15.cloned.1.call-start = ((), (), s32[]{:S(2)}) async-start(), calls=%async_computation.19 | async-start | bytes 2359296 | tf_op jit(solution)/shard_map/reduce_scatter | solution.py:366
  843.7 7.8 copy-start.15
  851.5 199.1 %reduce-scatter.17.cloned.1.call-start = ((), (), s32[]{:S(2)}) async-start(), calls=%async_computation.20 | async-start | bytes 2359296 | tf_op jit(solution)/shard_map/reduce_scatter | solution.py:375
  855.9 269.4 %reduce-scatter.19.cloned.1.call-start = ((), (), s32[]{:S(2)}) async-start(), calls=%async_computation.21 | async-start | bytes 9437184 | tf_op jit(solution)/shard_map/reduce_scatter | solution.py:246
  865.4 334.9 %reduce-scatter.21.cloned.1.call-start = ((), (), s32[]{:S(2)}) async-start(), calls=%async_computation.22 | async-start | bytes 9437184 | tf_op jit(solution)/shard_map/reduce_scatter | solution.py:252
  879.8 8.4 copy-start.56
  879.9 22.3 %copy-start.19 = (bf16[1,170,1024]{2,1,0:T(8,128)(2,1)S(1)}, bf16[1,170,1024]{2,1,0:T(8,128)(2,1)}, u32[]{:S(2)}) copy-start(bf16[1,170,1024]{2,1,0:T(8,128)(2,1)} %param.53) | copy-start | bytes 1044484
  879.9 23.1 %copy-start.12 = (bf16[170,3072]{1,0:T(8,128)(2,1)S(1)}, bf16[170,3072]{1,0:T(8,128)(2,1)}, u32[]{:S(2)}) copy-start(bf16[170,3072]{1,0:T(8,128)(2,1)} %copy-done.11) | copy-start | bytes 3133444
  879.9 480.7 %all-reduce.18.cloned.1.call-start = ((), (), s32[]{:S(2)}) async-start(), calls=%async_computation.24 | async-start | bytes 8388608 | tf_op jit(solution)/shard_map/psum | solution.py:382
  917.0 12.4 copy-start.37
  917.0 12.4 copy-start.38
  917.0 12.4 copy-start.39
  917.0 12.4 copy-start.40
  917.0 12.4 copy-start.45
  929.4 274.6 %slice-start = ((f32[1536]{0:T(1024)}), f32[512]{0:T(512)S(1)}, s32[]{:S(2)}) async-start(f32[1536]{0:T(1024)} %copy-done.28), calls=%async_computation.25 | async-start | bytes 4096 | tf_op jit(solution)/shard_map/slice | solution.py:349
  1360.6 7.4 copy-start.25
  1360.6 8.2 copy-start.21
  1362.5 7.9 copy-start.20
  (48 other events, 175.2 us)
Sparse Core Ops, SparseCore 0:
  9.9 30.5 all-gather.17
  42.4 27.8 all-gather.19
  72.3 27.9 all-gather.21
  102.0 27.8 all-gather.23
  131.6 27.8 all-gather.25
  161.3 54.4 all-gather.27
  217.6 54.3 all-gather.29
  273.9 45.5 all-gather.31
  322.9 61.7 reduce-scatter.22
  830.2 41.6 reduce-scatter.8
  875.2 41.1 reduce-scatter.10
  920.0 41.3 reduce-scatter.12
  964.7 41.1 reduce-scatter.14
  1009.4 41.2 reduce-scatter.16
  1054.0 71.2 reduce-scatter.18
  1129.0 71.2 reduce-scatter.20
  1203.1 157.4 all-reduce.17
where the time goes:
time: 1390 us; the launch traced here: 1380 us
  matrix products  411 us (30%)
  local copies, waits for them, and re-layouts  393 us (28%)
  waiting for transfers between devices  378 us (27%)
  blocking collectives  112 us (8%)
  other arithmetic  66.5 us (5%)
  between operations  17.8 us (1%)
    psum x1, waiting for transfers between devices, per_device(): lax.psum(attn_parts[2].astype(jnp.bfloat16), 'dp').astype(jnp.float32)  139 us
    reshape x24, local copies, waits for them, and re-layouts, rel_shift(): folded = padded.reshape(leading, cols + 1, rows)  125 us
    reduce_scatter x1, waiting for transfers between devices, per_device(): lax.psum_scatter(outer_grad.astype(jnp.bfloat16), 'fsdp', scatter_dimensi...  75 us
    reduce_scatter x1, waiting for transfers between devices, per_device(): lax.psum_scatter(inner_grad.astype(jnp.bfloat16), 'fsdp', scatter_dimensi...  74.6 us
    dot_general x16, matrix products, head_scores(): jnp.einsum('bid,bjd->bij', query_u_head, keys_head, preferred_element_typ...  70.8 us
    reshape x24, local copies, waits for them, and re-layouts, rel_shift(): return folded[:, 1:, :].reshape(leading, rows, cols)  67.2 us
    dynamic_update_slice x40, local copies, waits for them, and re-layouts, per_device(): lax.map(head_backward, heads_back)  47.9 us
    reduce_scatter x1, waiting for transfers between devices, per_device(): lax.psum_scatter(output_grad.astype(jnp.bfloat16), 'fsdp', scatter_dimens...  44.7 us
  transfers between devices with their start and end apart: 17, of which 5 were waited for; matrix products, arithmetic and copies ran while one was open for 61% of the time, Pallas kernels for 0%

commit v1 on v0

--- a/solution.py
+++ b/solution.py
@@ -3,11 +3,17 @@
 import jax
 import jax.numpy as jnp
 from jax import lax
+from jax.experimental import pallas as pl
+from jax.experimental.pallas import tpu as pltpu
 from jax.sharding import PartitionSpec as P
 
 HEADS = 8
 DH = 128
 RATE = 3
+BLK = 128
+NEG = -1.2e10
+f32 = jnp.float32
+bf16 = jnp.bfloat16
 
 
 EPSILON = 1e-05
@@ -44,34 +50,88 @@
     return jnp.concatenate([jnp.sin(angle), jnp.cos(angle)], axis=1)
 
 
-def rel_shift(table):
-    leading, rows, cols = table.shape
-    padded = jnp.pad(table, ((0, 0), (0, 0), (1, 0)))
-    folded = padded.reshape(leading, cols + 1, rows)
-    return folded[:, 1:, :].reshape(leading, rows, cols)
-
-
-def shift_back(grad):
-    pull = jax.vjp(rel_shift, grad)[1]
-    return pull(grad)[0]
-
-
-def key_mask(mem_fill, cmem_fill, pad_mask, cmem_rows, mem_rows):
-    seg_rows = pad_mask.shape[-1]
-    comp_valid = jnp.arange(cmem_rows, dtype=jnp.int32)[None, :] >= (cmem_rows - cmem_fill)[:, None]
-    mem_valid = jnp.arange(mem_rows, dtype=jnp.int32)[None, :] >= (mem_rows - mem_fill)[:, None]
-    keyvalid = jnp.concatenate([comp_valid, mem_valid, pad_mask == 1], axis=1)
-    column = jnp.arange(cmem_rows + mem_rows + seg_rows, dtype=jnp.int32)[None, :]
-    own = (cmem_rows + mem_rows + jnp.arange(seg_rows, dtype=jnp.int32))[:, None]
-    return (column <= own)[None] & (keyvalid[:, None, :] | (column == own)[None])
-
-
-def to_heads(array):
-    return jnp.moveaxis(array.reshape(array.shape[:-1] + (HEADS, DH)), -2, 0)
-
-
-def from_heads(array):
-    return jnp.moveaxis(array, 0, -2).reshape(array.shape[1:-1] + (HEADS * DH,))
+def dot_nt(a,b): return lax.dot_general(a,b,(((1,),(1,)),((),())),preferred_element_type=f32)
+def dot_nn(a,b): return lax.dot_general(a,b,(((1,),(0,)),((),())),preferred_element_type=f32)
+
+def attn_fwd_kernel(qu_ref,qv_ref,k_ref,v_ref,r_ref,bias_ref,o_ref,p_ref):
+    seg=qu_ref.shape[0]; total=k_ref.shape[0]; old=total-seg
+    c=math.log2(math.e)/math.sqrt(DH)
+    for ib in range(seg//BLK):
+        rows=pl.ds(ib*BLK,BLK)
+        L=old+(ib+1)*BLK
+        qu=qu_ref[rows,:]; qv=qv_ref[rows,:]
+        raw=dot_nt(qv,r_ref[pl.ds(total-L,L),:])
+        z=dot_nt(qu,k_ref[pl.ds(0,L),:])+pltpu.roll(raw,L-(BLK-1),axis=1,stride=1,stride_axis=0)
+        M=L-BLK
+        za=z[:,:M]+bias_ref[:,:M]
+        rr=lax.broadcasted_iota(jnp.int32,(BLK,BLK),0); cc=lax.broadcasted_iota(jnp.int32,(BLK,BLK),1)
+        zb=z[:,M:]
+        zb=jnp.where(cc==rr,zb,jnp.where(cc<rr,zb+bias_ref[:,pl.ds(M,BLK)],NEG))
+        top=jnp.maximum(jnp.max(za,axis=1,keepdims=True),jnp.max(zb,axis=1,keepdims=True))
+        ea=jnp.exp2((za-top)*c); eb=jnp.exp2((zb-top)*c)
+        inv=1.0/(jnp.sum(ea,axis=1,keepdims=True)+jnp.sum(eb,axis=1,keepdims=True))
+        pa=(ea*inv).astype(bf16); pb=(eb*inv).astype(bf16)
+        p_ref[0,rows,pl.ds(0,M)]=pa
+        p_ref[0,rows,pl.ds(M,BLK)]=pb
+        o_ref[rows,:]=(dot_nn(pa,v_ref[pl.ds(0,M),:])+dot_nn(pb,v_ref[pl.ds(M,BLK),:])).astype(bf16)
+
+def attn_fwd(qu,qv,k,v,r,bias):
+    seg,width=qu.shape; total=k.shape[0]; heads=width//DH
+    col=lambda n: pl.BlockSpec((n,DH),lambda h:(0,h))
+    return pl.pallas_call(attn_fwd_kernel,grid=(heads,),
+        in_specs=[col(seg),col(seg),col(total),col(total),col(total),pl.BlockSpec((1,total),lambda h:(0,0))],
+        out_specs=[col(seg),pl.BlockSpec((1,seg,total),lambda h:(h,0,0))],
+        out_shape=[jax.ShapeDtypeStruct((seg,width),bf16),jax.ShapeDtypeStruct((heads,seg,total),bf16)],
+        cost_estimate=pl.CostEstimate(flops=6*seg*total*width,bytes_accessed=2*(3*seg*width+3*total*width+heads*seg*total),transcendentals=heads*seg*total),
+        compiler_params=pltpu.CompilerParams(vmem_limit_bytes=40<<20),name="attn_fwd")(qu,qv,k,v,r,bias)
+
+def attn_bwd_kernel(qu_ref,qv_ref,qut_ref,qvrt_ref,k_ref,v_ref,r_ref,p_ref,g_ref,gt_ref,dq_ref,dkt_ref,dvt_ref,drt_ref,sums_ref,dk_acc,dv_acc,dr_acc):
+    seg=g_ref.shape[0]; total=k_ref.shape[0]; old=total-seg
+    scale=1.0/math.sqrt(DH)
+    rr=lax.broadcasted_iota(jnp.int32,(BLK,BLK),0); cc=lax.broadcasted_iota(jnp.int32,(BLK,BLK),1)
+    flip=(rr+cc==BLK-1).astype(bf16)
+    su=jnp.zeros((1,DH),f32); sv=jnp.zeros((1,DH),f32)
+    nb=seg//BLK
+    for ib in range(nb-1,-1,-1):
+        rows=pl.ds(ib*BLK,BLK)
+        L=old+(ib+1)*BLK
+        g=g_ref[rows,:]; gt=gt_ref[:,rows]; qut=qut_ref[:,rows]
+        plow=p_ref[0,rows,pl.ds(0,L)]
+        p=plow.astype(f32)
+        dp=dot_nt(g,v_ref[pl.ds(0,L),:])
+        d=jnp.sum(p*dp,axis=1,keepdims=True)
+        dz=(p*(dp-d)*scale).astype(bf16)
+        dvt=dot_nn(gt,plow)
+        dkt=dot_nn(qut,dz)
+        dqu=dot_nn(dz,k_ref[pl.ds(0,L),:])
+        rev=dot_nn(flip,dz)
+        raw=pltpu.roll(rev,0,axis=1,stride=1,stride_axis=0).astype(bf16)
+        T=pl.ds(total-L,L)
+        dqv_rev=dot_nn(raw,r_ref[T,:])
+        qvr=dot_nt(qvrt_ref[:,rows],flip).astype(bf16)
+        drt=dot_nn(qvr,raw)
+        dqv=lax.dot_general(flip.astype(f32),dqv_rev,(((1,),(0,)),((),())),preferred_element_type=f32,precision=lax.Precision.HIGHEST)
+        su+=jnp.sum(dqu,axis=0,keepdims=True); sv+=jnp.sum(dqv,axis=0,keepdims=True)
+        dq_ref[rows,:]=(dqu+dqv).astype(bf16)
+        J=pl.ds(0,L)
+        if ib==nb-1:
+            dv_acc[...]=dvt; dk_acc[...]=dkt; dr_acc[...]=drt
+        else:
+            dv_acc[:,J]+=dvt; dk_acc[:,J]+=dkt; dr_acc[:,T]+=drt
+    dkt_ref[...]=dk_acc[...].astype(bf16); dvt_ref[...]=dv_acc[...].astype(bf16); drt_ref[...]=dr_acc[...].astype(bf16)
+    sums_ref[0:1,:]=su; sums_ref[1:2,:]=sv
+
+def attn_bwd(qu,qv,k,v,r,p,g):
+    seg,width=qu.shape; total=k.shape[0]; heads=width//DH
+    col=lambda n: pl.BlockSpec((n,DH),lambda h:(0,h))
+    row=lambda n: pl.BlockSpec((DH,n),lambda h:(h,0))
+    return pl.pallas_call(attn_bwd_kernel,grid=(heads,),
+        in_specs=[col(seg),col(seg),row(seg),row(seg),col(total),col(total),col(total),pl.BlockSpec((1,seg,total),lambda h:(h,0,0)),col(seg),row(seg)],
+        out_specs=[col(seg),row(total),row(total),row(total),pl.BlockSpec((8,DH),lambda h:(0,h))],
+        out_shape=[jax.ShapeDtypeStruct((seg,width),bf16)]+[jax.ShapeDtypeStruct((width,total),bf16)]*3+[jax.ShapeDtypeStruct((8,width),f32)],
+        scratch_shapes=[pltpu.VMEM((DH,total),f32)]*3,
+        cost_estimate=pl.CostEstimate(flops=16*seg*total*width,bytes_accessed=2*(5*seg*width+6*total*width+heads*seg*total),transcendentals=0),
+        compiler_params=pltpu.CompilerParams(vmem_limit_bytes=40<<20),name="attn_bwd")(qu,qv,qu.T,qv.T,k,v,r,p,g,g.T)
 
 
 def per_device(
@@ -130,7 +190,6 @@
         lax.all_gather(position_bias, "fsdp", axis=0, tiled=True),
         lax.all_gather(output_weight, "fsdp", axis=0, tiled=True),
     )
-    allowed = key_mask(mem_fill, cmem_fill, pad_mask, cmem_rows, mem_rows)
     whole = jnp.concatenate([compressed, memory, tokens], axis=1).astype(f32)
     normed, scaled_one, spread_one = norm_parts(whole, full_first_gain, full_first_shift)
     normed_low = normed.astype(bf16)
@@ -145,32 +204,16 @@
     pos_low = positions(total, width).astype(bf16)
     relative = jnp.dot(pos_low, full_position, preferred_element_type=f32).astype(bf16)
 
-    def head_scores(query_u_head, query_v_head, keys_head, relative_head):
-        content = jnp.einsum("bid,bjd->bij", query_u_head, keys_head, preferred_element_type=f32)
-        position = rel_shift(
-            jnp.einsum("bid,jd->bij", query_v_head, relative_head, preferred_element_type=f32)
-        )
-        return jnp.where(allowed, (content + position) * scale, MASKED)
-
-    def head_forward(packed):
-        query_u_head, query_v_head, keys_head, values_head, relative_head = packed
-        scores = head_scores(query_u_head, query_v_head, keys_head, relative_head)
-        top = jnp.max(scores, axis=-1, keepdims=True)
-        expo = jnp.exp(scores - top)
-        summed = jnp.sum(expo, axis=-1, keepdims=True)
-        weights = (expo / summed).astype(bf16)
-        mixed_head = jnp.einsum("bij,bjd->bid", weights, values_head, preferred_element_type=f32)
-        return (mixed_head, top[..., 0] + jnp.log(summed[..., 0]))
-
-    heads_in = (
-        to_heads(query_u),
-        to_heads(query_v),
-        to_heads(keys),
-        to_heads(values),
-        to_heads(relative),
-    )
-    mixed_heads, logsum = lax.map(head_forward, heads_in)
-    mixed_low = from_heads(mixed_heads).astype(bf16)
+    valid = jnp.concatenate(
+        [
+            jnp.arange(cmem_rows, dtype=jnp.int32) >= cmem_rows - cmem_fill[0],
+            jnp.arange(mem_rows, dtype=jnp.int32) >= mem_rows - mem_fill[0],
+            pad_mask[0] == 1,
+        ]
+    )
+    bias = jnp.where(valid, 0.0, NEG).astype(f32)[None]
+    mixed_one, prob_low = attn_fwd(query_u[0], query_v[0], keys[0], values[0], relative, bias)
+    mixed_low = mixed_one[None]
     attended = jnp.einsum("bsd,de->bse", mixed_low, full_output, preferred_element_type=f32)
     hidden = tokens.astype(f32) + attended
     (
@@ -285,55 +328,13 @@
         "bse,de->bsd", hidden_low, back_output, preferred_element_type=f32
     ).astype(bf16)
 
-    def head_backward(packed):
-        (
-            query_u_head,
-            query_v_head,
-            keys_head,
-            values_head,
-            relative_head,
-            mixed_grad_head,
-            logsum_head,
-        ) = packed
-        scores = head_scores(query_u_head, query_v_head, keys_head, relative_head)
-        weights = jnp.exp(scores - logsum_head[..., None])
-        weights_low = weights.astype(bf16)
-        weight_grad = jnp.einsum(
-            "bid,bjd->bij", mixed_grad_head, values_head, preferred_element_type=f32
-        )
-        values_grad = jnp.einsum(
-            "bij,bid->bjd", weights_low, mixed_grad_head, preferred_element_type=f32
-        ).astype(bf16)
-        score_grad = weights * (
-            weight_grad - jnp.sum(weights * weight_grad, axis=-1, keepdims=True)
-        )
-        logit_grad = (score_grad * scale).astype(bf16)
-        query_u_grad = jnp.einsum("bij,bjd->bid", logit_grad, keys_head, preferred_element_type=f32)
-        keys_grad = jnp.einsum(
-            "bij,bid->bjd", logit_grad, query_u_head, preferred_element_type=f32
-        ).astype(bf16)
-        raw_grad = shift_back(logit_grad.astype(f32)).astype(bf16)
-        query_v_grad = jnp.einsum(
-            "bij,jd->bid", raw_grad, relative_head, preferred_element_type=f32
-        )
-        relative_grad = jnp.einsum(
-            "bij,bid->bjd", raw_grad, query_v_head, preferred_element_type=f32
-        ).astype(bf16)
-        return (query_u_grad, query_v_grad, keys_grad, values_grad, relative_grad)
-
-    heads_back = heads_in + (to_heads(mixed_grad), logsum)
-    query_u_heads, query_v_heads, keys_heads, values_heads, relative_heads = lax.map(
-        head_backward, heads_back
-    )
-    query_u_grad = from_heads(query_u_heads)
-    query_v_grad = from_heads(query_v_heads)
-    keys_grad = from_heads(keys_heads)
-    values_grad = from_heads(values_heads)
-    relative_grad = from_heads(relative_heads)
-    content_grad = jnp.sum(query_u_grad, axis=(0, 1))
-    posbias_grad = jnp.sum(query_v_grad, axis=(0, 1))
-    query_low_grad = (query_u_grad + query_v_grad).astype(bf16)
-    position_grad = jnp.einsum("ld,ble->de", pos_low, relative_grad, preferred_element_type=f32)
+    query_low, keys_t, values_t, relative_t, sums = attn_bwd(
+        query_u[0], query_v[0], keys[0], values[0], relative, prob_low, mixed_grad[0]
+    )
+    query_low_grad = query_low[None]
+    keys_grad, values_grad = keys_t.T[None], values_t.T[None]
+    content_grad, posbias_grad = sums[0], sums[1]
+    position_grad = jnp.einsum("ld,el->de", pos_low, relative_t, preferred_element_type=f32)
     query_grad = jnp.einsum("bsd,bse->de", own_rows, query_low_grad, preferred_element_type=f32)
     key_grad = jnp.einsum("bsd,bse->de", normed_low, keys_grad, preferred_element_type=f32)
     value_grad = jnp.einsum("bsd,bse->de", normed_low, values_grad, preferred_element_type=f32)

time: 1390 us -> 945 us (0.68)
  local copies, waits for them, and re-layouts: 393 us -> 23.6 us
  matrix products: 411 us -> 161 us
  waiting for transfers between devices: 378 us -> 496 us
  Pallas kernels: 0 us -> 71.1 us
    dot_general x89 -> x1, matrix products: 261 us -> 7.69 us  [per_device(): jnp.einsum('ld,el->de', pos_low, relative_t, preferred_element_type=f32)]
    reshape x52 -> x0, local copies, waits for them, and re-layouts: 208 us -> none  [the longest x24 125 us: rel_shift(): folded = padded.reshape(leading, cols + 1, rows)]
    pallas_call x0 -> x2, Pallas kernels: none -> 71.1 us  [the longest x1 42.4 us: attn_bwd(): pl.pallas_call(attn_bwd_kernel, grid=(heads,), in_specs=[col(seg), col(se...]
    dynamic_update_slice x48 -> x0, local copies, waits for them, and re-layouts: 52.6 us -> none  [the longest x40 47.9 us: per_device(): lax.map(head_backward, heads_back)]
    all_gather x1, waiting for transfers between devices: 0.01 us -> 44.2 us  [per_device(): lax.all_gather(outer_weight, 'fsdp', axis=0, tiled=True)]
    all_gather x1, waiting for transfers between devices: 0.02 us -> 42.6 us  [per_device(): lax.all_gather(inner_weight, 'fsdp', axis=0, tiled=True)]
    pad x24 -> x0, local copies, waits for them, and re-layouts: 39.6 us -> none  [the longest x8 24.6 us: rel_shift(): return folded[:, 1:, :].reshape(leading, rows, cols)]
    while x40 -> x0, local copies, waits for them, and re-layouts: 39.4 us -> none
  transfers between devices with their start and end apart: 17 -> 17, of which waited for: 5 -> 9; matrix products, arithmetic and copies ran while one was open for 61% -> 22% of each run, Pallas kernels for 0% -> 8%
where the time goes in v1:
time: 945 us; the launch traced here: 938 us
  waiting for transfers between devices  496 us (52%)
  matrix products  161 us (17%)
  blocking collectives  113 us (12%)
  Pallas kernels  71.1 us (8%)
  other arithmetic  54.8 us (6%)
  local copies, waits for them, and re-layouts  23.6 us (2%)
  between operations  17.5 us (2%)
    psum x1, waiting for transfers between devices, per_device(): lax.psum(attn_parts[2].astype(jnp.bfloat16), 'dp').astype(jnp.float32)  139 us
    reduce_scatter x1, waiting for transfers between devices, per_device(): lax.psum_scatter(outer_grad.astype(jnp.bfloat16), 'fsdp', scatter_dimensi...  75 us
    reduce_scatter x1, waiting for transfers between devices, per_device(): lax.psum_scatter(inner_grad.astype(jnp.bfloat16), 'fsdp', scatter_dimensi...  74.7 us
    reduce_scatter x1, waiting for transfers between devices, per_device(): lax.psum_scatter(output_grad.astype(jnp.bfloat16), 'fsdp', scatter_dimens...  44.7 us
    reduce_scatter x1, waiting for transfers between devices, per_device(): lax.psum_scatter(position_grad.astype(jnp.bfloat16), 'fsdp', scatter_dime...  44.5 us
    all_gather x1, waiting for transfers between devices, per_device(): lax.all_gather(outer_weight, 'fsdp', axis=0, tiled=True)  44.2 us
    all_gather x1, waiting for transfers between devices, per_device(): lax.all_gather(inner_weight, 'fsdp', axis=0, tiled=True)  42.6 us
    pallas_call x1, Pallas kernels, attn_bwd(): pl.pallas_call(attn_bwd_kernel, grid=(heads,), in_specs=[col(seg), col(se...  42.4 us
  transfers between devices with their start and end apart: 17, of which 9 were waited for; matrix products, arithmetic and copies ran while one was open for 22% of the time, Pallas kernels for 8%

profile of v1, /device:TPU:0, one launch (start us, length us, event | category | flops | bytes accessed | tf_op | source)
XLA Modules:
  0.0 938.2 jit_solution(3675710730113464715)
XLA Ops:
  14.3 4.5 convolution_convert_fusion.2
  19.5 10.3 %all-gather.3 = bf16[8,1,128]{2,1,0:T(2,128)(2,1)S(1)} all-gather(bf16[1,1,128]{2,1,0:T(2,128)(2,1)S(1)} %bitcast.139), channel_id=1, replica_groups=mesh['dp'=4,'fsdp'=8] {'fsdp'}, dimensions={0}, use_global_device_ids=true | all-gather | bytes 2304 | tf_op jit(solution)/shard_map/all_gather | solution.py:190
  30.4 8.7 all-gather.2
  40.3 3.0 fusion.9
  43.4 4.5 fusion.7
  47.9 7.8 all-gather.1
  55.7 8.7 all-gather
  65.2 7.8 all-gather.5
  73.5 8.7 all-gather.4
  82.8 8.1 all-gather.6
  91.5 12.9 %fusion.10 = (bf16[1536,512]{1,0:T(8,128)(2,1)}, bf16[1536,512]{1,0:T(8,128)(2,1)}) fusion(f32[512]{0:T(512)S(1)} %multiply_exponential_fusion, f32[1536]{0:T(1024)S(1)} %subtract_convert_fusion), kind=kLoop, calls=%fused_computation.27 | loop fusion | flops 2359296 | bytes 3153920 | tf_op jit(solution)/shard_map/convert.5
  104.5 4.3 add_convert_fusion
  108.8 3.7 add_convert_fusion.2
  114.4 7.6 convolution_convert_fusion.5.k_ref
  122.0 7.6 convolution_convert_fusion.4.v_ref
  129.9 6.1 convolution_convert_fusion.3.r_ref
  136.1 28.7 %attn_fwd.1 = (bf16[512,1024]{1,0:T(8,128)(2,1)S(1)}, bf16[8,512,1536]{2,1,0:T(8,128)(2,1)}) custom-call(bf16[512,1024]{1,0:T(8,128)(2,1)S(1)} %copy.55.qu_ref, bf16[512,1024]{1,0:T(8,128)(2,1)S(1)} %copy-done, bf16[1536,1024]{1,0:T(8,128)(2,1)S(1)} %copy-done.6, bf16[1536,1024]{1,0:T(8,128)(2,1)S(1)} %copy-done.7, ...), custom_call_target="tpu_custom_call" | custom-call | flops 4831838208 | bytes 25165824 | tf_op jit(solution)/shard_map/attn_fwd/pallas_call | solution.py:81
  167.5 4.0 fusion.54
  173.2 42.6 %all-gather.28.cloned.1.call-done = bf16[1024,4096]{1,0:T(8,128)(2,1)} async-done(((bf16[128,4096]{1,0:T(8,128)(2,1)}), bf16[1024,4096]{1,0:T(8,128)(2,1)}) %all-gather.28.cloned.1.call-update) | async-done | bytes 8388624 | tf_op jit(solution)/shard_map/all_gather | solution.py:231
  215.7 12.1 %fusion.49 = f32[512,4096]{1,0:T(8,128)} fusion(bf16[1024,4096]{1,0:T(8,128)(2,1)} %all-gather.28.cloned.1.call-done, f32[1,512,1024]{2,1,0:T(8,128)} %copy-done.22, f32[1024]{0:T(1024)S(1)} %bitcast.135, f32[1024]{0:T(1024)S(1)} %bitcast.118, f32[512]{0:T(512)S(1)} %add_rsqrt_fusion.1, f32[512]{0:T(512)S(1)} %broadcast_multiply_fusion.6), kind=kOutput, calls=%fused_computation.120 | convolution fusion | flops 4297588736 | bytes 18886656 | tf_op jit(solution)/shard_map/bsd,df->bsf/dot_general | solution.py:240
  227.9 44.2 %all-gather.30.cloned.1.call-done = bf16[4096,1024]{1,0:T(8,128)(2,1)} async-done(((bf16[512,1024]{1,0:T(8,128)(2,1)}), bf16[4096,1024]{1,0:T(8,128)(2,1)}) %all-gather.30.cloned.1.call-update) | async-done | bytes 8388624 | tf_op jit(solution)/shard_map/all_gather | solution.py:233
  272.1 15.3 %fusion.55 = (bf16[4096]{0:T(1024)(128)(2,1)}, bf16[512,4096]{1,0:T(8,128)(2,1)}) fusion(f32[512,4096]{1,0:T(8,128)} %fusion.49, f32[4096]{0:T(1024)S(1)} %bitcast.131, bf16[4096,1024]{1,0:T(8,128)(2,1)} %all-gather.30.cloned.1.call-done, bf16[1,512,1024]{2,1,0:T(8,128)(2,1)} %param.48), kind=kOutput, calls=%fused_computation.125 | convolution fusion | flops 4341100544 | bytes 22044672 | tf_op jit(solution)/shard_map/bsd,fd->bsf/dot_general | solution.py:270
  287.3 7.7 fusion.15
  297.9 2.3 convolution_convert_fusion.10
  300.2 2.3 copy.60.g_ref
  306.1 42.4 %attn_bwd.1 = (bf16[512,1024]{1,0:T(8,128)(2,1)S(1)}, bf16[1024,1536]{1,0:T(8,128)(2,1)S(1)}, bf16[1024,1536]{1,0:T(8,128)(2,1)S(1)}, bf16[1024,1536]{1,0:T(8,128)(2,1)}, f32[8,1024]{1,0:T(8,128)S(1)}) custom-call(bf16[512,1024]{1,0:T(8,128)(2,1)S(1)} %copy.55.qu_ref, bf16[512,1024]{1,0:T(8,128)(2,1)S(1)} %copy-done.1, bf16[1024,512]{1,0:T(8,128)(2,1)S(1)} %bitcast.113, ...), custom_call_target="tpu_custom_call" | custom-call | flops 12884901888 | bytes 36700160 | tf_op jit(solution)/shard_map/attn_bwd/pallas_call | solution.py:128
  352.8 4.4 convolution_convert_fusion.9
  357.2 6.7 convolution_convert_fusion.8
  364.2 7.8 convolution_convert_fusion.7
  372.1 7.7 fusion.22
  379.8 4.4 convolution_convert_fusion.6
  384.4 9.3 convolution_convert_fusion.1
  394.9 13.6 %convolution_convert_fusion = bf16[4096,1024]{1,0:T(8,128)(2,1)} fusion(bf16[1,512,1024]{2,1,0:T(8,128)(2,1)S(1)} %copy-done.28, f32[512,4096]{1,0:T(8,128)} %fusion.49, f32[4096]{0:T(1024)} %bitcast.130), kind=kOutput, calls=%fused_computation.12 | convolution fusion | flops 4320133120 | bytes 17842176 | tf_op jit(solution)/shard_map/bsf,bsd->fd/dot_general | solution.py:268
  409.2 8.9 all-gather.7
  418.7 8.3 all-gather.8
  431.2 5.2 fusion.25
  439.2 5.5 fusion.56
  444.8 11.8 %fusion.51 = (bf16[1024]{0:T(1024)(128)(2,1)S(1)}, bf16[1024]{0:T(1024)(128)(2,1)S(1)}, f32[1536]{0:T(1024)S(1)}, f32[1536]{0:T(1024)S(1)}, f32[1,1536,1024]{2,1,0:T(8,128)}) fusion(f32[1536]{0:T(1024)S(1)} %add_rsqrt_fusion, f32[1536]{0:T(1024)S(1)} %copy-done.36, bf16[1,512,1024]{2,1,0:T(8,128)(2,1)S(1)} %copy-done.19, ...), kind=kOutput, calls=%fused_computation.121 | convolution fusion | flops 3247959040 | bytes 23101440 | tf_op jit(solution)/shard_map/bse,de->bsd/dot_general | solution.py:342
  456.7 23.5 %all-reduce.10 = (bf16[1024]{0:T(1024)(128)(2,1)S(1)}, bf16[1024]{0:T(1024)(128)(2,1)S(1)}, bf16[1024]{0:T(1024)(128)(2,1)S(1)}, bf16[1024]{0:T(1024)(128)(2,1)S...) all-reduce(bf16[1024]{0:T(1024)(128)(2,1)S(1)} %get-tuple-element.3, ...), channel_id=2, replica_groups=mesh['dp'=4,'fsdp'=8] {'fsdp'}, use_global_device_ids=true, to_apply=%region_9.10.clone | all-reduce | flops 12288 | bytes 49152
  480.9 11.9 %all-reduce.11 = (bf16[128]{0:T(256)(128)(2,1)S(1)}, bf16[128]{0:T(256)(128)(2,1)S(1)}, bf16[128]{0:T(256)(128)(2,1)S(1)}, bf16[128]{0:T(256)(128)(2,1)S(1)}, bf...) all-reduce(bf16[128]{0:T(256)(128)(2,1)S(1)} %dynamic-slice.1, ...), channel_id=1, replica_groups=mesh['dp'=4,'fsdp'=8] {'dp'}, use_global_device_ids=true, to_apply=%region_10.11 | all-reduce | flops 1536 | bytes 6144 | tf_op jit(solution)/shard_map/psum | solution.py:381
  493.9 25.6 %reduce-scatter.13.cloned.1.call-done = bf16[128,1024]{1,0:T(8,128)(2,1)} async-done(((bf16[1024,1024]{1,0:T(8,128)(2,1)}), bf16[128,1024]{1,0:T(8,128)(2,1)}) %reduce-scatter.13.cloned.1.call-update) | async-done | bytes 262160 | tf_op jit(solution)/shard_map/reduce_scatter | solution.py:364
  519.5 44.5 %reduce-scatter.15.cloned.1.call-done = bf16[128,1024]{1,0:T(8,128)(2,1)} async-done(((bf16[1024,1024]{1,0:T(8,128)(2,1)}), bf16[128,1024]{1,0:T(8,128)(2,1)}) %reduce-scatter.15.cloned.1.call-update) | async-done | bytes 262160 | tf_op jit(solution)/shard_map/reduce_scatter | solution.py:367
  564.0 44.7 %reduce-scatter.17.cloned.1.call-done = bf16[128,1024]{1,0:T(8,128)(2,1)} async-done(((bf16[1024,1024]{1,0:T(8,128)(2,1)}), bf16[128,1024]{1,0:T(8,128)(2,1)}) %reduce-scatter.17.cloned.1.call-update) | async-done | bytes 262160 | tf_op jit(solution)/shard_map/reduce_scatter | solution.py:376
  608.7 74.7 %reduce-scatter.19.cloned.1.call-done = bf16[128,4096]{1,0:T(8,128)(2,1)} async-done(((bf16[1024,4096]{1,0:T(8,128)(2,1)}), bf16[128,4096]{1,0:T(8,128)(2,1)}) %reduce-scatter.19.cloned.1.call-update) | async-done | bytes 1048592 | tf_op jit(solution)/shard_map/reduce_scatter | solution.py:289
  683.4 75.0 %reduce-scatter.21.cloned.1.call-done = bf16[512,1024]{1,0:T(8,128)(2,1)} async-done(((bf16[4096,1024]{1,0:T(8,128)(2,1)}), bf16[512,1024]{1,0:T(8,128)(2,1)}) %reduce-scatter.21.cloned.1.call-update) | async-done | bytes 1048592 | tf_op jit(solution)/shard_map/reduce_scatter | solution.py:295
  762.1 4.6 fusion.14
  766.7 12.5 %fusion.20 = bf16[1,512,1024]{2,1,0:T(8,128)(2,1)} fusion(f32[1,512,1024]{2,1,0:T(8,128)S(1)} %copy-done.24, bf16[4096,1024]{1,0:T(8,128)(2,1)} %all-gather.30.cloned.1.call-done, f32[1024]{0:T(1024)S(1)} %bitcast.133, f32[512,4096]{1,0:T(8,128)} %fusion.49, f32[4096]{0:T(1024)S(1)} %bitcast.132), kind=kOutput, calls=%fused_computation.45 | convolution fusion | flops 4317511680 | bytes 19943424 | tf_op jit(solution)/shard_map/bsf,fd->bsd/dot_general | solution.py:246
  779.2 139.5 %all-reduce.15.cloned.1.call-done = (bf16[128,1024]{1,0:T(8,128)(2,1)}, bf16[128,1024]{1,0:T(8,128)(2,1)}, bf16[128,1024]{1,0:T(8,128)(2,1)}, bf16[128,1024]{1,0...) async-done(((bf16[128,1024]{1,0:T(8,128)(2,1)}, bf16[128,1024]{1,0:T(8,128)(2,1)}, ...) | async-done | bytes 4194320 | tf_op jit(solution)/shard_map/psum | solution.py:383
  (254 shorter events, 54.6 us)
Async XLA Ops:
  7.2 6.3 copy-start.16
  7.2 101.6 %all-gather.18.cloned.1.call-start = ((), (), s32[]{:S(2)}) async-start(), calls=%async_computation.8 | async-start | bytes 2359296 | tf_op jit(solution)/shard_map/all_gather | solution.py:185
  7.9 106.5 %all-gather.20.cloned.1.call-start = ((), (), s32[]{:S(2)}) async-start(), calls=%async_computation.9 | async-start | bytes 2359296 | tf_op jit(solution)/shard_map/all_gather | solution.py:186
  8.7 113.3 %all-gather.22.cloned.1.call-start = ((), (), s32[]{:S(2)}) async-start(), calls=%async_computation.10 | async-start | bytes 2359296 | tf_op jit(solution)/shard_map/all_gather | solution.py:187
  9.4 120.5 %all-gather.24.cloned.1.call-start = ((), (), s32[]{:S(2)}) async-start(), calls=%async_computation.11 | async-start | bytes 2359296 | tf_op jit(solution)/shard_map/all_gather | solution.py:188
  10.0 157.5 %all-gather.26.cloned.1.call-start = ((), (), s32[]{:S(2)}) async-start(), calls=%async_computation.12 | async-start | bytes 2359296 | tf_op jit(solution)/shard_map/all_gather | solution.py:191
  10.6 205.1 %all-gather.28.cloned.1.call-start = ((), (), s32[]{:S(2)}) async-start(), calls=%async_computation.13 | async-start | bytes 9437184 | tf_op jit(solution)/shard_map/all_gather | solution.py:231
  11.2 260.9 %all-gather.30.cloned.1.call-start = ((), (), s32[]{:S(2)}) async-start(), calls=%async_computation.14 | async-start | bytes 9437184 | tf_op jit(solution)/shard_map/all_gather | solution.py:233
  11.9 419.3 %all-gather.32.cloned.1.call-start = ((), (), s32[]{:S(2)}) async-start(), calls=%async_computation.15 | async-start | bytes 7077888 | tf_op jit(solution)/shard_map/all_gather | solution.py:235
  12.7 481.2 %reduce-scatter.23.cloned.1.call-start = ((), (), s32[]{:S(2)}) async-start(), calls=%async_computation.23 | async-start | bytes 7077888 | tf_op jit(solution)/shard_map/reduce_scatter | solution.py:301
  18.8 11.6 %copy-start.58 = (bf16[128]{0:T(256)(128)(2,1)S(1)}, bf16[128]{0:T(256)(128)(2,1)}, u32[]{:S(2)}) copy-start(bf16[128]{0:T(256)(128)(2,1)} %param.37) | copy-start | bytes 772
  18.8 20.9 %copy-start.18 = (bf16[1,512,1024]{2,1,0:T(8,128)(2,1)S(1)}, bf16[1,512,1024]{2,1,0:T(8,128)(2,1)}, u32[]{:S(2)}) copy-start(bf16[1,512,1024]{2,1,0:T(8,128)(2,1)} %param.25) | copy-start | bytes 3145732
  18.8 20.9 %copy-start.20 = (bf16[1,512,1024]{2,1,0:T(8,128)(2,1)S(1)}, bf16[1,512,1024]{2,1,0:T(8,128)(2,1)}, u32[]{:S(2)}) copy-start(bf16[1,512,1024]{2,1,0:T(8,128)(2,1)} %param.27) | copy-start | bytes 3145732
  18.9 475.0 %reduce-scatter.9.cloned.1.call-start = ((), (), s32[]{:S(2)}) async-start(), calls=%async_computation.16 | async-start | bytes 2359296 | tf_op jit(solution)/shard_map/reduce_scatter | solution.py:358
  40.3 64.2 %copy-start.35 = (f32[1536]{0:T(1024)}, f32[1536]{0:T(1024)S(1)}, u32[]{:S(2)}) copy-start(f32[1536]{0:T(1024)S(1)} %broadcast_multiply_fusion.3) | copy-start | bytes 18436
  43.3 401.3 %copy-start.37 = (f32[1536]{0:T(1024)}, f32[1536]{0:T(1024)S(1)}, u32[]{:S(2)}) copy-start(f32[1536]{0:T(1024)S(1)} %add_rsqrt_fusion) | copy-start | bytes 18436
  43.4 12.3 %copy-start.60 = (bf16[128]{0:T(256)(128)(2,1)S(1)}, bf16[128]{0:T(256)(128)(2,1)}, u32[]{:S(2)}) copy-start(bf16[128]{0:T(256)(128)(2,1)} %param.31) | copy-start | bytes 772
  43.4 21.1 %copy-start.54 = (s32[1,512]{1,0:T(1,128)S(1)}, s32[1,512]{1,0:T(1,128)}, u32[]{:S(2)}) copy-start(s32[1,512]{1,0:T(1,128)} %param.30) | copy-start | bytes 6148
  43.4 21.8 %copy-start.61 = (bf16[128]{0:T(256)(128)(2,1)S(1)}, bf16[128]{0:T(256)(128)(2,1)}, u32[]{:S(2)}) copy-start(bf16[128]{0:T(256)(128)(2,1)} %param.41) | copy-start | bytes 772
  43.4 30.1 %copy-start.62 = (bf16[128]{0:T(256)(128)(2,1)S(1)}, bf16[128]{0:T(256)(128)(2,1)}, u32[]{:S(2)}) copy-start(bf16[128]{0:T(256)(128)(2,1)} %param.40) | copy-start | bytes 772
  43.4 39.4 %copy-start.56 = (bf16[512]{0:T(512)(128)(2,1)S(1)}, bf16[512]{0:T(512)(128)(2,1)}, u32[]{:S(2)}) copy-start(bf16[512]{0:T(512)(128)(2,1)} %param.43) | copy-start | bytes 3076
  55.7 48.8 %copy-start.42 = (f32[8,1,128]{2,1,0:T(1,128)}, f32[8,1,128]{2,1,0:T(1,128)S(1)}, u32[]{:S(2)}) copy-start(f32[8,1,128]{2,1,0:T(1,128)S(1)} %convert_element_type.395) | copy-start | bytes 12292
  64.4 40.1 %copy-start.39 = (f32[8,1,128]{2,1,0:T(1,128)}, f32[8,1,128]{2,1,0:T(1,128)S(1)}, u32[]{:S(2)}) copy-start(f32[8,1,128]{2,1,0:T(1,128)S(1)} %convert_element_type.394) | copy-start | bytes 12292
  167.5 48.3 %copy-start.38 = (f32[8,1,128]{2,1,0:T(1,128)S(1)}, f32[8,1,128]{2,1,0:T(1,128)}, u32[]{:S(2)}) copy-start(f32[8,1,128]{2,1,0:T(1,128)} %convert_element_type.398) | copy-start | bytes 12292
  167.5 48.3 %copy-start.50 = (f32[8,1,128]{2,1,0:T(1,128)S(1)}, f32[8,1,128]{2,1,0:T(1,128)}, u32[]{:S(2)}) copy-start(f32[8,1,128]{2,1,0:T(1,128)} %convert_element_type.399) | copy-start | bytes 12292
  173.2 122.7 %copy-start.48 = (f32[512]{0:T(512)}, f32[512]{0:T(512)S(1)}, u32[]{:S(2)}) copy-start(f32[512]{0:T(512)S(1)} %add_rsqrt_fusion.1) | copy-start | bytes 6148
  215.7 56.3 %copy-start.44 = (f32[8,1,512]{2,1,0:T(1,128)S(1)}, f32[8,1,512]{2,1,0:T(1,128)}, u32[]{:S(2)}) copy-start(f32[8,1,512]{2,1,0:T(1,128)} %convert_element_type.400) | copy-start | bytes 49156
  272.1 15.3 %copy-start.23 = (f32[1,512,1024]{2,1,0:T(8,128)S(1)}, f32[1,512,1024]{2,1,0:T(8,128)}, u32[]{:S(2)}) copy-start(f32[1,512,1024]{2,1,0:T(8,128)} %copy-done.22) | copy-start | bytes 6291460
  272.1 15.3 %copy-start.64 = (bf16[1024,4096]{1,0:T(8,128)(2,1)S(1)}, bf16[1024,4096]{1,0:T(8,128)(2,1)}, u32[]{:S(2)}) copy-start(bf16[1024,4096]{1,0:T(8,128)(2,1)} %all-gather.28.cloned.1.call-done) | copy-start | bytes 25165828
  287.3 8.5 copy-start.27
  306.1 46.6 %copy-start.40 = (f32[8,1,128]{2,1,0:T(1,128)S(1)}, f32[8,1,128]{2,1,0:T(1,128)}, u32[]{:S(2)}) copy-start(f32[8,1,128]{2,1,0:T(1,128)} %copy-done.39) | copy-start | bytes 12292
  306.1 46.6 %copy-start.43 = (f32[8,1,128]{2,1,0:T(1,128)S(1)}, f32[8,1,128]{2,1,0:T(1,128)}, u32[]{:S(2)}) copy-start(f32[8,1,128]{2,1,0:T(1,128)} %copy-done.42) | copy-start | bytes 12292
  357.2 136.7 %reduce-scatter.11.cloned.1.call-start = ((), (), s32[]{:S(2)}) async-start(), calls=%async_computation.17 | async-start | bytes 2359296 | tf_op jit(solution)/shard_map/reduce_scatter | solution.py:361
  363.9 155.6 %reduce-scatter.13.cloned.1.call-start = ((), (), s32[]{:S(2)}) async-start(), calls=%async_computation.18 | async-start | bytes 2359296 | tf_op jit(solution)/shard_map/reduce_scatter | solution.py:364
  364.2 7.9 copy-start.29
  372.0 192.0 %reduce-scatter.15.cloned.1.call-start = ((), (), s32[]{:S(2)}) async-start(), calls=%async_computation.19 | async-start | bytes 2359296 | tf_op jit(solution)/shard_map/reduce_scatter | solution.py:367
  372.0 7.8 copy-start.5
  379.8 229.0 %reduce-scatter.17.cloned.1.call-start = ((), (), s32[]{:S(2)}) async-start(), calls=%async_computation.20 | async-start | bytes 2359296 | tf_op jit(solution)/shard_map/reduce_scatter | solution.py:376
  384.3 299.1 %reduce-scatter.19.cloned.1.call-start = ((), (), s32[]{:S(2)}) async-start(), calls=%async_computation.21 | async-start | bytes 9437184 | tf_op jit(solution)/shard_map/reduce_scatter | solution.py:289
  393.7 364.7 %reduce-scatter.21.cloned.1.call-start = ((), (), s32[]{:S(2)}) async-start(), calls=%async_computation.22 | async-start | bytes 9437184 | tf_op jit(solution)/shard_map/reduce_scatter | solution.py:295
  408.6 510.1 %all-reduce.15.cloned.1.call-start = ((), (), s32[]{:S(2)}) async-start(), calls=%async_computation.24 | async-start | bytes 8388608 | tf_op jit(solution)/shard_map/psum | solution.py:383
  444.8 11.9 %copy-start.46 = (bf16[4096]{0:T(1024)(128)(2,1)S(1)}, bf16[4096]{0:T(1024)(128)(2,1)}, u32[]{:S(2)}) copy-start(bf16[4096]{0:T(1024)(128)(2,1)} %get-tuple-element.81) | copy-start | bytes 24580
  444.8 11.9 %copy-start.47 = (bf16[1024]{0:T(1024)(128)(2,1)S(1)}, bf16[1024]{0:T(1024)(128)(2,1)}, u32[]{:S(2)}) copy-start(bf16[1024]{0:T(1024)(128)(2,1)} %get-tuple-element.40) | copy-start | bytes 6148
  444.8 11.9 %copy-start.53 = (bf16[1024]{0:T(1024)(128)(2,1)S(1)}, bf16[1024]{0:T(1024)(128)(2,1)}, u32[]{:S(2)}) copy-start(bf16[1024]{0:T(1024)(128)(2,1)} %get-tuple-element.38) | copy-start | bytes 6148
  456.6 305.5 %slice-start = ((f32[1536]{0:T(1024)}), f32[512]{0:T(512)S(1)}, s32[]{:S(2)}) async-start(f32[1536]{0:T(1024)} %copy-done.37), calls=%async_computation.25 | async-start | bytes 4096 | tf_op jit(solution)/shard_map/slice | solution.py:350
  918.7 7.4 copy-start.34
  918.7 8.2 copy-start.32
  920.6 7.9 copy-start.31
  (39 other events, 137.1 us)
Sparse Core Ops, SparseCore 0:
  9.9 30.5 all-gather.17
  42.5 27.8 all-gather.19
  72.3 27.8 all-gather.21
  102.0 27.8 all-gather.23
  131.6 27.8 all-gather.25
  161.3 54.3 all-gather.27
  217.6 54.3 all-gather.29
  273.9 45.5 all-gather.31
  322.9 61.8 reduce-scatter.22
  388.8 41.2 reduce-scatter.8
  433.4 41.2 reduce-scatter.10
  478.2 41.2 reduce-scatter.12
  522.8 41.1 reduce-scatter.14
  567.5 41.2 reduce-scatter.16
  612.0 71.2 reduce-scatter.18
  687.1 71.2 reduce-scatter.20
  761.2 157.4 all-reduce.14

commit v2 on v1

v2 whole, which is shorter than its diff:
```python
import functools
import math

import jax
import jax.numpy as jnp
from jax import lax
from jax.experimental import pallas as pl
from jax.experimental.pallas import tpu as pltpu
from jax.sharding import PartitionSpec as P

HEADS = 8
DH = 128
RATE = 3
BLK = 128
NEG = -1.2e10
f32 = jnp.float32
bf16 = jnp.bfloat16


EPSILON = 1e-05
MASKED = -1000000000.0


def smooth_gate(values):
    return jax.nn.gelu(values, approximate=True)


def norm_parts(rows, gain, shift):
    center = jnp.mean(rows, axis=-1, keepdims=True)
    centered = rows - center
    spread = lax.rsqrt(jnp.mean(centered * centered, axis=-1, keepdims=True) + EPSILON)
    scaled = centered * spread
    return (scaled * gain.astype(jnp.float32) + shift.astype(jnp.float32), scaled, spread)


def norm_back(grad, scaled, spread, gain):
    inner = grad * gain.astype(jnp.float32)
    return spread * (
        inner
        - jnp.mean(inner, axis=-1, keepdims=True)
        - scaled * jnp.mean(inner * scaled, axis=-1, keepdims=True)
    )


def positions(count, width):
    distance = (count - 1 - jnp.arange(count, dtype=jnp.int32)).astype(jnp.float32)
    rates = jnp.exp(
        jnp.arange(0, width, 2, dtype=jnp.int32).astype(jnp.float32) * (-math.log(10000.0) / width)
    )
    angle = distance[:, None] * rates[None, :]
    return jnp.concatenate([jnp.sin(angle), jnp.cos(angle)], axis=1)


def dot_nt(a,b): return lax.dot_general(a,b,(((1,),(1,)),((),())),preferred_element_type=f32)
def dot_nn(a,b): return lax.dot_general(a,b,(((1,),(0,)),((),())),preferred_element_type=f32)

def attn_fwd_kernel(qu_ref,qv_ref,k_ref,v_ref,r_ref,bias_ref,o_ref,p_ref):
    seg=qu_ref.shape[0]; total=k_ref.shape[0]; old=total-seg
    c=math.log2(math.e)/math.sqrt(DH)
    for ib in range(seg//BLK):
        rows=pl.ds(ib*BLK,BLK)
        L=old+(ib+1)*BLK
        qu=qu_ref[rows,:]; qv=qv_ref[rows,:]
        raw=dot_nt(qv,r_ref[pl.ds(total-L,L),:])
        z=dot_nt(qu,k_ref[pl.ds(0,L),:])+pltpu.roll(raw,L-(BLK-1),axis=1,stride=1,stride_axis=0)
        M=L-BLK
        za=z[:,:M]+bias_ref[:,:M]
        rr=lax.broadcasted_iota(jnp.int32,(BLK,BLK),0); cc=lax.broadcasted_iota(jnp.int32,(BLK,BLK),1)
        zb=z[:,M:]
        zb=jnp.where(cc==rr,zb,jnp.where(cc<rr,zb+bias_ref[:,pl.ds(M,BLK)],NEG))
        top=jnp.maximum(jnp.max(za,axis=1,keepdims=True),jnp.max(zb,axis=1,keepdims=True))
        ea=jnp.exp2((za-top)*c); eb=jnp.exp2((zb-top)*c)
        inv=1.0/(jnp.sum(ea,axis=1,keepdims=True)+jnp.sum(eb,axis=1,keepdims=True))
        pa=(ea*inv).astype(bf16); pb=(eb*inv).astype(bf16)
        p_ref[0,rows,pl.ds(0,M)]=pa
        p_ref[0,rows,pl.ds(M,BLK)]=pb
        o_ref[rows,:]=(dot_nn(pa,v_ref[pl.ds(0,M),:])+dot_nn(pb,v_ref[pl.ds(M,BLK),:])).astype(bf16)

def attn_fwd(qu,qv,k,v,r,bias,first,heads):
    seg,width=qu.shape[0],heads*DH; total=k.shape[0]
    col=lambda n: pl.BlockSpec((n,DH),lambda h:(0,h+first))
    out=lambda n: pl.BlockSpec((n,DH),lambda h:(0,h))
    return pl.pallas_call(attn_fwd_kernel,grid=(heads,),
        in_specs=[col(seg),col(seg),col(total),col(total),col(total),pl.BlockSpec((1,total),lambda h:(0,0))],
        out_specs=[out(seg),pl.BlockSpec((1,seg,total),lambda h:(h,0,0))],
        out_shape=[jax.ShapeDtypeStruct((seg,width),bf16),jax.ShapeDtypeStruct((heads,seg,total),bf16)],
        cost_estimate=pl.CostEstimate(flops=6*seg*total*width,bytes_accessed=2*(3*seg*width+3*total*width+heads*seg*total),transcendentals=heads*seg*total),
        compiler_params=pltpu.CompilerParams(vmem_limit_bytes=40<<20),name="attn_fwd")(qu,qv,k,v,r,bias)

def attn_bwd_kernel(qu_ref,qv_ref,qut_ref,qvrt_ref,k_ref,v_ref,r_ref,p_ref,g_ref,gt_ref,dq_ref,dkt_ref,dvt_ref,drt_ref,sums_ref,dk_acc,dv_acc,dr_acc):
    seg=g_ref.shape[0]; total=k_ref.shape[0]; old=total-seg
    scale=1.0/math.sqrt(DH)
    rr=lax.broadcasted_iota(jnp.int32,(BLK,BLK),0); cc=lax.broadcasted_iota(jnp.int32,(BLK,BLK),1)
    flip=(rr+cc==BLK-1).astype(bf16)
    su=jnp.zeros((1,DH),f32); sv=jnp.zeros((1,DH),f32)
    nb=seg//BLK
    for ib in range(nb-1,-1,-1):
        rows=pl.ds(ib*BLK,BLK)
        L=old+(ib+1)*BLK
        g=g_ref[rows,:]; gt=gt_ref[:,rows]; qut=qut_ref[:,rows]
        plow=p_ref[0,rows,pl.ds(0,L)]
        p=plow.astype(f32)
        dp=dot_nt(g,v_ref[pl.ds(0,L),:])
        d=jnp.sum(p*dp,axis=1,keepdims=True)
        dz=(p*(dp-d)*scale).astype(bf16)
        dvt=dot_nn(gt,plow)
        dkt=dot_nn(qut,dz)
        dqu=dot_nn(dz,k_ref[pl.ds(0,L),:])
        rev=dot_nn(flip,dz)
        raw=pltpu.roll(rev,0,axis=1,stride=1,stride_axis=0).astype(bf16)
        T=pl.ds(total-L,L)
        dqv_rev=dot_nn(raw,r_ref[T,:])
        qvr=dot_nt(qvrt_ref[:,rows],flip).astype(bf16)
        drt=dot_nn(qvr,raw)
        dqv=lax.dot_general(flip.astype(f32),dqv_rev,(((1,),(0,)),((),())),preferred_element_type=f32,precision=lax.Precision.HIGHEST)
        su+=jnp.sum(dqu,axis=0,keepdims=True); sv+=jnp.sum(dqv,axis=0,keepdims=True)
        dq_ref[rows,:]=(dqu+dqv).astype(bf16)
        J=pl.ds(0,L)
        if ib==nb-1:
            dv_acc[...]=dvt; dk_acc[...]=dkt; dr_acc[...]=drt
        else:
            dv_acc[:,J]+=dvt; dk_acc[:,J]+=dkt; dr_acc[:,T]+=drt
    dkt_ref[...]=dk_acc[...].astype(bf16); dvt_ref[...]=dv_acc[...].astype(bf16); drt_ref[...]=dr_acc[...].astype(bf16)
    sums_ref[0:1,:]=su; sums_ref[1:2,:]=sv

def attn_bwd(qu,qv,qut,qvt,k,v,r,p,g,gt,first,heads):
    seg,width=qu.shape[0],heads*DH; total=k.shape[0]
    col=lambda n: pl.BlockSpec((n,DH),lambda h:(0,h+first))
    row=lambda n: pl.BlockSpec((DH,n),lambda h:(h+first,0))
    out=lambda n: pl.BlockSpec((n,DH),lambda h:(0,h))
    rowout=lambda n: pl.BlockSpec((DH,n),lambda h:(h,0))
    return pl.pallas_call(attn_bwd_kernel,grid=(heads,),
        in_specs=[col(seg),col(seg),row(seg),row(seg),col(total),col(total),col(total),pl.BlockSpec((1,seg,total),lambda h:(h,0,0)),col(seg),row(seg)],
        out_specs=[out(seg),rowout(total),rowout(total),rowout(total),pl.BlockSpec((8,DH),lambda h:(0,h))],
        out_shape=[jax.ShapeDtypeStruct((seg,width),bf16)]+[jax.ShapeDtypeStruct((width,total),bf16)]*3+[jax.ShapeDtypeStruct((8,width),f32)],
        scratch_shapes=[pltpu.VMEM((DH,total),f32)]*3,
        cost_estimate=pl.CostEstimate(flops=16*seg*total*width,bytes_accessed=2*(5*seg*width+6*total*width+heads*seg*total),transcendentals=0),
        compiler_params=pltpu.CompilerParams(vmem_limit_bytes=40<<20),name="attn_bwd")(qu,qv,qut,qvt,k,v,r,p,g,gt)


def hop(value, move):
    dp, fsdp = lax.axis_size("dp"), lax.axis_size("fsdp")
    pairs = []
    for z in range(dp):
        for f in range(fsdp):
            to = move(z, f)
            if to is not None:
                pairs.append((z * fsdp + f, to[0] * fsdp + to[1]))
    return lax.ppermute(value, ("dp", "fsdp"), pairs)


def assemble_kernel(count, places, index_ref, *refs):
    parts = len(places)
    slots, outs = refs[:count], refs[count : count + parts]
    whole, arrive, leave = refs[count + parts : -2], refs[-2], refs[-1]
    coming, going = [], []
    for s in range(count):
        for p, (start, rows) in enumerate(places):
            at = pl.ds(pl.multiple_of(index_ref[s] * rows, 16), rows)
            n = s * parts + p
            coming.append(
                pltpu.make_async_copy(
                    slots[s].at[pl.ds(start, rows), :], whole[p].at[at, :], arrive.at[n]
                )
            )
            going.append(
                pltpu.make_async_copy(whole[p].at[at, :], outs[p].at[at, :], leave.at[n])
            )
    for copy in coming:
        copy.start()
    for copy, onward in zip(coming, going):
        copy.wait()
        onward.start()
    for onward in going:
        onward.wait()


def assemble(slots, index, heights):
    count, cols, dtype = len(slots), slots[0].shape[1], slots[0].dtype
    places, start = [], 0
    for rows in heights:
        places.append((start, rows))
        start += rows
    moved = 2 * count * start * cols * 2
    return pl.pallas_call(
        functools.partial(assemble_kernel, count, tuple(places)),
        grid_spec=pltpu.PrefetchScalarGridSpec(
            num_scalar_prefetch=1,
            grid=(1,),
            in_specs=[pl.BlockSpec(memory_space=pl.ANY)] * count,
            out_specs=[pl.BlockSpec(memory_space=pl.ANY)] * len(heights),
            scratch_shapes=[pltpu.VMEM((count * rows, cols), dtype) for rows in heights]
            + [pltpu.SemaphoreType.DMA((count * len(heights),))] * 2,
        ),
        out_shape=[jax.ShapeDtypeStruct((count * rows, cols), dtype) for rows in heights],
        cost_estimate=pl.CostEstimate(flops=0, bytes_accessed=moved, transcendentals=0),
        compiler_params=pltpu.CompilerParams(vmem_limit_bytes=16 << 20),
        name="assemble",
    )(index, *slots)


def cut(*values):
    return lax.optimization_barrier(values)


def first_hop(w):
    return hop(w, lambda z, f: (z, f ^ (4 if z % 2 else 2)))


def second_hop(w):
    return hop(w, lambda z, f: (z, f ^ (2 if z % 2 else 4)))


def plane_hop(w):
    return hop(w, lambda z, f: (z ^ 1, f))


def core_hop(w):
    return hop(w, lambda z, f: (z, f ^ 1))


def x_hop(w):
    return hop(w, lambda z, f: (z, f ^ 2))


def y_hop(w):
    return hop(w, lambda z, f: (z, f ^ 4))


def inward_hop(w):
    to = {0: 1, 3: 2}
    return hop(w, lambda z, f: (to[z], f) if z in to else None)


def middle_hop(w):
    return hop(w, lambda z, f: (3 - z, f) if z in (1, 2) else None)


def outward_hop(w):
    to = {1: 0, 2: 3}
    return hop(w, lambda z, f: (to[z], f) if z in to else None)


def slot_index():
    odd = lax.axis_index("dp") % 2
    near = 2 + 2 * odd
    masks = jnp.stack([0 * odd, near, 6 - near, 0 * odd + 6])
    return (lax.axis_index("fsdp") ^ jnp.concatenate([masks, masks ^ 1])).astype(jnp.int32)


def gather(shards):
    return [lax.all_gather(w, "fsdp", axis=0, tiled=True) for w in shards]


def reduce(grads, share):
    done = []
    for g in grads:
        part = lax.psum_scatter(g, "fsdp", scatter_dimension=0, tiled=True)
        done.append(lax.psum(part, "dp").astype(f32) * share)
    return done


def add_rows(out, parts, scale=None):
    rows = out.shape[0]
    height = 32 if rows % 32 == 0 else 16

    def one(i, carry):
        at = pl.ds(pl.multiple_of(i * height, height), height)
        total = parts[0][at, :].astype(f32)
        for part in parts[1:]:
            total = total + part[at, :].astype(f32)
        if scale is not None:
            total = total * scale
        out[at, :] = total.astype(out.dtype)
        return carry

    lax.fori_loop(0, rows // height, one, 0)


FULL_BUFFERS = ("mine", "theirs", "far", "half_x", "half_y", "to_y", "to_x", "got_y", "got_x")
LINE_BUFFERS = ("own", "end", "pair", "mid", "whole", "last", "out")


def tail_scratch(plan):
    shapes = []
    for full, rows, cols in plan:
        line = [pltpu.VMEM((rows, cols), bf16)] * 6 + [pltpu.VMEM((rows, cols), f32)]
        if full:
            half = pltpu.VMEM((rows // 2, cols), bf16)
            one = pltpu.VMEM((rows, cols), bf16)
            shapes += [pltpu.VMEM((4, rows, cols), bf16)] * 2 + [one, half, half] + [one] * 4
        shapes += line
        shapes += [pltpu.SemaphoreType.DMA((n,)) for n in (4, 11, 11, 1)]
    return shapes


def tail_kernel(plan, sources, share, count, *refs):
    grads, outs, scratch = refs[:count], refs[count : 2 * count], refs[2 * count :]
    z, f = lax.axis_index("dp"), lax.axis_index("fsdp")
    chip, core = f // 2, f % 2
    middle = (z == 1) | (z == 2)
    edge = jnp.logical_not(middle)
    inward = jnp.where(z < 2, 1, 2)
    outward = jnp.where(z < 2, 0, 3)
    mesh = pl.DeviceIdType.MESH
    sibling, by_x, by_y = (z, f ^ 1), (z, f ^ 2), (z, f ^ 4)
    items, at = [], 0
    for n, (full, rows, cols) in enumerate(plan):
        names = (FULL_BUFFERS if full else ()) + LINE_BUFFERS + ("local", "sent", "came", "stored")
        b = dict(zip(names, scratch[at : at + len(names)]))
        at += len(names)
        b.update(full=full, rows=rows, source=grads[sources[n][0]], first=sources[n][1])
        b.update(target=outs[sources[n][0]])
        items.append(b)

    def copy(b, n, src, dst, device):
        return pltpu.make_async_remote_copy(
            src_ref=src,
            dst_ref=dst,
            send_sem=b["sent"].at[n],
            recv_sem=b["came"].at[n],
            device_id=device,
            device_id_type=mesh,
        )

    def rows_of(b):
        return pl.ds(b["first"], b["rows"])

    def across_cores(b, s):
        block = (chip ^ (3 - s)) * 2 + 1 - core
        return copy(b, s, b["source"].at[block, rows_of(b), :], b["theirs"].at[s], sibling)

    def load(b, s):
        if not b["full"]:
            src, dst = b["source"].at[rows_of(b), :], b["own"]
        else:
            block = (chip ^ (3 - s)) * 2 + core
            src, dst = b["source"].at[block, rows_of(b), :], b["mine"].at[s]
        return pltpu.make_async_copy(src, dst, b["local"].at[s])

    def halves_out(b):
        half = b["rows"] // 2
        return (
            copy(b, 4, b["far"].at[pl.ds(0, half), :], b["half_x"], by_x),
            copy(b, 5, b["far"].at[pl.ds(half, half), :], b["half_y"], by_y),
        )

    def near_out(b):
        return copy(b, 6, b["to_y"], b["got_y"], by_y), copy(b, 7, b["to_x"], b["got_x"], by_x)

    def go_in(b):
        return copy(b, 8, b["own"], b["end"], (inward, f))

    def go_mid(b):
        return copy(b, 9, b["pair"], b["mid"], (3 - z, f))

    def go_out(b):
        return copy(b, 10, b["whole"], b["last"], (outward, f))

    def store(b):
        return pltpu.make_async_copy(b["out"], b["target"].at[rows_of(b), :], b["stored"].at[0])

    def begin(b):
        if b["full"]:
            for s in range(4):
                across_cores(b, s).start()
                load(b, s).start()
        else:
            load(b, 0).start()

    def arrived(b, s):
        across_cores(b, s).wait_recv()
        load(b, s).wait()

    def far_phase(b):
        arrived(b, 0)
        add_rows(b["far"], [b["mine"].at[0], b["theirs"].at[0]])
        for c in halves_out(b):
            c.start()

    def near_phase(b):
        half = b["rows"] // 2
        low, high = pl.ds(0, half), pl.ds(half, half)
        arrived(b, 1)
        arrived(b, 2)
        x_half, y_half = halves_out(b)
        x_half.wait_recv()
        y_half.wait_recv()
        mine, theirs = b["mine"], b["theirs"]
        add_rows(b["to_y"].at[low, :], [mine.at[1, low, :], theirs.at[1, low, :], b["half_x"]])
        add_rows(b["to_y"].at[high, :], [mine.at[1, high, :], theirs.at[1, high, :]])
        add_rows(b["to_x"].at[low, :], [mine.at[2, low, :], theirs.at[2, low, :]])
        add_rows(b["to_x"].at[high, :], [mine.at[2, high, :], theirs.at[2, high, :], b["half_y"]])
        for c in near_out(b):
            c.start()

    def own_phase(b):
        arrived(b, 3)
        for c in near_out(b):
            c.wait_recv()
        add_rows(b["own"], [b["mine"].at[3], b["theirs"].at[3], b["got_x"], b["got_y"]])

    def line_in(b):
        if not b["full"]:
            load(b, 0).wait()

        @pl.when(edge)
        def _():
            go_in(b).start()

    def line_mid(b):
        @pl.when(middle)
        def _():
            go_in(b).wait_recv()
            add_rows(b["pair"], [b["own"], b["end"]])
            go_mid(b).start()

    def line_out(b):
        @pl.when(middle)
        def _():
            go_mid(b).wait_recv()
            add_rows(b["whole"], [b["pair"], b["mid"]])
            go_out(b).start()
            add_rows(b["out"], [b["whole"]], share)
            store(b).start()

    def line_last(b):
        @pl.when(edge)
        def _():
            go_out(b).wait_recv()
            add_rows(b["out"], [b["last"]], share)
            store(b).start()

    barrier = pltpu.get_barrier_semaphore()
    for device in (sibling, by_x, by_y):
        pl.semaphore_signal(barrier, inc=1, device_id=device, device_id_type=mesh)

    @pl.when(middle)
    def _():
        pl.semaphore_signal(barrier, inc=1, device_id=(outward, f), device_id_type=mesh)
        pl.semaphore_signal(barrier, inc=1, device_id=(3 - z, f), device_id_type=mesh)
        pl.semaphore_wait(barrier, 5)

    @pl.when(edge)
    def _():
        pl.semaphore_signal(barrier, inc=1, device_id=(inward, f), device_id_type=mesh)
        pl.semaphore_wait(barrier, 4)

    wide = [b for b in items if b["full"]]
    queue = [b for b in items if not b["full"]]
    for b in queue:
        begin(b)
    ready = 2
    line = []
    slot = 0
    while sum(b is not None for b in line) < len(items):
        due = [b for n, b in enumerate(wide) if n + ready <= slot and not any(b is q for q in line)]
        left = [b for b in queue if not any(b is q for q in line)]
        if left and (not due or slot % 2 == 0):
            line.append(left[0])
        elif due:
            line.append(due[0])
        else:
            line.append(None)
        slot += 1
    for b in wide[:2]:
        begin(b)
    for t in range(len(line) + 3):
        if t + 2 < len(wide):
            begin(wide[t + 2])
        if t < len(wide):
            far_phase(wide[t])
        if 0 <= t - 1 < len(wide):
            near_phase(wide[t - 1])
        if 0 <= t - 2 < len(wide):
            own_phase(wide[t - 2])
        for phase, back in ((line_in, 0), (line_mid, 1), (line_out, 2), (line_last, 3)):
            if 0 <= t - back < len(line) and line[t - back] is not None:
                phase(line[t - back])
    for b in items:
        if b["full"]:
            for s in range(4):
                across_cores(b, s).wait_send()
            for c in halves_out(b) + near_out(b):
                c.wait_send()
        store(b).wait()

    @pl.when(edge)
    def _():
        for b in items:
            go_in(b).wait_send()

    @pl.when(middle)
    def _():
        for b in items:
            go_mid(b).wait_send()
            go_out(b).wait_send()


def reduce_tail(fulls, shards, share, number):
    plan, sources, arrays, shapes = [], [], [], []
    for full, group in ((True, fulls), (False, shards)):
        for g, pieces in group:
            rows, cols = g.shape[0] // (8 if full else 1), g.shape[1]
            for p in range(pieces):
                plan.append((full, rows // pieces, cols))
                sources.append((len(arrays), p * (rows // pieces)))
            arrays.append(g.reshape(8, rows, cols) if full else g)
            shapes.append(jax.ShapeDtypeStruct((rows, cols), f32))
    return pl.pallas_call(
        functools.partial(tail_kernel, tuple(plan), tuple(sources), share, len(arrays)),
        in_specs=[pl.BlockSpec(memory_space=pl.ANY)] * len(arrays),
        out_specs=[pl.BlockSpec(memory_space=pl.ANY)] * len(arrays),
        out_shape=shapes,
        scratch_shapes=tail_scratch(plan),
        compiler_params=pltpu.CompilerParams(
            collective_id=number, has_side_effects=True, vmem_limit_bytes=56 << 20
        ),
        name="reduce_tail",
    )(*arrays)


def pack_vectors(vectors, parts):
    flat = jnp.concatenate([v.reshape(parts, -1) for v in vectors], axis=1)
    width = 1024
    lines = 32 * (-(-flat.shape[1] // (32 * width)))
    flat = jnp.pad(flat, ((0, 0), (0, lines * width - flat.shape[1])))
    return flat.reshape(parts * lines, width)


def unpack_vectors(table, parts, sizes):
    flat = table.reshape(parts, -1)
    result, start = [], 0
    for size in sizes:
        result.append(flat[:, start : start + size].reshape(parts * size))
        start += size
    return result


def per_device_plain(
    tokens,
    memory,
    compressed,
    mem_fill,
    cmem_fill,
    pad_mask,
    first_gain,
    first_shift,
    query_weight,
    key_weight,
    value_weight,
    position_weight,
    content_bias,
    position_bias,
    output_weight,
    second_gain,
    second_shift,
    inner_weight,
    inner_bias,
    outer_weight,
    outer_bias,
    conv_weight,
    conv_bias,
    out_grad,
    comp_grad,
):
    streams, seg_rows, width = tokens.shape
    mem_rows = memory.shape[1]
    cmem_rows = compressed.shape[1]
    total = cmem_rows + mem_rows + seg_rows
    shards = lax.axis_size("fsdp")
    share = 1.0 / (streams * lax.axis_size("dp") * shards)
    vectors = (
        first_gain,
        first_shift,
        content_bias,
        position_bias,
        second_gain,
        second_shift,
        inner_bias,
        outer_bias,
        conv_bias,
    )
    sizes = [v.shape[0] for v in vectors]

    groups = mem_rows // RATE
    start = mem_rows - RATE * groups
    mem_valid = (
        jnp.arange(mem_rows, dtype=jnp.int32)[None, :] >= (mem_rows - mem_fill)[:, None]
    ).astype(bf16)
    taps = (memory * mem_valid[..., None])[:, start:, :].reshape(streams * groups, RATE * width)
    group_valid = (
        (start + RATE * jnp.arange(groups, dtype=jnp.int32) + RATE - 1)[None, :]
        >= (mem_rows - mem_fill)[:, None]
    ).reshape(streams * groups, 1)
    made_grad = comp_grad.reshape(streams * groups, width) * group_valid.astype(bf16)
    conv_grad = jnp.einsum("nk,nd->kd", taps, made_grad, preferred_element_type=f32).astype(bf16)
    conv_bias_grad = jnp.sum(made_grad.astype(f32), axis=0)

    query_w, key_w, value_w, table = gather(
        [query_weight, key_weight, value_weight, pack_vectors(vectors, 1)]
    )
    (gain_one, shift_one, content_b, position_b, gain_two, shift_two, inner_b, outer_b, conv_b) = (
        unpack_vectors(table, shards, sizes)
    )
    position_w, output_w = gather([position_weight, output_weight])
    (inner_w,) = gather([inner_weight])
    (outer_w,) = gather([outer_weight])
    (conv_w,) = gather([conv_weight])

    whole = jnp.concatenate([compressed[0], memory[0], tokens[0]], axis=0).astype(f32)
    normed, scaled_one, spread_one = norm_parts(whole, gain_one, shift_one)
    normed_low = normed.astype(bf16)
    own_rows = normed_low[total - seg_rows :]
    query = jnp.dot(own_rows, query_w, preferred_element_type=f32)
    query_u = (query + content_b.astype(f32)).astype(bf16)
    query_v = (query + position_b.astype(f32)).astype(bf16)
    keys = jnp.dot(normed_low, key_w, preferred_element_type=f32).astype(bf16)
    values = jnp.dot(normed_low, value_w, preferred_element_type=f32).astype(bf16)
    pos_low = positions(total, width).astype(bf16)
    relative = jnp.dot(pos_low, position_w, preferred_element_type=f32).astype(bf16)
    valid = jnp.concatenate(
        [
            jnp.arange(cmem_rows, dtype=jnp.int32) >= cmem_rows - cmem_fill[0],
            jnp.arange(mem_rows, dtype=jnp.int32) >= mem_rows - mem_fill[0],
            pad_mask[0] == 1,
        ]
    )
    bias = jnp.where(valid, 0.0, NEG).astype(f32)[None]
    mixed, prob_low = attn_fwd(query_u, query_v, keys, values, relative, bias, 0, HEADS)
    hidden = tokens[0].astype(f32) + jnp.dot(mixed, output_w, preferred_element_type=f32)
    inner_norm, scaled_two, spread_two = norm_parts(hidden, gain_two, shift_two)
    inner_low = inner_norm.astype(bf16)
    preact = jnp.dot(inner_low, inner_w, preferred_element_type=f32) + inner_b.astype(f32)
    active = smooth_gate(preact).astype(bf16)
    result = (
        hidden
        + jnp.dot(active, outer_w, preferred_element_type=f32)
        + outer_b.astype(f32)
    )
    made = (
        jnp.dot(taps, conv_w, preferred_element_type=f32) + conv_b.astype(f32)
    ) * group_valid.astype(f32)

    grad = out_grad[0]
    grad_wide = grad.astype(f32)
    outer_grad = jnp.einsum("sf,sd->fd", active, grad, preferred_element_type=f32).astype(bf16)
    (outer_mean,) = reduce([outer_grad], share)
    outer_bias_grad = jnp.sum(grad_wide, axis=0)
    active_grad = jnp.einsum("sd,fd->sf", grad, outer_w, preferred_element_type=f32)
    gate_pull = jax.vjp(smooth_gate, preact)[1]
    preact_grad = gate_pull(active_grad)[0].astype(bf16)
    inner_grad = jnp.einsum("sd,sf->df", inner_low, preact_grad, preferred_element_type=f32).astype(
        bf16
    )
    (inner_mean,) = reduce([inner_grad], share)
    (conv_mean,) = reduce([conv_grad], share)
    inner_bias_grad = jnp.sum(preact_grad.astype(f32), axis=0)
    inner_norm_grad = jnp.einsum("sf,df->sd", preact_grad, inner_w, preferred_element_type=f32)
    second_gain_grad = jnp.sum(inner_norm_grad * scaled_two, axis=0)
    second_shift_grad = jnp.sum(inner_norm_grad, axis=0)
    hidden_grad = grad_wide + norm_back(inner_norm_grad, scaled_two, spread_two, gain_two)

    hidden_low = hidden_grad.astype(bf16)
    output_grad = jnp.einsum("sd,se->de", mixed, hidden_low, preferred_element_type=f32).astype(bf16)
    mixed_grad = jnp.einsum("se,de->sd", hidden_low, output_w, preferred_element_type=f32).astype(
        bf16
    )
    query_low, keys_t, values_t, relative_t, sums = attn_bwd(
        query_u,
        query_v,
        query_u.T,
        query_v.T,
        keys,
        values,
        relative,
        prob_low,
        mixed_grad,
        mixed_grad.T,
        0,
        HEADS,
    )
    position_grad = jnp.einsum("ld,el->de", pos_low, relative_t, preferred_element_type=f32).astype(
        bf16
    )
    query_grad = jnp.einsum("sd,se->de", own_rows, query_low, preferred_element_type=f32).astype(
        bf16
    )
    key_grad = jnp.einsum("sd,es->de", normed_low, keys_t, preferred_element_type=f32).astype(bf16)
    value_grad = jnp.einsum("sd,es->de", normed_low, values_t, preferred_element_type=f32).astype(
        bf16
    )
    normed_grad = jnp.einsum("es,de->sd", keys_t, key_w, preferred_element_type=f32)
    normed_grad = normed_grad + jnp.einsum(
        "es,de->sd", values_t, value_w, preferred_element_type=f32
    )
    own_grad = jnp.einsum("se,de->sd", query_low, query_w, preferred_element_type=f32)
    normed_grad = normed_grad + jnp.pad(own_grad, ((total - seg_rows, 0), (0, 0)))
    first_gain_grad = jnp.sum(normed_grad * scaled_one, axis=0)
    first_shift_grad = jnp.sum(normed_grad, axis=0)
    own = slice(total - seg_rows, None)
    token_gradient = hidden_grad + norm_back(
        normed_grad[own], scaled_one[own], spread_one[own], gain_one
    )
    vector_grads = (
        first_gain_grad,
        first_shift_grad,
        sums[0],
        sums[1],
        second_gain_grad,
        second_shift_grad,
        inner_bias_grad,
        outer_bias_grad,
        conv_bias_grad,
    )
    packed = pack_vectors([v.astype(bf16) for v in vector_grads], shards)
    (output_mean,) = reduce([output_grad], share)
    query_mean, key_mean, value_mean, position_mean, table_mean = reduce(
        [query_grad, key_grad, value_grad, position_grad, packed], share
    )
    (
        first_gain_mean,
        first_shift_mean,
        content_mean,
        posbias_mean,
        second_gain_mean,
        second_shift_mean,
        inner_bias_mean,
        outer_bias_mean,
        conv_bias_mean,
    ) = unpack_vectors(table_mean, 1, sizes)
    return (
        result.astype(bf16)[None],
        token_gradient[None],
        made.astype(bf16)[None],
        first_gain_mean,
        first_shift_mean,
        query_mean,
        key_mean,
        value_mean,
        position_mean,
        content_mean,
        posbias_mean,
        output_mean,
        second_gain_mean,
        second_shift_mean,
        inner_mean,
        inner_bias_mean,
        outer_mean,
        outer_bias_mean,
        conv_mean,
        conv_bias_mean,
    )


def per_device_direct(
    tokens,
    memory,
    compressed,
    mem_fill,
    cmem_fill,
    pad_mask,
    first_gain,
    first_shift,
    query_weight,
    key_weight,
    value_weight,
    position_weight,
    content_bias,
    position_bias,
    output_weight,
    second_gain,
    second_shift,
    inner_weight,
    inner_bias,
    outer_weight,
    outer_bias,
    conv_weight,
    conv_bias,
    out_grad,
    comp_grad,
):
    streams, seg_rows, width = tokens.shape
    mem_rows = memory.shape[1]
    cmem_rows = compressed.shape[1]
    total = cmem_rows + mem_rows + seg_rows
    old = total - seg_rows
    shards = lax.axis_size("fsdp")
    share = 1.0 / (streams * lax.axis_size("dp") * shards)
    lower = HEADS // 2
    edge = lower * DH
    index = slot_index()
    vectors = (
        first_gain,
        first_shift,
        content_bias,
        position_bias,
        second_gain,
        second_shift,
        inner_bias,
        outer_bias,
        conv_bias,
    )
    sizes = [v.shape[0] for v in vectors]
    rows = query_weight.shape[0]
    pack_1 = jnp.concatenate([query_weight, key_weight, value_weight, pack_vectors(vectors, 1)], axis=0)
    pack_2 = jnp.concatenate([position_weight, output_weight], axis=0)

    first_1 = first_hop(pack_1)
    whole = jnp.concatenate([compressed[0], memory[0], tokens[0]], axis=0).astype(f32)
    center = jnp.mean(whole, axis=-1, keepdims=True)
    spread_one = lax.rsqrt(jnp.mean((whole - center) ** 2, axis=-1, keepdims=True) + EPSILON)
    scaled_one = (whole - center) * spread_one
    groups = mem_rows // RATE
    start = mem_rows - RATE * groups
    mem_valid = (jnp.arange(mem_rows, dtype=jnp.int32) >= mem_rows - mem_fill[0]).astype(bf16)
    taps = (memory[0] * mem_valid[:, None])[start:, :].reshape(groups, RATE * width)
    group_valid = (
        start + RATE * jnp.arange(groups, dtype=jnp.int32) + RATE - 1 >= mem_rows - mem_fill[0]
    )[:, None]
    made_grad = comp_grad[0] * group_valid.astype(bf16)
    conv_grad = jnp.einsum("nk,nd->kd", taps, made_grad, preferred_element_type=f32).astype(bf16)
    conv_bias_grad = jnp.sum(made_grad.astype(f32), axis=0)
    first_1, scaled_one, conv_grad, taps, pack_2, pack_1 = cut(
        first_1, scaled_one, conv_grad, taps, pack_2, pack_1
    )

    second_1, across_1 = second_hop(first_1), plane_hop(first_1)
    first_2 = first_hop(pack_2)
    core_1a, core_1b = core_hop(pack_1), core_hop(first_1)
    pos_low = positions(total, width).astype(bf16)
    second_1, across_1, first_2, core_1a, core_1b, pos_low, inner_weight = cut(
        second_1, across_1, first_2, core_1a, core_1b, pos_low, inner_weight
    )

    core_1c, core_1d = core_hop(across_1), core_hop(second_1)
    second_2, across_2 = second_hop(first_2), plane_hop(first_2)
    core_2a, core_2b = core_hop(pack_2), core_hop(first_2)
    first_3 = first_hop(inner_weight)
    query_w, key_w, value_w, table = assemble(
        [pack_1, first_1, across_1, second_1, core_1a, core_1b, core_1c, core_1d],
        index,
        [rows, rows, rows, pack_1.shape[0] - 3 * rows],
    )
    (gain_one, shift_one, content_b, position_b, gain_two, shift_two, inner_b, outer_b, conv_b) = (
        unpack_vectors(table, shards, sizes)
    )
    normed_low = (scaled_one * gain_one.astype(f32) + shift_one.astype(f32)).astype(bf16)
    own_rows = normed_low[old:]
    query = jnp.dot(own_rows, query_w, preferred_element_type=f32)
    query_u = (query + content_b.astype(f32)).astype(bf16)
    query_v = (query + position_b.astype(f32)).astype(bf16)
    keys = jnp.dot(normed_low, key_w, preferred_element_type=f32).astype(bf16)
    values = jnp.dot(normed_low, value_w, preferred_element_type=f32).astype(bf16)
    (second_2, across_2, core_2a, core_2b, first_3, query_u, query_v, keys, values, outer_weight) = cut(
        second_2, across_2, core_2a, core_2b, first_3, query_u, query_v, keys, values, outer_weight
    )

    core_2c, core_2d = core_hop(across_2), core_hop(second_2)
    second_3, across_3 = second_hop(first_3), plane_hop(first_3)
    core_3a, core_3b = core_hop(inner_weight), core_hop(first_3)
    first_4 = first_hop(outer_weight)
    position_w, output_w = assemble(
        [pack_2, first_2, across_2, second_2, core_2a, core_2b, core_2c, core_2d], index, [rows, rows]
    )
    relative = jnp.dot(pos_low, position_w, preferred_element_type=f32).astype(bf16)
    valid = jnp.concatenate(
        [
            jnp.arange(cmem_rows, dtype=jnp.int32) >= cmem_rows - cmem_fill[0],
            jnp.arange(mem_rows, dtype=jnp.int32) >= mem_rows - mem_fill[0],
            pad_mask[0] == 1,
        ]
    )
    bias = jnp.where(valid, 0.0, NEG).astype(f32)[None]
    mixed_a, prob_a = attn_fwd(query_u, query_v, keys, values, relative, bias, 0, lower)
    second_3, across_3, core_3a, core_3b, first_4, mixed_a, prob_a, conv_weight = cut(
        second_3, across_3, core_3a, core_3b, first_4, mixed_a, prob_a, conv_weight
    )

    core_3c, core_3d = core_hop(across_3), core_hop(second_3)
    second_4, across_4 = second_hop(first_4), plane_hop(first_4)
    core_4a, core_4b = core_hop(outer_weight), core_hop(first_4)
    first_5 = first_hop(conv_weight)
    mixed_b, prob_b = attn_fwd(
        query_u, query_v, keys, values, relative, bias, lower, HEADS - lower
    )
    mixed = jnp.concatenate([mixed_a, mixed_b], axis=1)
    hidden = tokens[0].astype(f32) + jnp.dot(mixed, output_w, preferred_element_type=f32)
    inner_norm, scaled_two, spread_two = norm_parts(hidden, gain_two, shift_two)
    inner_low = inner_norm.astype(bf16)
    (second_4, across_4, core_4a, core_4b, first_5, core_3c, core_3d, inner_low, hidden, prob_b) = cut(
        second_4, across_4, core_4a, core_4b, first_5, core_3c, core_3d, inner_low, hidden, prob_b
    )

    core_4c, core_4d = core_hop(across_4), core_hop(second_4)
    second_5, across_5 = second_hop(first_5), plane_hop(first_5)
    core_5a, core_5b = core_hop(conv_weight), core_hop(first_5)
    (inner_w,) = assemble(
        [inner_weight, first_3, across_3, second_3, core_3a, core_3b, core_3c, core_3d], index, [rows]
    )
    preact = jnp.dot(inner_low, inner_w, preferred_element_type=f32) + inner_b.astype(f32)
    active = smooth_gate(preact).astype(bf16)
    (second_5, across_5, core_5a, core_5b, core_4c, core_4d, preact, active, conv_grad) = cut(
        second_5, across_5, core_5a, core_5b, core_4c, core_4d, preact, active, conv_grad
    )

    grad = out_grad[0]
    grad_wide = grad.astype(f32)
    core_5c, core_5d = core_hop(across_5), core_hop(second_5)
    conv_part = lax.psum_scatter(conv_grad, "fsdp", scatter_dimension=0, tiled=True)
    outer_grad = jnp.einsum("sf,sd->fd", active, grad, preferred_element_type=f32).astype(bf16)
    outer_bias_grad = jnp.sum(grad_wide, axis=0)
    core_5c, core_5d, outer_grad = cut(core_5c, core_5d, outer_grad)

    outer_part = lax.psum_scatter(outer_grad, "fsdp", scatter_dimension=0, tiled=True)
    (outer_w,) = assemble(
        [outer_weight, first_4, across_4, second_4, core_4a, core_4b, core_4c, core_4d],
        index,
        [outer_weight.shape[0]],
    )
    active_grad = jnp.einsum("sd,fd->sf", grad, outer_w, preferred_element_type=f32)
    gate_pull = jax.vjp(smooth_gate, preact)[1]
    preact_grad = gate_pull(active_grad)[0].astype(bf16)
    inner_bias_grad = jnp.sum(preact_grad.astype(f32), axis=0)
    inner_grad = jnp.einsum("sd,sf->df", inner_low, preact_grad, preferred_element_type=f32).astype(
        bf16
    )
    inner_grad, preact_grad = cut(inner_grad, preact_grad)

    inner_part = lax.psum_scatter(inner_grad, "fsdp", scatter_dimension=0, tiled=True)
    inner_norm_grad = jnp.einsum("sf,df->sd", preact_grad, inner_w, preferred_element_type=f32)
    second_gain_grad = jnp.sum(inner_norm_grad * scaled_two, axis=0)
    second_shift_grad = jnp.sum(inner_norm_grad, axis=0)
    hidden_grad = grad_wide + norm_back(inner_norm_grad, scaled_two, spread_two, gain_two)
    hidden_low = hidden_grad.astype(bf16)
    output_grad = jnp.einsum("sd,se->de", mixed, hidden_low, preferred_element_type=f32).astype(bf16)
    mixed_grad = jnp.einsum("se,de->sd", hidden_low, output_w, preferred_element_type=f32).astype(
        bf16
    )
    bwd = (query_u, query_v, query_u.T, query_v.T, keys, values, relative)
    query_a, keys_a, values_a, relative_a, sums_a = attn_bwd(
        *bwd, prob_a, mixed_grad, mixed_grad.T, 0, lower
    )
    query_b, keys_b, values_b, relative_b, sums_b = attn_bwd(
        *bwd, prob_b, mixed_grad, mixed_grad.T, lower, HEADS - lower
    )
    query_g = jnp.concatenate([query_a, query_b], axis=1)
    keys_g = jnp.concatenate([keys_a, keys_b], axis=0)
    values_g = jnp.concatenate([values_a, values_b], axis=0)
    relative_g = jnp.concatenate([relative_a, relative_b], axis=0)
    query_grad = jnp.einsum("sd,se->de", own_rows, query_g, preferred_element_type=f32).astype(bf16)
    key_grad = jnp.einsum("sd,es->de", normed_low, keys_g, preferred_element_type=f32).astype(bf16)
    value_grad = jnp.einsum("sd,es->de", normed_low, values_g, preferred_element_type=f32).astype(bf16)
    position_grad = jnp.einsum("ld,el->de", pos_low, relative_g, preferred_element_type=f32).astype(
        bf16
    )
    normed_grad = jnp.einsum("es,de->sd", keys_g, key_w, preferred_element_type=f32)
    normed_grad = normed_grad + jnp.einsum("es,de->sd", values_g, value_w, preferred_element_type=f32)
    own_grad = jnp.einsum("se,de->sd", query_g, query_w, preferred_element_type=f32)
    normed_grad = normed_grad + jnp.pad(own_grad, ((old, 0), (0, 0)))
    first_gain_grad = jnp.sum(normed_grad * scaled_one, axis=0)
    first_shift_grad = jnp.sum(normed_grad, axis=0)
    token_gradient = hidden_grad + norm_back(
        normed_grad[old:], scaled_one[old:], spread_one[old:], gain_one
    )
    vector_grads = (
        first_gain_grad,
        first_shift_grad,
        jnp.concatenate([sums_a[0], sums_b[0]]),
        jnp.concatenate([sums_a[1], sums_b[1]]),
        second_gain_grad,
        second_shift_grad,
        inner_bias_grad,
        outer_bias_grad,
        conv_bias_grad,
    )
    packed = pack_vectors([v.astype(bf16) for v in vector_grads], shards)
    result = (
        hidden + jnp.dot(active, outer_w, preferred_element_type=f32) + outer_b.astype(f32)
    ).astype(bf16)
    (conv_w,) = assemble(
        [conv_weight, first_5, across_5, second_5, core_5a, core_5b, core_5c, core_5d],
        index,
        [conv_weight.shape[0]],
    )
    made = (
        (jnp.dot(taps, conv_w, preferred_element_type=f32) + conv_b.astype(f32))
        * group_valid.astype(f32)
    ).astype(bf16)
    (
        query_mean,
        key_mean,
        value_mean,
        position_mean,
        output_mean,
        table_mean,
        conv_mean,
        outer_mean,
        inner_mean,
    ) = reduce_tail(
        [(g, 2) for g in (query_grad, key_grad, value_grad, position_grad, output_grad)]
        + [(packed, 1)],
        [(conv_part, 3), (outer_part, 4), (inner_part, 4)],
        share,
        1,
    )
    (
        first_gain_mean,
        first_shift_mean,
        content_mean,
        posbias_mean,
        second_gain_mean,
        second_shift_mean,
        inner_bias_mean,
        outer_bias_mean,
        conv_bias_mean,
    ) = unpack_vectors(table_mean, 1, sizes)
    return (
        result[None],
        token_gradient[None],
        made[None],
        first_gain_mean,
        first_shift_mean,
        query_mean,
        key_mean,
        value_mean,
        position_mean,
        content_mean,
        posbias_mean,
        output_mean,
        second_gain_mean,
        second_shift_mean,
        inner_mean,
        inner_bias_mean,
        outer_mean,
        outer_bias_mean,
        conv_mean,
        conv_bias_mean,
    )


def per_device(*arguments):
    if lax.axis_size("dp") == 4 and lax.axis_size("fsdp") == 8:
        return per_device_direct(*arguments)
    return per_device_plain(*arguments)


def solution(mesh):
    in_specs = (
        P(("dp", "fsdp"), None, None),
        P(("dp", "fsdp"), None, None),
        P(("dp", "fsdp"), None, None),
        P(("dp", "fsdp")),
        P(("dp", "fsdp")),
        P(("dp", "fsdp"), None),
        P("fsdp"),
        P("fsdp"),
        P("fsdp", None),
        P("fsdp", None),
        P("fsdp", None),
        P("fsdp", None),
        P("fsdp"),
        P("fsdp"),
        P("fsdp", None),
        P("fsdp"),
        P("fsdp"),
        P("fsdp", None),
        P("fsdp"),
        P("fsdp", None),
        P("fsdp"),
        P("fsdp", None),
        P("fsdp"),
        P(("dp", "fsdp"), None, None),
        P(("dp", "fsdp"), None, None),
    )
    out_specs = (
        P(("dp", "fsdp"), None, None),
        P(("dp", "fsdp"), None, None),
        P(("dp", "fsdp"), None, None),
        P("fsdp"),
        P("fsdp"),
        P("fsdp", None),
        P("fsdp", None),
        P("fsdp", None),
        P("fsdp", None),
        P("fsdp"),
        P("fsdp"),
        P("fsdp", None),
        P("fsdp"),
        P("fsdp"),
        P("fsdp", None),
        P("fsdp"),
        P("fsdp", None),
        P("fsdp"),
        P("fsdp", None),
        P("fsdp"),
    )
    return jax.shard_map(
        per_device, mesh=mesh, in_specs=in_specs, out_specs=out_specs, check_vma=False
    )
```

time: 945 us -> 563 us (0.60)
  waiting for transfers between devices: 496 us -> 53.7 us
  Pallas kernels: 71.1 us -> 210 us
  blocking collectives: 113 us -> 0 us
  local copies, waits for them, and re-layouts: 23.6 us -> 95.3 us
  matrix products: 161 us -> 107 us
  starting transfers between devices: 1.14 us -> 21.9 us
    reduce_scatter x8 -> x3, waiting for transfers between devices: 264 us -> 21.7 us  [the longest x1 21.7 us: per_device_direct(): lax.psum_scatter(outer_grad, 'fsdp', scatter_dimension=0, tiled=True)]
    psum x1 -> x0, waiting for transfers between devices: 139 us -> none  [per_device(): lax.psum(attn_parts[2].astype(jnp.bfloat16), 'dp').astype(jnp.float32)]
    pallas_call x0 -> x6, Pallas kernels: none -> 137 us  [the longest x1 121 us: reduce_tail(): pl.pallas_call(functools.partial(tail_kernel, tuple(plan), tuple(sources)...]
    all_gather x8 -> x0, waiting for transfers between devices: 87 us -> none  [the longest x1 44.2 us: per_device(): lax.all_gather(outer_weight, 'fsdp', axis=0, tiled=True)]
    all_gather x9 -> x0, blocking collectives: 77.3 us -> none  [the longest x1 10.3 us: per_device(): lax.all_gather(position_bias, 'fsdp', axis=0, tiled=True)]
    unnamed x149 -> x250, local copies, waits for them, and re-layouts: 18.8 us -> 81.1 us
    dot_general x22, matrix products: 161 us -> 107 us  [the longest x1 9.31 us: per_device_direct(): jnp.dot(inner_low, inner_w, preferred_element_type=f32)]
    ppermute x0 -> x35, waiting for transfers between devices: none -> 31.9 us  [hop(): return lax.ppermute(value, ('dp', 'fsdp'), pairs)]
  transfers between devices with their start and end apart: 17 -> 38, of which waited for: 9 -> 9; matrix products, arithmetic and copies ran while one was open for 22% -> 31% of each run, Pallas kernels for 8% -> 16%
where the time goes in v2:
time: 563 us; the launch traced here: 553 us
  Pallas kernels  210 us (37%)
  matrix products  107 us (19%)
  local copies, waits for them, and re-layouts  95.3 us (17%)
  waiting for transfers between devices  53.7 us (10%)
  other arithmetic  48.8 us (9%)
  starting transfers between devices  21.9 us (4%)
  between operations  16.7 us (3%)
    pallas_call x1, Pallas kernels, reduce_tail(): pl.pallas_call(functools.partial(tail_kernel, tuple(plan), tuple(sources)...  121 us
    unnamed x250, local copies, waits for them, and re-layouts  81.1 us
    pallas_call x2, Pallas kernels, attn_bwd(): pl.pallas_call(attn_bwd_kernel, grid=(heads,), in_specs=[col(seg), col(se...  43.4 us
    ppermute x35, waiting for transfers between devices, hop(): return lax.ppermute(value, ('dp', 'fsdp'), pairs)  31.9 us
    pallas_call x2, Pallas kernels, attn_fwd(): pl.pallas_call(attn_fwd_kernel, grid=(heads,), in_specs=[col(seg), col(se...  29.5 us
    ppermute x35, starting transfers between devices, hop(): return lax.ppermute(value, ('dp', 'fsdp'), pairs)  21.7 us
    reduce_scatter x1, waiting for transfers between devices, per_device_direct(): lax.psum_scatter(outer_grad, 'fsdp', scatter_dimension=0, tiled=True)  21.7 us
    pallas_call x5, Pallas kernels, assemble(): pl.pallas_call(functools.partial(assemble_kernel, count, tuple(places)),...  16.3 us
  transfers between devices with their start and end apart: 38, of which 9 were waited for; matrix products, arithmetic and copies ran while one was open for 31% of the time, Pallas kernels for 16%

profile of v2, /device:TPU:0, one launch (start us, length us, event | category | flops | bytes accessed | tf_op | source)
XLA Modules:
  0.0 553.5 jit_solution(12704921651206635845)
XLA Ops:
  16.6 3.0 collective-permute-start
  20.4 2.1 convert_reduce_fusion
  22.5 3.0 fusion.20
  26.8 2.4 reshape.367
  31.0 5.7 %convolution_convert_fusion.2 = bf16[3072,1024]{1,0:T(8,128)(2,1)} fusion(bf16[170,3072]{1,0:T(8,128)(2,1)} %reshape.367, bf16[1,170,1024]{2,1,0:T(8,128)(2,1)S(1)} %copy-done.84, bf16[170]{0:T(256)(128)(2,1)S(1)} %fusion.56), kind=kOutput, calls=%fused_computation.34 | convolution fusion | flops 1072867328 | bytes 7684436 | tf_op jit(solution)/shard_map/nk,nd->kd/dot_general | solution.py:822
  36.7 5.1 fusion.18
  45.5 11.9 %fusion.21 = (bf16[1536,512]{1,0:T(8,128)(2,1)S(1)}, bf16[1536,512]{1,0:T(8,128)(2,1)S(1)}) fusion(f32[512]{0:T(512)S(1)} %multiply_exponential_fusion, f32[1536]{0:T(1024)S(1)} %subtract_convert_fusion), kind=kLoop, calls=%fused_computation.40 | loop fusion | flops 2359296 | bytes 3153920 | tf_op jit(solution)/shard_map/convert.24
  60.4 2.8 collective-permute-done.2.refs_2_
  71.4 3.5 assemble.5
  81.6 3.9 add_convert_fusion
  85.6 4.1 convolution_convert_fusion.4.v_ref
  89.7 4.8 convolution_convert_fusion.5.k_ref
  94.6 2.7 add_convert_fusion.3
  103.3 2.3 copy.47.qu_ref
  105.5 2.3 copy.48.qv_ref
  110.9 2.9 assemble.6
  114.0 3.6 convolution_convert_fusion.3.r_ref
  117.6 14.7 %attn_fwd.2 = (bf16[512,512]{1,0:T(8,128)(2,1)S(1)}, bf16[4,512,1536]{2,1,0:T(8,128)(2,1)}) custom-call(bf16[512,1024]{1,0:T(8,128)(2,1)S(1)} %copy-done.3, bf16[512,1024]{1,0:T(8,128)(2,1)S(1)} %copy-done.5, bf16[1536,1024]{1,0:T(8,128)(2,1)S(1)} %copy-done.1, bf16[1536,1024]{1,0:T(8,128)(2,1)S(1)} %convolution_convert_fusion.4.v_ref, ...), custom_call_target="tpu_custom_call" | custom-call | flops 2415919104 | bytes 12582912 | tf_op jit(solution)/shard_map/attn_fwd/pallas_call | solution.py:83
  134.8 14.8 %attn_fwd.3 = (bf16[512,512]{1,0:T(8,128)(2,1)S(1)}, bf16[4,512,1536]{2,1,0:T(8,128)(2,1)}) custom-call(bf16[512,1024]{1,0:T(8,128)(2,1)S(1)} %copy-done.3, bf16[512,1024]{1,0:T(8,128)(2,1)S(1)} %copy-done.5, bf16[1536,1024]{1,0:T(8,128)(2,1)S(1)} %copy-done.1, bf16[1536,1024]{1,0:T(8,128)(2,1)S(1)} %convolution_convert_fusion.4.v_ref, ...), custom_call_target="tpu_custom_call" | custom-call | flops 2415919104 | bytes 12582912 | tf_op jit(solution)/shard_map/attn_fwd/pallas_call | solution.py:83
  155.2 20.2 %collective-permute-done.21.refs_2_ = bf16[512,1024]{1,0:T(8,128)(2,1)S(1)} collective-permute-done((bf16[512,1024]{1,0:T(8,128)(2,1)}, bf16[512,1024]{1,0:T(8,128)(2,1)S(1)}, u32[]{:S(2)}, u32[]{:S(2)}) %collective-permute-start.21) | collective-permute-done | bytes 1048608 | tf_op jit(solution)/shard_map/ppermute | solution.py:149
  178.0 3.7 assemble.7
  182.3 9.3 %fusion.14 = (bf16[512,4096]{1,0:T(8,128)(2,1)}, f32[512,4096]{1,0:T(8,128)}) fusion(f32[4096]{0:T(1024)S(1)} %bitcast.216, bf16[512,1024]{1,0:T(8,128)(2,1)S(1)} %add_convert_fusion.2, bf16[1024,4096]{1,0:T(8,128)(2,1)S(1)} %assemble.7), kind=kOutput, calls=%fused_computation.17 | convolution fusion | flops 4315938816 | bytes 22036480 | tf_op jit(solution)/shard_map/dot_general | solution.py:901
  192.5 3.5 collective-permute-done.28.refs_2_
  204.1 3.5 assemble.8
  207.6 4.1 copy-done.7
  211.8 4.5 fusion.36
  216.4 6.0 %fusion.60 = (bf16[4096]{0:T(1024)(128)(2,1)S(1)}, bf16[512,4096]{1,0:T(8,128)(2,1)S(1)}) fusion(f32[512,4096]{1,0:T(8,128)S(1)} %bitcast.205, f32[4096,512]{0,1:T(8,128)S(1)} %fusion.36), kind=kLoop, calls=%fused_computation.172 | loop fusion | flops 44036096 | bytes 20979712 | tf_op jit(solution)/shard_map/reduce_sum | solution.py:924
  222.4 2.4 copy-done.73
  224.8 6.9 %convolution_convert_fusion.1 = bf16[1024,4096]{1,0:T(8,128)(2,1)} fusion(bf16[512,1024]{1,0:T(8,128)(2,1)S(1)} %copy-done.86, bf16[512,4096]{1,0:T(8,128)(2,1)S(1)} %get-tuple-element.156), kind=kOutput, calls=%fused_computation.26 | convolution fusion | flops 4299161600 | bytes 13631488 | tf_op jit(solution)/shard_map/sd,sf->df/dot_general | solution.py:925
  234.9 9.2 %multiply_reduce_fusion.1 = (bf16[1024]{0:T(1024)(128)(2,1)S(1)}, f32[512]{0:T(512)S(1)}, f32[512]{0:T(512)S(1)}, bf16[1024]{0:T(1024)(128)(2,1)S(1)}, f32[512,1024]{1,0:T(8,128)S(1)}) fusion(f32[512,1024]{1,0:T(8,128)S(1)} %copy-done.65, f32[512]{0:T(512)S(1)} %add_rsqrt_fusion.1, f32[512]{0:T(512)S(1)} %broadcast_multiply_fusion.5, ...), kind=kOutput, calls=%fused_computation.49 | convolution fusion | flops 4299682816 | bytes 16793600 | tf_op jit(solution)/shard_map/sf,df->sd/dot_general | solution.py:931
  244.1 2.1 multiply_add_fusion
  247.1 6.8 %convolution_convert_fusion = bf16[4096,1024]{1,0:T(8,128)(2,1)} fusion(bf16[512,4096]{1,0:T(8,128)(2,1)S(1)} %copy-done.101, bf16[1,512,1024]{2,1,0:T(8,128)(2,1)S(1)} %copy-done.75), kind=kOutput, calls=%fused_computation.25 | convolution fusion | flops 4299161600 | bytes 13631488 | tf_op jit(solution)/shard_map/sf,sd->fd/dot_general | solution.py:911
  253.8 4.8 convolution_convert_fusion.10
  258.6 2.3 copy.54.g_ref
  264.6 21.6 %attn_bwd.3 = (bf16[512,512]{1,0:T(8,128)(2,1)S(1)}, bf16[512,1536]{1,0:T(8,128)(2,1)S(1)}, bf16[512,1536]{1,0:T(8,128)(2,1)S(1)}, bf16[512,1536]{1,0:T(8,128)(2,1)S(1)}, f32[8,512]{1,0:T(8,128)S(1)}) custom-call(bf16[512,1024]{1,0:T(8,128)(2,1)S(1)} %copy-done.4, bf16[512,1024]{1,0:T(8,128)(2,1)S(1)} %copy-done.6, bf16[1024,512]{1,0:T(8,128)(2,1)S(1)} %bitcast.188, ...), custom_call_target="tpu_custom_call" | custom-call | flops 6442450944 | bytes 18350080 | tf_op jit(solution)/shard_map/attn_bwd/pallas_call | solution.py:132
  294.3 21.7 %attn_bwd.2 = (bf16[512,512]{1,0:T(8,128)(2,1)S(1)}, bf16[512,1536]{1,0:T(8,128)(2,1)S(1)}, bf16[512,1536]{1,0:T(8,128)(2,1)S(1)}, bf16[512,1536]{1,0:T(8,128)(2,1)S(1)}, f32[8,512]{1,0:T(8,128)S(1)}) custom-call(bf16[512,1024]{1,0:T(8,128)(2,1)S(1)} %copy-done.4, bf16[512,1024]{1,0:T(8,128)(2,1)S(1)} %copy-done.6, bf16[1024,512]{1,0:T(8,128)(2,1)S(1)} %bitcast.189, ...), custom_call_target="tpu_custom_call" | custom-call | flops 6442450944 | bytes 18350080 | tf_op jit(solution)/shard_map/attn_bwd/pallas_call | solution.py:132
  330.5 5.4 fusion.64
  335.9 9.2 %fusion.59 = (bf16[1024]{0:T(1024)(128)(2,1)S(1)}, bf16[1024]{0:T(1024)(128)(2,1)S(1)}, f32[1536,1024]{1,0:T(8,128)S(1)}) fusion(f32[1536,1024]{1,0:T(8,128)S(1)} %bitcast.193, f32[512,1024]{1,0:T(8,128)S(1)} %fusion.65, f32[1536,1024]{1,0:T(8,128)} %fusion.64, bf16[1024,1536]{1,0:T(8,128)(2,1)} %copy-done.89, bf16[1024,1024]{1,0:T(8,128)(2,1)S(1)} %copy-done.52), kind=kOutput, calls=%fused_computation.171 | convolution fusion | flops 3229087744 | bytes 26218496 | tf_op jit(solution)/shard_map/es,de->sd/dot_general | solution.py:957
  349.7 2.6 convolution_convert_fusion.9
  352.6 2.7 convolution_convert_fusion.6
  358.5 4.5 fusion.63
  364.6 4.0 add_bitcast_fusion
  369.2 5.8 %fusion.27 = bf16[1024,1024]{1,0:T(8,128)(2,1)} fusion(bf16[1536,1024]{1,0:T(8,128)(2,1)S(1)} %copy-done.77, bf16[512,1536]{1,0:T(8,128)(2,1)S(1)} %copy-done.61, bf16[512,1536]{1,0:T(8,128)(2,1)S(1)} %copy-done.63), kind=kOutput, calls=%fused_computation.65 | convolution fusion | flops 3228565504 | bytes 8388608 | tf_op jit(solution)/shard_map/ld,el->de/dot_general | solution.py:954
  375.0 4.7 convolution_convert_fusion.8
  379.7 5.1 convolution_convert_fusion.7
  384.8 2.8 assemble.9
  389.7 21.7 %reduce-scatter.6.cloned.1.call-done.refs_7_ = bf16[512,1024]{1,0:T(8,128)(2,1)} async-done(((bf16[4096,1024]{1,0:T(8,128)(2,1)}), bf16[512,1024]{1,0:T(8,128)(2,1)}) %reduce-scatter.6.cloned.1.call-update) | async-done | bytes 1048592 | tf_op jit(solution)/shard_map/reduce_scatter | solution.py:915
  411.4 120.9 %reduce_tail.1 = (f32[128,1024]{1,0:T(8,128)}, f32[128,1024]{1,0:T(8,128)}, f32[128,1024]{1,0:T(8,128)}, f32[128,1024]{1,0:T(8,128)}, f32[128,1024]{1,0:T(8,128)...) custom-call(bf16[8,128,1024]{2,1,0:T(8,128)(2,1)} %bitcast.207, ...), custom_call_target="tpu_custom_call" | custom-call | tf_op jit(solution)/shard_map/reduce_tail/pallas_call | solution.py:510
  (383 shorter events, 119.3 us)
Async XLA Ops:
  7.2 15.3 %copy-start.67 = (bf16[1,512,1024]{2,1,0:T(8,128)(2,1)S(1)}, bf16[1,512,1024]{2,1,0:T(8,128)(2,1)}, u32[]{:S(2)}) copy-start(bf16[1,512,1024]{2,1,0:T(8,128)(2,1)} %param.26) | copy-start | bytes 3145732
  7.2 382.4 %reduce-scatter.4.cloned.1.call-start = ((), (), s32[]{:S(2)}) async-start(), calls=%async_computation.3 | async-start | bytes 7077888 | tf_op jit(solution)/shard_map/reduce_scatter | solution.py:910
  16.6 25.2 %collective-permute-start = (bf16[416,1024]{1,0:T(8,128)(2,1)S(1)}, bf16[416,1024]{1,0:T(8,128)(2,1)S(1)}, u32[]{:S(2)}, u32[]{:S(2)}) collective-permute-start(bf16[416,1024]{1,0:T(8,128)(2,1)S(1)} %constant_dynamic-update-slice_fusion.9.refs_0_), channel_id=1, source_target_pairs={{0,2},{1,3},{2,0},{3,1},{4,6},{5,7},{6,4},{7,5},{8,12},{9,13},{10,... | collective-permute-start | bytes 2555912 | tf_op jit(solution)/shard_map/ppermute | solution.py:149
  36.7 195.1 %copy-start.97 = (f32[1536]{0:T(1024)}, f32[1536]{0:T(1024)S(1)}, u32[]{:S(2)}) copy-start(f32[1536]{0:T(1024)S(1)} %add_rsqrt_fusion) | copy-start | bytes 18436
  41.8 18.6 %collective-permute-start.5 = (bf16[416,1024]{1,0:T(8,128)(2,1)S(1)}, bf16[416,1024]{1,0:T(8,128)(2,1)S(1)}, u32[]{:S(2)}, u32[]{:S(2)}) collective-permute-start(bf16[416,1024]{1,0:T(8,128)(2,1)S(1)} %collective-permute-done.refs_1_), channel_id=1, source_target_pairs={{0,1},{1,0},{2,3},{3,2},{4,5},{5,4},{6,7},{7,6},{8,9},{9,8},{10,11... | collective-permute-start | bytes 2555912 | tf_op jit(solution)/shard_map/ppermute | solution.py:149
  41.8 21.4 %collective-permute-start.2 = (bf16[416,1024]{1,0:T(8,128)(2,1)S(1)}, bf16[416,1024]{1,0:T(8,128)(2,1)S(1)}, u32[]{:S(2)}, u32[]{:S(2)}) collective-permute-start(bf16[416,1024]{1,0:T(8,128)(2,1)S(1)} %collective-permute-done.refs_1_), channel_id=1, source_target_pairs={{0,8},{1,9},{2,10},{3,11},{4,12},{5,13},{6,14},{7,15},{8,0},{9,1},... | collective-permute-start | bytes 2555912 | tf_op jit(solution)/shard_map/ppermute | solution.py:149
  43.5 21.1 %collective-permute-start.1 = (bf16[416,1024]{1,0:T(8,128)(2,1)S(1)}, bf16[416,1024]{1,0:T(8,128)(2,1)}, u32[]{:S(2)}, u32[]{:S(2)}) collective-permute-start(bf16[416,1024]{1,0:T(8,128)(2,1)S(1)} %collective-permute-done.refs_1_), channel_id=1, source_target_pairs={{0,4},{1,5},{2,6},{3,7},{4,0},{5,1},{6,2},{7,3},{8,10},{9,11},{10,... | collective-permute-start | bytes 2555912 | tf_op jit(solution)/shard_map/ppermute | solution.py:149
  44.0 15.4 %collective-permute-start.3 = (bf16[256,1024]{1,0:T(8,128)(2,1)}, bf16[256,1024]{1,0:T(8,128)(2,1)S(1)}, u32[]{:S(2)}, u32[]{:S(2)}) collective-permute-start(bf16[256,1024]{1,0:T(8,128)(2,1)} %pad_maximum_fusion.2.refs_0_), channel_id=1, source_target_pairs={{0,2},{1,3},{2,0},{3,1},{4,6},{5,7},{6,4},{7,5},{8,12},{9,13},{10,... | collective-permute-start | bytes 1572872 | tf_op jit(solution)/shard_map/ppermute | solution.py:149
  45.5 14.0 %collective-permute-start.4 = (bf16[416,1024]{1,0:T(8,128)(2,1)S(1)}, bf16[416,1024]{1,0:T(8,128)(2,1)S(1)}, u32[]{:S(2)}, u32[]{:S(2)}) collective-permute-start(bf16[416,1024]{1,0:T(8,128)(2,1)S(1)} %constant_dynamic-update-slice_fusion.9.refs_0_), channel_id=1, source_target_pairs={{0,1},{1,0},{2,3},{3,2},{4,5},{5,4},{6,7},{7,6},{8,9},{9,8},{10,11... | collective-permute-start | bytes 2555912 | tf_op jit(solution)/shard_map/ppermute | solution.py:149
  64.6 3.7 collective-permute-start.11
  64.6 4.2 collective-permute-start.12
  65.3 29.2 %collective-permute-start.8 = (bf16[256,1024]{1,0:T(8,128)(2,1)}, bf16[256,1024]{1,0:T(8,128)(2,1)}, u32[]{:S(2)}, u32[]{:S(2)}) collective-permute-start(bf16[256,1024]{1,0:T(8,128)(2,1)} %pad_maximum_fusion.2.refs_0_), channel_id=1, source_target_pairs={{0,1},{1,0},{2,3},{3,2},{4,5},{5,4},{6,7},{7,6},{8,9},{9,8},{10,11... | collective-permute-start | bytes 1572872 | tf_op jit(solution)/shard_map/ppermute | solution.py:149
  65.3 32.0 %collective-permute-start.9 = (bf16[256,1024]{1,0:T(8,128)(2,1)}, bf16[256,1024]{1,0:T(8,128)(2,1)}, u32[]{:S(2)}, u32[]{:S(2)}) collective-permute-start(bf16[256,1024]{1,0:T(8,128)(2,1)} %copy-done.41), channel_id=1, source_target_pairs={{0,1},{1,0},{2,3},{3,2},{4,5},{5,4},{6,7},{7,6},{8,9},{9,8},{10,11... | collective-permute-start | bytes 1572872 | tf_op jit(solution)/shard_map/ppermute | solution.py:149
  65.8 31.5 %collective-permute-start.7 = (bf16[256,1024]{1,0:T(8,128)(2,1)}, bf16[256,1024]{1,0:T(8,128)(2,1)}, u32[]{:S(2)}, u32[]{:S(2)}) collective-permute-start(bf16[256,1024]{1,0:T(8,128)(2,1)} %copy-done.41), channel_id=1, source_target_pairs={{0,8},{1,9},{2,10},{3,11},{4,12},{5,13},{6,14},{7,15},{8,0},{9,1},... | collective-permute-start | bytes 1572872 | tf_op jit(solution)/shard_map/ppermute | solution.py:149
  68.3 29.0 %collective-permute-start.6 = (bf16[256,1024]{1,0:T(8,128)(2,1)}, bf16[256,1024]{1,0:T(8,128)(2,1)}, u32[]{:S(2)}, u32[]{:S(2)}) collective-permute-start(bf16[256,1024]{1,0:T(8,128)(2,1)} %copy-done.41), channel_id=1, source_target_pairs={{0,4},{1,5},{2,6},{3,7},{4,0},{5,1},{6,2},{7,3},{8,10},{9,11},{10,... | collective-permute-start | bytes 1572872 | tf_op jit(solution)/shard_map/ppermute | solution.py:149
  68.8 28.5 %collective-permute-start.10 = (bf16[128,4096]{1,0:T(8,128)(2,1)}, bf16[128,4096]{1,0:T(8,128)(2,1)}, u32[]{:S(2)}, u32[]{:S(2)}) collective-permute-start(bf16[128,4096]{1,0:T(8,128)(2,1)} %refs_0_), channel_id=1, source_target_pairs={{0,2},{1,3},{2,0},{3,1},{4,6},{5,7},{6,4},{7,5},{8,12},{9,13},{10,... | collective-permute-start | bytes 3145736 | tf_op jit(solution)/shard_map/ppermute | solution.py:149
  89.7 45.1 %copy-start = (bf16[1536,1024]{1,0:T(8,128)(2,1)}, bf16[1536,1024]{1,0:T(8,128)(2,1)S(1)}, u32[]{:S(2)}) copy-start(bf16[1536,1024]{1,0:T(8,128)(2,1)S(1)} %convolution_convert_fusion.4.v_ref) | copy-start | bytes 9437188
  94.5 19.3 %collective-permute-start.15 = (bf16[128,4096]{1,0:T(8,128)(2,1)}, bf16[128,4096]{1,0:T(8,128)(2,1)}, u32[]{:S(2)}, u32[]{:S(2)}) collective-permute-start(bf16[128,4096]{1,0:T(8,128)(2,1)} %refs_0_), channel_id=1, source_target_pairs={{0,1},{1,0},{2,3},{3,2},{4,5},{5,4},{6,7},{7,6},{8,9},{9,8},{10,11... | collective-permute-start | bytes 3145736 | tf_op jit(solution)/shard_map/ppermute | solution.py:149
  97.3 2.3 collective-permute-start.18
  97.8 4.1 collective-permute-start.19
  98.6 33.7 %collective-permute-start.16 = (bf16[128,4096]{1,0:T(8,128)(2,1)}, bf16[128,4096]{1,0:T(8,128)(2,1)}, u32[]{:S(2)}, u32[]{:S(2)}) collective-permute-start(bf16[128,4096]{1,0:T(8,128)(2,1)} %collective-permute-done.10.refs_1_), channel_id=1, source_target_pairs={{0,1},{1,0},{2,3},{3,2},{4,5},{5,4},{6,7},{7,6},{8,9},{9,8},{10,11... | collective-permute-start | bytes 3145736 | tf_op jit(solution)/shard_map/ppermute | solution.py:149
  99.1 33.2 %collective-permute-start.14 = (bf16[128,4096]{1,0:T(8,128)(2,1)}, bf16[128,4096]{1,0:T(8,128)(2,1)}, u32[]{:S(2)}, u32[]{:S(2)}) collective-permute-start(bf16[128,4096]{1,0:T(8,128)(2,1)} %collective-permute-done.10.refs_1_), channel_id=1, source_target_pairs={{0,8},{1,9},{2,10},{3,11},{4,12},{5,13},{6,14},{7,15},{8,0},{9,1},... | collective-permute-start | bytes 3145736 | tf_op jit(solution)/shard_map/ppermute | solution.py:149
  100.4 31.9 %collective-permute-start.13 = (bf16[128,4096]{1,0:T(8,128)(2,1)}, bf16[128,4096]{1,0:T(8,128)(2,1)}, u32[]{:S(2)}, u32[]{:S(2)}) collective-permute-start(bf16[128,4096]{1,0:T(8,128)(2,1)} %collective-permute-done.10.refs_1_), channel_id=1, source_target_pairs={{0,4},{1,5},{2,6},{3,7},{4,0},{5,1},{6,2},{7,3},{8,10},{9,11},{10,... | collective-permute-start | bytes 3145736 | tf_op jit(solution)/shard_map/ppermute | solution.py:149
  102.7 29.6 %collective-permute-start.17 = (bf16[512,1024]{1,0:T(8,128)(2,1)}, bf16[512,1024]{1,0:T(8,128)(2,1)}, u32[]{:S(2)}, u32[]{:S(2)}) collective-permute-start(bf16[512,1024]{1,0:T(8,128)(2,1)} %refs_0_.1), channel_id=1, source_target_pairs={{0,2},{1,3},{2,0},{3,1},{4,6},{5,7},{6,4},{7,5},{8,12},{9,13},{10,... | collective-permute-start | bytes 3145736 | tf_op jit(solution)/shard_map/ppermute | solution.py:149
  113.8 38.5 %copy-start.59 = (bf16[1024,1024]{1,0:T(8,128)(2,1)}, bf16[1024,1024]{1,0:T(8,128)(2,1)S(1)}, u32[]{:S(2)}) copy-start(bf16[1024,1024]{1,0:T(8,128)(2,1)S(1)} %get-tuple-element.138) | copy-start | bytes 6291460
  113.8 36.9 %collective-permute-start.22 = (bf16[512,1024]{1,0:T(8,128)(2,1)}, bf16[512,1024]{1,0:T(8,128)(2,1)S(1)}, u32[]{:S(2)}, u32[]{:S(2)}) collective-permute-start(bf16[512,1024]{1,0:T(8,128)(2,1)} %refs_0_.1), channel_id=1, source_target_pairs={{0,1},{1,0},{2,3},{3,2},{4,5},{5,4},{6,7},{7,6},{8,9},{9,8},{10,11... | collective-permute-start | bytes 3145736 | tf_op jit(solution)/shard_map/ppermute | solution.py:149
  117.6 17.2 %copy-start.2 = (bf16[1536,1024]{1,0:T(8,128)(2,1)}, bf16[1536,1024]{1,0:T(8,128)(2,1)S(1)}, u32[]{:S(2)}) copy-start(bf16[1536,1024]{1,0:T(8,128)(2,1)S(1)} %convolution_convert_fusion.3.r_ref) | copy-start | bytes 9437188
  117.6 14.7 %copy-start.33 = (bf16[384,1024]{1,0:T(8,128)(2,1)S(1)}, bf16[384,1024]{1,0:T(8,128)(2,1)}, u32[]{:S(2)}) copy-start(bf16[384,1024]{1,0:T(8,128)(2,1)} %refs_0_.2) | copy-start | bytes 2359300
  132.3 20.0 %collective-permute-start.24 = (bf16[384,1024]{1,0:T(8,128)(2,1)S(1)}, bf16[384,1024]{1,0:T(8,128)(2,1)S(1)}, u32[]{:S(2)}, u32[]{:S(2)}) collective-permute-start(bf16[384,1024]{1,0:T(8,128)(2,1)S(1)} %copy-done.33), channel_id=1, source_target_pairs={{0,2},{1,3},{2,0},{3,1},{4,6},{5,7},{6,4},{7,5},{8,12},{9,13},{10,... | collective-permute-start | bytes 2359304 | tf_op jit(solution)/shard_map/ppermute | solution.py:149
  133.9 19.8 %collective-permute-start.25 = (bf16[128,4096]{1,0:T(8,128)(2,1)}, bf16[128,4096]{1,0:T(8,128)(2,1)S(1)}, u32[]{:S(2)}, u32[]{:S(2)}) collective-permute-start(bf16[128,4096]{1,0:T(8,128)(2,1)} %collective-permute-done.14.refs_2_), channel_id=1, source_target_pairs={{0,1},{1,0},{2,3},{3,2},{4,5},{5,4},{6,7},{7,6},{8,9},{9,8},{10,11... | collective-permute-start | bytes 3145736 | tf_op jit(solution)/shard_map/ppermute | solution.py:149
  134.8 17.5 %copy-start.70 = (bf16[1,512,1024]{2,1,0:T(8,128)(2,1)S(1)}, bf16[1,512,1024]{2,1,0:T(8,128)(2,1)}, u32[]{:S(2)}) copy-start(bf16[1,512,1024]{2,1,0:T(8,128)(2,1)} %param.25) | copy-start | bytes 3145732
  149.7 5.5 %collective-permute-start.23 = (bf16[512,1024]{1,0:T(8,128)(2,1)}, bf16[512,1024]{1,0:T(8,128)(2,1)S(1)}, u32[]{:S(2)}, u32[]{:S(2)}) collective-permute-start(bf16[512,1024]{1,0:T(8,128)(2,1)} %collective-permute-done.17.refs_1_), channel_id=1, source_target_pairs={{0,1},{1,0},{2,3},{3,2},{4,5},{5,4},{6,7},{7,6},{8,9},{9,8},{10,11... | collective-permute-start | bytes 3145736 | tf_op jit(solution)/shard_map/ppermute | solution.py:149
  150.0 25.5 %collective-permute-start.21 = (bf16[512,1024]{1,0:T(8,128)(2,1)}, bf16[512,1024]{1,0:T(8,128)(2,1)S(1)}, u32[]{:S(2)}, u32[]{:S(2)}) collective-permute-start(bf16[512,1024]{1,0:T(8,128)(2,1)} %collective-permute-done.17.refs_1_), channel_id=1, source_target_pairs={{0,8},{1,9},{2,10},{3,11},{4,12},{5,13},{6,14},{7,15},{8,0},{9,1},... | collective-permute-start | bytes 3145736 | tf_op jit(solution)/shard_map/ppermute | solution.py:149
  150.7 25.2 %collective-permute-start.20 = (bf16[512,1024]{1,0:T(8,128)(2,1)}, bf16[512,1024]{1,0:T(8,128)(2,1)S(1)}, u32[]{:S(2)}, u32[]{:S(2)}) collective-permute-start(bf16[512,1024]{1,0:T(8,128)(2,1)} %collective-permute-done.17.refs_1_), channel_id=1, source_target_pairs={{0,4},{1,5},{2,6},{3,7},{4,0},{5,1},{6,2},{7,3},{8,10},{9,11},{10,... | collective-permute-start | bytes 3145736 | tf_op jit(solution)/shard_map/ppermute | solution.py:149
  152.3 25.1 %copy-start.35 = (bf16[384,1024]{1,0:T(8,128)(2,1)}, bf16[384,1024]{1,0:T(8,128)(2,1)S(1)}, u32[]{:S(2)}) copy-start(bf16[384,1024]{1,0:T(8,128)(2,1)S(1)} %collective-permute-done.24.refs_1_) | copy-start | bytes 2359300
  152.3 2.9 collective-permute-start.26
  153.7 23.7 %copy-start.64 = (f32[512,1024]{1,0:T(8,128)}, f32[512,1024]{1,0:T(8,128)S(1)}, u32[]{:S(2)}) copy-start(f32[512,1024]{1,0:T(8,128)S(1)} %get-tuple-element.140) | copy-start | bytes 6291460
  153.7 28.0 %collective-permute-start.29 = (bf16[384,1024]{1,0:T(8,128)(2,1)S(1)}, bf16[384,1024]{1,0:T(8,128)(2,1)S(1)}, u32[]{:S(2)}, u32[]{:S(2)}) collective-permute-start(bf16[384,1024]{1,0:T(8,128)(2,1)S(1)} %copy-done.33), channel_id=1, source_target_pairs={{0,1},{1,0},{2,3},{3,2},{4,5},{5,4},{6,7},{7,6},{8,9},{9,8},{10,11... | collective-permute-start | bytes 2359304 | tf_op jit(solution)/shard_map/ppermute | solution.py:149
  155.1 27.2 %copy-start.85 = (bf16[512,1024]{1,0:T(8,128)(2,1)}, bf16[512,1024]{1,0:T(8,128)(2,1)S(1)}, u32[]{:S(2)}) copy-start(bf16[512,1024]{1,0:T(8,128)(2,1)S(1)} %add_convert_fusion.2) | copy-start | bytes 3145732
  176.0 15.6 %collective-permute-start.30 = (bf16[384,1024]{1,0:T(8,128)(2,1)S(1)}, bf16[384,1024]{1,0:T(8,128)(2,1)S(1)}, u32[]{:S(2)}, u32[]{:S(2)}) collective-permute-start(bf16[384,1024]{1,0:T(8,128)(2,1)S(1)} %collective-permute-done.24.refs_1_), channel_id=1, source_target_pairs={{0,1},{1,0},{2,3},{3,2},{4,5},{5,4},{6,7},{7,6},{8,9},{9,8},{10,11... | collective-permute-start | bytes 2359304 | tf_op jit(solution)/shard_map/ppermute | solution.py:149
  176.0 20.1 %collective-permute-start.28 = (bf16[384,1024]{1,0:T(8,128)(2,1)S(1)}, bf16[384,1024]{1,0:T(8,128)(2,1)}, u32[]{:S(2)}, u32[]{:S(2)}) collective-permute-start(bf16[384,1024]{1,0:T(8,128)(2,1)S(1)} %collective-permute-done.24.refs_1_), channel_id=1, source_target_pairs={{0,8},{1,9},{2,10},{3,11},{4,12},{5,13},{6,14},{7,15},{8,0},{9,1},... | collective-permute-start | bytes 2359304 | tf_op jit(solution)/shard_map/ppermute | solution.py:149
  177.4 19.8 %collective-permute-start.27 = (bf16[384,1024]{1,0:T(8,128)(2,1)S(1)}, bf16[384,1024]{1,0:T(8,128)(2,1)}, u32[]{:S(2)}, u32[]{:S(2)}) collective-permute-start(bf16[384,1024]{1,0:T(8,128)(2,1)S(1)} %collective-permute-done.24.refs_1_), channel_id=1, source_target_pairs={{0,4},{1,5},{2,6},{3,7},{4,0},{5,1},{6,2},{7,3},{8,10},{9,11},{10,... | collective-permute-start | bytes 2359304 | tf_op jit(solution)/shard_map/ppermute | solution.py:149
  178.0 19.3 %collective-permute-start.31 = (bf16[512,1024]{1,0:T(8,128)(2,1)S(1)}, bf16[512,1024]{1,0:T(8,128)(2,1)S(1)}, u32[]{:S(2)}, u32[]{:S(2)}) collective-permute-start(bf16[512,1024]{1,0:T(8,128)(2,1)S(1)} %collective-permute-done.21.refs_2_), channel_id=1, source_target_pairs={{0,1},{1,0},{2,3},{3,2},{4,5},{5,4},{6,7},{7,6},{8,9},{9,8},{10,11... | collective-permute-start | bytes 3145736 | tf_op jit(solution)/shard_map/ppermute | solution.py:149
  181.7 16.5 %collective-permute-start.32 = (bf16[512,1024]{1,0:T(8,128)(2,1)S(1)}, bf16[512,1024]{1,0:T(8,128)(2,1)S(1)}, u32[]{:S(2)}, u32[]{:S(2)}) collective-permute-start(bf16[512,1024]{1,0:T(8,128)(2,1)S(1)} %collective-permute-done.20.refs_3_), channel_id=1, source_target_pairs={{0,1},{1,0},{2,3},{3,2},{4,5},{5,4},{6,7},{7,6},{8,9},{9,8},{10,11... | collective-permute-start | bytes 3145736 | tf_op jit(solution)/shard_map/ppermute | solution.py:149
  199.2 190.4 %reduce-scatter.8.cloned.1.call-start = ((), (), s32[]{:S(2)}) async-start(), calls=%async_computation.5 | async-start | bytes 9437184 | tf_op jit(solution)/shard_map/reduce_scatter | solution.py:930
  231.7 179.6 %reduce-scatter.6.cloned.1.call-start = ((), (), s32[]{:S(2)}) async-start(), calls=%async_computation.4 | async-start | bytes 9437184 | tf_op jit(solution)/shard_map/reduce_scatter | solution.py:915
  234.3 56.3 %collective-permute-start.33 = (bf16[384,1024]{1,0:T(8,128)(2,1)}, bf16[384,1024]{1,0:T(8,128)(2,1)}, u32[]{:S(2)}, u32[]{:S(2)}) collective-permute-start(bf16[384,1024]{1,0:T(8,128)(2,1)} %collective-permute-done.28.refs_2_), channel_id=1, source_target_pairs={{0,1},{1,0},{2,3},{3,2},{4,5},{5,4},{6,7},{7,6},{8,9},{9,8},{10,11... | collective-permute-start | bytes 2359304 | tf_op jit(solution)/shard_map/ppermute | solution.py:149
  234.4 56.3 %collective-permute-start.34 = (bf16[384,1024]{1,0:T(8,128)(2,1)}, bf16[384,1024]{1,0:T(8,128)(2,1)}, u32[]{:S(2)}, u32[]{:S(2)}) collective-permute-start(bf16[384,1024]{1,0:T(8,128)(2,1)} %collective-permute-done.27.refs_3_), channel_id=1, source_target_pairs={{0,1},{1,0},{2,3},{3,2},{4,5},{5,4},{6,7},{7,6},{8,9},{9,8},{10,11... | collective-permute-start | bytes 2359304 | tf_op jit(solution)/shard_map/ppermute | solution.py:149
  (100 other events, 374.0 us)
Sparse Core Ops, SparseCore 0:
  199.4 61.9 reduce-scatter.3
  265.3 71.3 reduce-scatter.7
  340.1 71.2 reduce-scatter.5

commit v3 on v2

v3 whole, which is shorter than its diff:
```python
import functools
import math

import jax
import jax.numpy as jnp
from jax import lax
from jax.experimental import pallas as pl
from jax.experimental.pallas import tpu as pltpu
from jax.sharding import PartitionSpec as P

HEADS = 8
DH = 128
RATE = 3
BLK = 128
NEG = -1.2e10
f32 = jnp.float32
bf16 = jnp.bfloat16


EPSILON = 1e-05
MASKED = -1000000000.0


def smooth_gate(values):
    return jax.nn.gelu(values, approximate=True)


def norm_parts(rows, gain, shift):
    center = jnp.mean(rows, axis=-1, keepdims=True)
    centered = rows - center
    spread = lax.rsqrt(jnp.mean(centered * centered, axis=-1, keepdims=True) + EPSILON)
    scaled = centered * spread
    return (scaled * gain.astype(jnp.float32) + shift.astype(jnp.float32), scaled, spread)


def norm_back(grad, scaled, spread, gain):
    inner = grad * gain.astype(jnp.float32)
    return spread * (
        inner
        - jnp.mean(inner, axis=-1, keepdims=True)
        - scaled * jnp.mean(inner * scaled, axis=-1, keepdims=True)
    )


def positions(count, width):
    distance = (count - 1 - jnp.arange(count, dtype=jnp.int32)).astype(jnp.float32)
    rates = jnp.exp(
        jnp.arange(0, width, 2, dtype=jnp.int32).astype(jnp.float32) * (-math.log(10000.0) / width)
    )
    angle = distance[:, None] * rates[None, :]
    return jnp.concatenate([jnp.sin(angle), jnp.cos(angle)], axis=1)


def dot_nt(a,b): return lax.dot_general(a,b,(((1,),(1,)),((),())),preferred_element_type=f32)
def dot_nn(a,b): return lax.dot_general(a,b,(((1,),(0,)),((),())),preferred_element_type=f32)

def attn_fwd_kernel(qu_ref,qv_ref,k_ref,v_ref,r_ref,bias_ref,o_ref,p_ref,beside=None):
    seg=qu_ref.shape[0]; total=k_ref.shape[0]; old=total-seg
    c=math.log2(math.e)/math.sqrt(DH)
    for ib in range(seg//BLK):
        if beside is not None: beside(ib)
        rows=pl.ds(ib*BLK,BLK)
        L=old+(ib+1)*BLK
        qu=qu_ref[rows,:]; qv=qv_ref[rows,:]
        raw=dot_nt(qv,r_ref[pl.ds(total-L,L),:])
        z=dot_nt(qu,k_ref[pl.ds(0,L),:])+pltpu.roll(raw,L-(BLK-1),axis=1,stride=1,stride_axis=0)
        M=L-BLK
        za=z[:,:M]+bias_ref[:,:M]
        rr=lax.broadcasted_iota(jnp.int32,(BLK,BLK),0); cc=lax.broadcasted_iota(jnp.int32,(BLK,BLK),1)
        zb=z[:,M:]
        zb=jnp.where(cc==rr,zb,jnp.where(cc<rr,zb+bias_ref[:,pl.ds(M,BLK)],NEG))
        top=jnp.maximum(jnp.max(za,axis=1,keepdims=True),jnp.max(zb,axis=1,keepdims=True))
        ea=jnp.exp2((za-top)*c); eb=jnp.exp2((zb-top)*c)
        inv=1.0/(jnp.sum(ea,axis=1,keepdims=True)+jnp.sum(eb,axis=1,keepdims=True))
        pa=(ea*inv).astype(bf16); pb=(eb*inv).astype(bf16)
        p_ref[0,rows,pl.ds(0,M)]=pa
        p_ref[0,rows,pl.ds(M,BLK)]=pb
        o_ref[rows,:]=(dot_nn(pa,v_ref[pl.ds(0,M),:])+dot_nn(pb,v_ref[pl.ds(M,BLK),:])).astype(bf16)

def attn_fwd_gather_kernel(pieces, *refs):
    shard, whole = refs[6], refs[9]
    local, sent, came = refs[10:]
    head = pl.program_id(0)
    height = shard.shape[0]
    rows = height // pieces
    moved = Gathering([(shard, n * rows, rows, whole, height) for n in range(pieces)], local, sent, came)

    @pl.when(head == 0)
    def _():
        moved.greet()
        for n in range(pieces):
            moved.begin(n)

    tiles = refs[0].shape[0] // BLK
    steps = {}
    for n in range(pieces):
        slot = 7 + (26 * n) // pieces
        steps.setdefault(slot, []).append((moved.onward, n))
        if n:
            steps.setdefault(slot, []).append((moved.last, n - 1))

    def beside(tile):
        for slot, phases in steps.items():
            if slot % tiles == tile:

                @pl.when(head == slot // tiles)
                def _(phases=phases):
                    for phase, n in phases:
                        phase(n)

    attn_fwd_kernel(*refs[:6], *refs[7:9], beside=beside)

    @pl.when(head == HEADS - 1)
    def _():
        moved.last(pieces - 1)
        for n in range(pieces):
            moved.complete(n)
        moved.drain()


def attn_fwd(qu, qv, k, v, r, bias, shard=None, pieces=8):
    seg, width = qu.shape
    total = k.shape[0]
    col = lambda n: pl.BlockSpec((n, DH), lambda h: (0, h))
    in_specs = [col(seg), col(seg), col(total), col(total), col(total)]
    in_specs += [pl.BlockSpec((1, total), lambda h: (0, 0))]
    out_specs = [col(seg), pl.BlockSpec((1, seg, total), lambda h: (h, 0, 0))]
    out_shape = [
        jax.ShapeDtypeStruct((seg, width), bf16),
        jax.ShapeDtypeStruct((HEADS, seg, total), bf16),
    ]
    cost = pl.CostEstimate(
        flops=6 * seg * total * width,
        bytes_accessed=2 * (3 * seg * width + 3 * total * width + HEADS * seg * total),
        transcendentals=HEADS * seg * total,
    )
    if shard is None:
        return pl.pallas_call(
            attn_fwd_kernel,
            grid=(HEADS,),
            in_specs=in_specs,
            out_specs=out_specs,
            out_shape=out_shape,
            cost_estimate=cost,
            compiler_params=pltpu.CompilerParams(vmem_limit_bytes=58 << 20),
            name="attn_fwd",
        )(qu, qv, k, v, r, bias)
    return pl.pallas_call(
        functools.partial(attn_fwd_gather_kernel, pieces),
        grid=(HEADS,),
        in_specs=in_specs + [pl.BlockSpec(shard.shape, lambda h: (0, 0))],
        out_specs=out_specs + [pl.BlockSpec(memory_space=pl.ANY)],
        out_shape=out_shape + [jax.ShapeDtypeStruct((8 * shard.shape[0], shard.shape[1]), bf16)],
        scratch_shapes=[pltpu.SemaphoreType.DMA((n * pieces,)) for n in (1, 7, 7)],
        cost_estimate=cost,
        compiler_params=pltpu.CompilerParams(
            collective_id=3, has_side_effects=True, vmem_limit_bytes=58 << 20
        ),
        name="attn_fwd_gather",
    )(qu, qv, k, v, r, bias, shard)


def attn_bwd_kernel(qu_ref,qv_ref,qut_ref,qvrt_ref,k_ref,v_ref,r_ref,p_ref,g_ref,gt_ref,dq_ref,dkt_ref,dvt_ref,drt_ref,sums_ref,dk_acc,dv_acc,dr_acc):
    seg=g_ref.shape[0]; total=k_ref.shape[0]; old=total-seg
    scale=1.0/math.sqrt(DH)
    rr=lax.broadcasted_iota(jnp.int32,(BLK,BLK),0); cc=lax.broadcasted_iota(jnp.int32,(BLK,BLK),1)
    flip=(rr+cc==BLK-1).astype(bf16)
    su=jnp.zeros((1,DH),f32); sv=jnp.zeros((1,DH),f32)
    nb=seg//BLK
    for ib in range(nb-1,-1,-1):
        rows=pl.ds(ib*BLK,BLK)
        L=old+(ib+1)*BLK
        g=g_ref[rows,:]; gt=gt_ref[:,rows]; qut=qut_ref[:,rows]
        plow=p_ref[0,rows,pl.ds(0,L)]
        p=plow.astype(f32)
        dp=dot_nt(g,v_ref[pl.ds(0,L),:])
        d=jnp.sum(p*dp,axis=1,keepdims=True)
        dz=(p*(dp-d)*scale).astype(bf16)
        dvt=dot_nn(gt,plow)
        dkt=dot_nn(qut,dz)
        dqu=dot_nn(dz,k_ref[pl.ds(0,L),:])
        rev=dot_nn(flip,dz)
        raw=pltpu.roll(rev,0,axis=1,stride=1,stride_axis=0).astype(bf16)
        T=pl.ds(total-L,L)
        dqv_rev=dot_nn(raw,r_ref[T,:])
        qvr=dot_nt(qvrt_ref[:,rows],flip).astype(bf16)
        drt=dot_nn(qvr,raw)
        dqv=lax.dot_general(flip.astype(f32),dqv_rev,(((1,),(0,)),((),())),preferred_element_type=f32,precision=lax.Precision.HIGHEST)
        su+=jnp.sum(dqu,axis=0,keepdims=True); sv+=jnp.sum(dqv,axis=0,keepdims=True)
        dq_ref[rows,:]=(dqu+dqv).astype(bf16)
        J=pl.ds(0,L)
        if ib==nb-1:
            dv_acc[...]=dvt; dk_acc[...]=dkt; dr_acc[...]=drt
        else:
            dv_acc[:,J]+=dvt; dk_acc[:,J]+=dkt; dr_acc[:,T]+=drt
    dkt_ref[...]=dk_acc[...].astype(bf16); dvt_ref[...]=dv_acc[...].astype(bf16); drt_ref[...]=dr_acc[...].astype(bf16)
    sums_ref[0:1,:]=su; sums_ref[1:2,:]=sv

def attn_bwd_sums_kernel(plan, sources, count, *refs):
    base, grads = refs[:10], refs[10 : 10 + count]
    refs = refs[10 + count :]
    results, outs, refs = refs[:5], refs[5 : 5 + count], refs[5 + count :]
    totals = refs[:3]
    sums = Sums(plan, sources, grads, outs, refs[3:])
    steps = sums.schedule()
    head = pl.program_id(0)
    per = -(-len(steps) // HEADS) if len(steps) > HEADS + 2 else 1

    for n in range(HEADS):

        @pl.when(head == n)
        def _(n=n):
            if n == 0:
                sums.greet()
            for step in steps[n * per : (n + 1) * per]:
                for phase, item in step:
                    phase(item)

    attn_bwd_kernel(*base, *results, *totals)

    @pl.when(head == HEADS - 1)
    def _():
        for step in steps[HEADS * per :]:
            for phase, item in step:
                phase(item)
        sums.drain()


def attn_bwd(qu, qv, k, v, r, p, g, grads=(), share=1.0):
    seg, width = qu.shape
    total = k.shape[0]
    col = lambda n: pl.BlockSpec((n, DH), lambda h: (0, h))
    row = lambda n: pl.BlockSpec((DH, n), lambda h: (h, 0))
    any_spec = pl.BlockSpec(memory_space=pl.ANY)
    in_specs = [col(seg), col(seg), row(seg), row(seg), col(total), col(total), col(total)]
    in_specs += [pl.BlockSpec((1, seg, total), lambda h: (h, 0, 0)), col(seg), row(seg)]
    out_specs = [col(seg), row(total), row(total), row(total), pl.BlockSpec((8, DH), lambda h: (0, h))]
    out_shape = [jax.ShapeDtypeStruct((seg, width), bf16)]
    out_shape += [jax.ShapeDtypeStruct((width, total), bf16)] * 3
    out_shape += [jax.ShapeDtypeStruct((8, width), f32)]
    scratch = [pltpu.VMEM((DH, total), f32)] * 3
    cost = pl.CostEstimate(
        flops=16 * seg * total * width,
        bytes_accessed=2 * (5 * seg * width + 6 * total * width + HEADS * seg * total),
        transcendentals=0,
    )
    operands = (qu, qv, qu.T, qv.T, k, v, r, p, g, g.T)
    if not grads:
        return pl.pallas_call(
            attn_bwd_kernel,
            grid=(HEADS,),
            in_specs=in_specs,
            out_specs=out_specs,
            out_shape=out_shape,
            scratch_shapes=scratch,
            cost_estimate=cost,
            compiler_params=pltpu.CompilerParams(vmem_limit_bytes=58 << 20),
            name="attn_bwd",
        )(*operands)
    plan, sources, arrays, shapes = sums_plan(grads, ())
    results = pl.pallas_call(
        functools.partial(attn_bwd_sums_kernel, plan, sources, len(arrays)),
        grid=(HEADS,),
        in_specs=in_specs + [any_spec] * len(arrays),
        out_specs=out_specs + [any_spec] * len(arrays),
        out_shape=out_shape + shapes,
        scratch_shapes=scratch + sums_scratch(plan),
        cost_estimate=cost,
        compiler_params=pltpu.CompilerParams(
            collective_id=4, has_side_effects=True, vmem_limit_bytes=58 << 20
        ),
        name="attn_bwd_sums",
    )(*operands, *arrays)
    return tuple(results[:5]) + tuple(total.astype(f32) * share for total in results[5:])


def cut(*values):
    return lax.optimization_barrier(values)


def positions_low(count, width):
    tile = 64
    rates = jnp.exp(
        jnp.arange(0, width, 2, dtype=jnp.int32).astype(f32) * (-math.log(10000.0) / width)
    )
    rates = jnp.concatenate([rates, rates])[None, :]
    upper = (jnp.arange(width, dtype=jnp.int32) < width // 2)[None, :]
    far = (count - 1 - tile * jnp.arange(count // tile, dtype=jnp.int32)).astype(f32)[:, None] * rates
    near = jnp.arange(tile, dtype=jnp.int32).astype(f32)[:, None] * rates
    sine, cosine = jnp.sin(far), jnp.cos(far)
    with_cos = jnp.where(upper, sine, cosine)[:, None, :]
    with_sin = jnp.where(upper, -cosine, sine)[:, None, :]
    near_cos, near_sin, with_cos, with_sin = cut(jnp.cos(near), jnp.sin(near), with_cos, with_sin)
    table = with_cos * near_cos[None] + with_sin * near_sin[None]
    return table.astype(bf16).reshape(count, width)


def hop(value, move):
    dp, fsdp = lax.axis_size("dp"), lax.axis_size("fsdp")
    pairs = []
    for z in range(dp):
        for f in range(fsdp):
            to = move(z, f)
            if to is not None:
                pairs.append((z * fsdp + f, to[0] * fsdp + to[1]))
    return lax.ppermute(value, ("dp", "fsdp"), pairs)


def inward_hop(w):
    to = {0: 1, 3: 2}
    return hop(w, lambda z, f: (to[z], f) if z in to else None)


def middle_hop(w):
    return hop(w, lambda z, f: (3 - z, f) if z in (1, 2) else None)


def outward_hop(w):
    to = {1: 0, 2: 3}
    return hop(w, lambda z, f: (to[z], f) if z in to else None)


def add(first, second):
    return (first.astype(f32) + second.astype(f32)).astype(bf16)


def finish(whole, last, share):
    plane = lax.axis_index("dp")
    return jnp.where((plane == 1) | (plane == 2), whole, last).astype(f32) * share


def add_rows(out, parts):
    rows = out.shape[0]
    height = 32 if rows % 32 == 0 else 16

    def one(i, carry):
        at = pl.ds(pl.multiple_of(i * height, height), height)
        total = parts[0][at, :].astype(f32)
        for part in parts[1:]:
            total = total + part[at, :].astype(f32)
        out[at, :] = total.astype(out.dtype)
        return carry

    lax.fori_loop(0, rows // height, one, 0)


FULL_BUFFERS = ("mine", "theirs", "far", "half_x", "half_y", "to_y", "to_x", "got_y", "got_x")
LINE_BUFFERS = ("own", "end", "mid")


def sums_scratch(plan):
    shapes = []
    for full, rows, cols in plan:
        if full:
            half = pltpu.VMEM((rows // 2, cols), bf16)
            one = pltpu.VMEM((rows, cols), bf16)
            shapes += [pltpu.VMEM((4, rows, cols), bf16)] * 2 + [one, half, half] + [one] * 4
        shapes += [pltpu.VMEM((rows, cols), bf16)] * 3
        shapes += [pltpu.SemaphoreType.DMA((n,)) for n in (4, 11, 11, 1)]
    return shapes


GAP, LINE_GAP = 2, 2


class Sums:
    def __init__(self, plan, sources, grads, outs, scratch):
        self.z, self.f = lax.axis_index("dp"), lax.axis_index("fsdp")
        self.chip, self.core = self.f // 2, self.f % 2
        self.middle = (self.z == 1) | (self.z == 2)
        self.edge = jnp.logical_not(self.middle)
        self.inward = (jnp.where(self.z < 2, 1, 2), self.f)
        self.outward = (jnp.where(self.z < 2, 0, 3), self.f)
        self.across = (3 - self.z, self.f)
        self.sibling, self.by_x, self.by_y = (
            (self.z, self.f ^ 1),
            (self.z, self.f ^ 2),
            (self.z, self.f ^ 4),
        )
        self.items, at = [], 0
        for n, (full, rows, cols) in enumerate(plan):
            names = (FULL_BUFFERS if full else ()) + LINE_BUFFERS + ("local", "sent", "came", "stored")
            b = dict(zip(names, scratch[at : at + len(names)]))
            at += len(names)
            b.update(full=full, rows=rows, source=grads[sources[n][0]], first=sources[n][1])
            b.update(target=outs[sources[n][0]])
            self.items.append(b)

    def greet(self):
        barrier = pltpu.get_barrier_semaphore()

        def signal(device):
            pl.semaphore_signal(
                barrier, inc=1, device_id=device, device_id_type=pl.DeviceIdType.MESH
            )

        for device in (self.sibling, self.by_x, self.by_y):
            signal(device)

        @pl.when(self.middle)
        def _():
            signal(self.outward)
            signal(self.across)
            pl.semaphore_wait(barrier, 5)

        @pl.when(self.edge)
        def _():
            signal(self.inward)
            pl.semaphore_wait(barrier, 4)

    def copy(self, b, n, src, dst, device):
        return pltpu.make_async_remote_copy(
            src_ref=src,
            dst_ref=dst,
            send_sem=b["sent"].at[n],
            recv_sem=b["came"].at[n],
            device_id=device,
            device_id_type=pl.DeviceIdType.MESH,
        )

    def rows_of(self, b):
        return pl.ds(b["first"], b["rows"])

    def across_cores(self, b, s):
        block = (self.chip ^ (3 - s)) * 2 + 1 - self.core
        src = b["source"].at[block, self.rows_of(b), :]
        return self.copy(b, s, src, b["theirs"].at[s], self.sibling)

    def load(self, b, s):
        if not b["full"]:
            src, dst = b["source"].at[self.rows_of(b), :], b["own"]
        else:
            block = (self.chip ^ (3 - s)) * 2 + self.core
            src, dst = b["source"].at[block, self.rows_of(b), :], b["mine"].at[s]
        return pltpu.make_async_copy(src, dst, b["local"].at[s])

    def halves_out(self, b):
        half = b["rows"] // 2
        return (
            self.copy(b, 4, b["far"].at[pl.ds(0, half), :], b["half_x"], self.by_x),
            self.copy(b, 5, b["far"].at[pl.ds(half, half), :], b["half_y"], self.by_y),
        )

    def near_out(self, b):
        return (
            self.copy(b, 6, b["to_y"], b["got_y"], self.by_y),
            self.copy(b, 7, b["to_x"], b["got_x"], self.by_x),
        )

    def go_in(self, b):
        return self.copy(b, 8, b["own"], b["end"], self.inward)

    def go_mid(self, b):
        return self.copy(b, 9, b["own"], b["mid"], self.across)

    def go_out(self, b):
        return self.copy(b, 10, b["mid"], b["end"], self.outward)

    def store(self, b, name):
        return pltpu.make_async_copy(b[name], b["target"].at[self.rows_of(b), :], b["stored"].at[0])

    def begin(self, b):
        if b["full"]:
            for s in range(4):
                self.across_cores(b, s).start()
                self.load(b, s).start()
        else:
            self.load(b, 0).start()

    def arrived(self, b, s):
        self.across_cores(b, s).wait_recv()
        self.load(b, s).wait()

    def far(self, b):
        self.arrived(b, 0)
        add_rows(b["far"], [b["mine"].at[0], b["theirs"].at[0]])
        for c in self.halves_out(b):
            c.start()

    def near(self, b):
        half = b["rows"] // 2
        low, high = pl.ds(0, half), pl.ds(half, half)
        self.arrived(b, 1)
        self.arrived(b, 2)
        for c in self.halves_out(b):
            c.wait_recv()
        mine, theirs = b["mine"], b["theirs"]
        add_rows(b["to_y"].at[low, :], [mine.at[1, low, :], theirs.at[1, low, :], b["half_x"]])
        add_rows(b["to_y"].at[high, :], [mine.at[1, high, :], theirs.at[1, high, :]])
        add_rows(b["to_x"].at[low, :], [mine.at[2, low, :], theirs.at[2, low, :]])
        add_rows(b["to_x"].at[high, :], [mine.at[2, high, :], theirs.at[2, high, :], b["half_y"]])
        for c in self.near_out(b):
            c.start()

    def own(self, b):
        self.arrived(b, 3)
        for c in self.near_out(b):
            c.wait_recv()
        add_rows(b["own"], [b["mine"].at[3], b["theirs"].at[3], b["got_x"], b["got_y"]])

    def line_in(self, b):
        if not b["full"]:
            self.load(b, 0).wait()

        @pl.when(self.edge)
        def _():
            self.go_in(b).start()

    def line_mid(self, b):
        @pl.when(self.middle)
        def _():
            self.go_in(b).wait_recv()
            add_rows(b["own"], [b["own"], b["end"]])
            self.go_mid(b).start()

    def line_out(self, b):
        @pl.when(self.middle)
        def _():
            self.go_mid(b).wait_recv()
            add_rows(b["mid"], [b["own"], b["mid"]])
            self.go_out(b).start()
            self.store(b, "mid").start()

    def line_last(self, b):
        @pl.when(self.edge)
        def _():
            self.go_out(b).wait_recv()
            self.store(b, "end").start()

    def schedule(self):
        wide = [b for b in self.items if b["full"]]
        left = [b for b in self.items if not b["full"]]
        line, due, slot = [], [], 0
        while sum(b is not None for b in line) < len(self.items):
            if 0 <= slot - 2 * GAP < len(wide):
                due.append(wide[slot - 2 * GAP])
            if left and (not due or slot % 2 == 0):
                line.append(left.pop(0))
            elif due:
                line.append(due.pop(0))
            else:
                line.append(None)
            slot += 1
        steps = []
        for t in range(len(line) + 3 * LINE_GAP):
            step = []
            if t + 2 < len(wide):
                step.append((self.begin, wide[t + 2]))
            for phase, back in ((self.far, 0), (self.near, GAP), (self.own, 2 * GAP)):
                if 0 <= t - back < len(wide):
                    step.append((phase, wide[t - back]))
            phases = (self.line_in, self.line_mid, self.line_out, self.line_last)
            for back, phase in enumerate(phases):
                at = t - back * LINE_GAP
                if 0 <= at < len(line) and line[at] is not None:
                    step.append((phase, line[at]))
            steps.append(step)
        first = [(self.begin, b) for b in self.items if not b["full"]]
        first += [(self.begin, b) for b in wide[:2]]
        return [first] + steps

    def drain(self):
        for b in self.items:
            if b["full"]:
                for s in range(4):
                    self.across_cores(b, s).wait_send()
                for c in self.halves_out(b) + self.near_out(b):
                    c.wait_send()
            self.store(b, "mid").wait()

        @pl.when(self.edge)
        def _():
            for b in self.items:
                self.go_in(b).wait_send()

        @pl.when(self.middle)
        def _():
            for b in self.items:
                self.go_mid(b).wait_send()
                self.go_out(b).wait_send()


def sums_plan(fulls, shards):
    plan, sources, arrays, shapes = [], [], [], []
    for full, group in ((True, fulls), (False, shards)):
        for g, pieces in group:
            rows, cols = g.shape[0] // (8 if full else 1), g.shape[1]
            for p in range(pieces):
                plan.append((full, rows // pieces, cols))
                sources.append((len(arrays), p * (rows // pieces)))
            arrays.append(g.reshape(8, rows, cols) if full else g)
            shapes.append(jax.ShapeDtypeStruct((rows, cols), bf16))
    return tuple(plan), tuple(sources), arrays, shapes


def tail_kernel(plan, sources, count, *refs):
    sums = Sums(plan, sources, refs[:count], refs[count : 2 * count], refs[2 * count :])
    sums.greet()
    for step in sums.schedule():
        for phase, item in step:
            phase(item)
    sums.drain()


def reduce_tail(fulls, shards, share, number):
    plan, sources, arrays, shapes = sums_plan(fulls, shards)
    totals = pl.pallas_call(
        functools.partial(tail_kernel, plan, sources, len(arrays)),
        in_specs=[pl.BlockSpec(memory_space=pl.ANY)] * len(arrays),
        out_specs=[pl.BlockSpec(memory_space=pl.ANY)] * len(arrays),
        out_shape=shapes,
        scratch_shapes=sums_scratch(plan),
        compiler_params=pltpu.CompilerParams(
            collective_id=number, has_side_effects=True, vmem_limit_bytes=56 << 20
        ),
        name="reduce_tail",
    )(*arrays)
    return [total.astype(f32) * share for total in totals]


class Gathering:
    def __init__(self, pieces, local, sent, came):
        self.pieces, self.local, self.sent, self.came = pieces, local, sent, came
        z, f = lax.axis_index("dp"), lax.axis_index("fsdp")
        near = 2 + 2 * lax.rem(z, 2)
        self.first_to, self.second_to = (z, f ^ near), (z, f ^ (6 - near))
        self.pair_to, self.core_to = (z ^ 1, f), (z, f ^ 1)
        self.slots = (f, f ^ near, f ^ (6 - near), f ^ 6)

    def greet(self):
        barrier = pltpu.get_barrier_semaphore()
        for device in (self.first_to, self.second_to, self.pair_to, self.core_to):
            pl.semaphore_signal(
                barrier, inc=1, device_id=device, device_id_type=pl.DeviceIdType.MESH
            )
        pl.semaphore_wait(barrier, 4)

    def part(self, n, slot):
        shard, start, rows, whole, height = self.pieces[n]
        return whole.at[pl.ds(pl.multiple_of(slot * height + start, 16), rows), :]

    def shard(self, n):
        shard, start, rows, whole, height = self.pieces[n]
        return shard.at[pl.ds(start, rows), :]

    def copy(self, n, k, src, slot, device):
        return pltpu.make_async_remote_copy(
            src_ref=src,
            dst_ref=self.part(n, slot),
            send_sem=self.sent.at[n * 7 + k],
            recv_sem=self.came.at[n * 7 + k],
            device_id=device,
            device_id_type=pl.DeviceIdType.MESH,
        )

    def first(self, n):
        return self.copy(n, 0, self.shard(n), self.slots[0], self.first_to)

    def pair(self, n):
        return self.copy(n, 1, self.part(n, self.slots[1]), self.slots[1], self.pair_to)

    def second(self, n):
        return self.copy(n, 2, self.part(n, self.slots[1]), self.slots[1], self.second_to)

    def core(self, n, s):
        src = self.shard(n) if s == 0 else self.part(n, self.slots[s])
        return self.copy(n, 3 + s, src, self.slots[s], self.core_to)

    def mine(self, n):
        return pltpu.make_async_copy(self.shard(n), self.part(n, self.slots[0]), self.local.at[n])

    def begin(self, n):
        self.first(n).start()
        self.mine(n).start()
        self.core(n, 0).start()

    def onward(self, n):
        self.first(n).wait_recv()
        self.pair(n).start()
        self.second(n).start()
        self.core(n, 1).start()

    def last(self, n):
        self.pair(n).wait_recv()
        self.core(n, 2).start()
        self.second(n).wait_recv()
        self.core(n, 3).start()

    def complete(self, n):
        self.mine(n).wait()
        for s in range(4):
            self.core(n, s).wait_recv()

    def drain(self):
        for n in range(len(self.pieces)):
            for copy in (self.first(n), self.pair(n), self.second(n)):
                copy.wait_send()
            for s in range(4):
                self.core(n, s).wait_send()


def tile_loop(rows, height, body):
    def one(i, carry):
        body(pl.ds(pl.multiple_of(i * height, height), height))
        return carry

    lax.fori_loop(0, rows // height, one, 0)


HEAD_ITEMS = ("table", "keys", "values", "query", "position", "output", "inner")
INNER_PIECES = 4


def head_kernel(*refs):
    count = len(HEAD_ITEMS)
    rows_in, shards, pos_ref = refs[:3], refs[3 : 3 + count], refs[3 + count]
    refs = refs[4 + count :]
    (xhat_out, normed_out, qu_out, qv_out, keys_out, values_out, relative_out) = refs[:7]
    weights_out, refs = refs[7 : 7 + count], refs[7 + count :]
    wholes, refs = refs[:count], refs[count:]
    xhat, normed, pos, qu, qv, keys, values, relative = refs[:8]
    local, sent, came, left = refs[8:]
    moved = Gathering(
        [(shards[n], 0, shards[n].shape[0], wholes[n], shards[n].shape[0]) for n in range(count - 1)]
        + [
            (shards[-1], p * shards[-1].shape[0] // INNER_PIECES, shards[-1].shape[0] // INNER_PIECES)
            + (wholes[-1], shards[-1].shape[0])
            for p in range(INNER_PIECES)
        ],
        local,
        sent,
        came,
    )
    moved.greet()
    posload = pltpu.make_async_copy(pos_ref, pos, local.at[count - 1 + INNER_PIECES])
    stores = []

    def leave(src, dst):
        copy = pltpu.make_async_copy(src, dst, left.at[len(stores)])
        copy.start()
        stores.append(copy)

    def complete(n):
        moved.complete(n)
        if n < count - 1:
            leave(wholes[n], weights_out[n])

    def comm(*steps):
        for kind, n in steps:
            {"b": moved.begin, "o": moved.onward, "l": moved.last, "c": complete}[kind](n)

    comm(("b", 0), ("b", 1), ("b", 2))
    posload.start()
    per = rows_in[0].shape[0]
    for b in range(3):
        source = rows_in[b]

        def normalize(at, b=b, source=source):
            rows = source[at, :].astype(f32)
            centered = rows - jnp.mean(rows, axis=-1, keepdims=True)
            spread = lax.rsqrt(jnp.mean(centered * centered, axis=-1, keepdims=True) + EPSILON)
            xhat[b, at, :] = centered * spread

        tile_loop(per, 64, normalize)
        if b == 1:
            comm(("o", 0))
    leave(xhat.at[2], xhat_out)
    comm(("o", 1), ("b", 3), ("l", 0), ("c", 0))

    def row_of(k):
        height = shards[0].shape[0]
        return jnp.concatenate(
            [wholes[0][d * height : (d + 1) * height, :].astype(f32)[k : k + 1, :] for d in range(8)], axis=1
        )

    gain, shift, content, posbias = (row_of(k) for k in range(4))
    for b in range(3):

        def scale(at, b=b):
            normed[b, at, :] = (xhat[b, at, :] * gain + shift).astype(bf16)

        tile_loop(per, 64, scale)
    leave(normed, normed_out)
    comm(("o", 2), ("b", 4), ("l", 1), ("b", 5), ("c", 1))

    def project(src, weight, dst, steps):
        for b in range(3):

            def one(at, b=b):
                dst[b, at, :] = jnp.dot(
                    src[b, at, :], weight[...], preferred_element_type=f32
                ).astype(bf16)

            tile_loop(per, 256, one)
            comm(*steps[b])

    project(normed, wholes[1], keys, ((("o", 3), ("b", 6)), (("l", 2),), ()))
    leave(keys, keys_out)
    comm(("c", 2), ("o", 4), ("b", 7), ("l", 3))
    project(normed, wholes[2], values, ((), (("o", 5), ("b", 8)), (("l", 4),)))
    leave(values, values_out)
    comm(("c", 3))

    def queries(at):
        query = jnp.dot(normed[2, at, :], wholes[3][...], preferred_element_type=f32)
        qu[at, :] = (query + content).astype(bf16)
        qv[at, :] = (query + posbias).astype(bf16)

    tile_loop(per, 256, queries)
    leave(qu, qu_out)
    leave(qv, qv_out)
    comm(("o", 6), ("b", 9), ("l", 5), ("c", 4))
    posload.wait()
    project(pos, wholes[4], relative, ((("o", 7),), (("l", 6),), (("o", 8),)))
    leave(relative, relative_out)
    comm(("c", 5), ("l", 7), ("o", 9), ("l", 8), ("l", 9))
    for n in range(6, 10):
        complete(n)
    leave(wholes[-1], weights_out[-1])
    moved.drain()
    for copy in stores:
        copy.wait()


def head_stage(rows_in, shards, pos_low):
    per, width = rows_in[0].shape
    three = (3, per, width)
    count = len(shards)
    full = [(8 * w.shape[0], w.shape[1]) for w in shards]
    any_spec = pl.BlockSpec(memory_space=pl.ANY)
    shape = jax.ShapeDtypeStruct
    shapes = [shape((per, width), f32), shape(three, bf16)] + [shape((per, width), bf16)] * 2
    shapes += [shape(three, bf16)] * 3 + [shape(s, bf16) for s in full]
    vmem = pltpu.VMEM
    scratch = [vmem(s, bf16) for s in full] + [vmem(three, f32), vmem(three, bf16), vmem(three, bf16)]
    scratch += [vmem((per, width), bf16)] * 2 + [vmem(three, bf16)] * 3
    scratch += [pltpu.SemaphoreType.DMA((n,)) for n in (count + INNER_PIECES, 7 * (count + 3), 7 * (count + 3), 7 + count)]
    return pl.pallas_call(
        head_kernel,
        in_specs=[pl.BlockSpec(memory_space=pltpu.VMEM)] * 3 + [any_spec] * (count + 1),
        out_specs=[any_spec] * len(shapes),
        out_shape=shapes,
        scratch_shapes=scratch,
        compiler_params=pltpu.CompilerParams(
            collective_id=2, has_side_effects=True, vmem_limit_bytes=56 << 20
        ),
        name="head_stage",
    )(*rows_in, *shards, pos_low.reshape(three))


def gather(shards):
    return [lax.all_gather(w, "fsdp", axis=0, tiled=True) for w in shards]


def reduce(grads, share):
    done = []
    for g in grads:
        part = lax.psum_scatter(g, "fsdp", scatter_dimension=0, tiled=True)
        done.append(lax.psum(part, "dp").astype(f32) * share)
    return done


def pack_vectors(vectors, parts):
    flat = jnp.concatenate([v.reshape(parts, -1) for v in vectors], axis=1)
    width = 1024
    lines = 32 * (-(-flat.shape[1] // (32 * width)))
    flat = jnp.pad(flat, ((0, 0), (0, lines * width - flat.shape[1])))
    return flat.reshape(parts * lines, width)


def unpack_vectors(table, parts, sizes):
    flat = table.reshape(parts, -1)
    result, start = [], 0
    for size in sizes:
        result.append(flat[:, start : start + size].reshape(parts * size))
        start += size
    return result


def per_device_plain(
    tokens,
    memory,
    compressed,
    mem_fill,
    cmem_fill,
    pad_mask,
    first_gain,
    first_shift,
    query_weight,
    key_weight,
    value_weight,
    position_weight,
    content_bias,
    position_bias,
    output_weight,
    second_gain,
    second_shift,
    inner_weight,
    inner_bias,
    outer_weight,
    outer_bias,
    conv_weight,
    conv_bias,
    out_grad,
    comp_grad,
):
    streams, seg_rows, width = tokens.shape
    mem_rows = memory.shape[1]
    cmem_rows = compressed.shape[1]
    total = cmem_rows + mem_rows + seg_rows
    shards = lax.axis_size("fsdp")
    share = 1.0 / (streams * lax.axis_size("dp") * shards)
    vectors = (
        first_gain,
        first_shift,
        content_bias,
        position_bias,
        second_gain,
        second_shift,
        inner_bias,
        outer_bias,
        conv_bias,
    )
    sizes = [v.shape[0] for v in vectors]

    groups = mem_rows // RATE
    start = mem_rows - RATE * groups
    mem_valid = (
        jnp.arange(mem_rows, dtype=jnp.int32)[None, :] >= (mem_rows - mem_fill)[:, None]
    ).astype(bf16)
    taps = (memory * mem_valid[..., None])[:, start:, :].reshape(streams * groups, RATE * width)
    group_valid = (
        (start + RATE * jnp.arange(groups, dtype=jnp.int32) + RATE - 1)[None, :]
        >= (mem_rows - mem_fill)[:, None]
    ).reshape(streams * groups, 1)
    made_grad = comp_grad.reshape(streams * groups, width) * group_valid.astype(bf16)
    conv_grad = jnp.einsum("nk,nd->kd", taps, made_grad, preferred_element_type=f32).astype(bf16)
    conv_bias_grad = jnp.sum(made_grad.astype(f32), axis=0)

    query_w, key_w, value_w, table = gather(
        [query_weight, key_weight, value_weight, pack_vectors(vectors, 1)]
    )
    (gain_one, shift_one, content_b, position_b, gain_two, shift_two, inner_b, outer_b, conv_b) = (
        unpack_vectors(table, shards, sizes)
    )
    position_w, output_w = gather([position_weight, output_weight])
    (inner_w,) = gather([inner_weight])
    (outer_w,) = gather([outer_weight])
    (conv_w,) = gather([conv_weight])

    whole = jnp.concatenate([compressed[0], memory[0], tokens[0]], axis=0).astype(f32)
    normed, scaled_one, spread_one = norm_parts(whole, gain_one, shift_one)
    normed_low = normed.astype(bf16)
    own_rows = normed_low[total - seg_rows :]
    query = jnp.dot(own_rows, query_w, preferred_element_type=f32)
    query_u = (query + content_b.astype(f32)).astype(bf16)
    query_v = (query + position_b.astype(f32)).astype(bf16)
    keys = jnp.dot(normed_low, key_w, preferred_element_type=f32).astype(bf16)
    values = jnp.dot(normed_low, value_w, preferred_element_type=f32).astype(bf16)
    pos_low = positions(total, width).astype(bf16)
    relative = jnp.dot(pos_low, position_w, preferred_element_type=f32).astype(bf16)
    valid = jnp.concatenate(
        [
            jnp.arange(cmem_rows, dtype=jnp.int32) >= cmem_rows - cmem_fill[0],
            jnp.arange(mem_rows, dtype=jnp.int32) >= mem_rows - mem_fill[0],
            pad_mask[0] == 1,
        ]
    )
    bias = jnp.where(valid, 0.0, NEG).astype(f32)[None]
    mixed, prob_low = attn_fwd(query_u, query_v, keys, values, relative, bias)
    hidden = tokens[0].astype(f32) + jnp.dot(mixed, output_w, preferred_element_type=f32)
    inner_norm, scaled_two, spread_two = norm_parts(hidden, gain_two, shift_two)
    inner_low = inner_norm.astype(bf16)
    preact = jnp.dot(inner_low, inner_w, preferred_element_type=f32) + inner_b.astype(f32)
    active = smooth_gate(preact).astype(bf16)
    result = (
        hidden
        + jnp.dot(active, outer_w, preferred_element_type=f32)
        + outer_b.astype(f32)
    )
    made = (
        jnp.dot(taps, conv_w, preferred_element_type=f32) + conv_b.astype(f32)
    ) * group_valid.astype(f32)

    grad = out_grad[0]
    grad_wide = grad.astype(f32)
    outer_grad = jnp.einsum("sf,sd->fd", active, grad, preferred_element_type=f32).astype(bf16)
    (outer_mean,) = reduce([outer_grad], share)
    outer_bias_grad = jnp.sum(grad_wide, axis=0)
    active_grad = jnp.einsum("sd,fd->sf", grad, outer_w, preferred_element_type=f32)
    gate_pull = jax.vjp(smooth_gate, preact)[1]
    preact_grad = gate_pull(active_grad)[0].astype(bf16)
    inner_grad = jnp.einsum("sd,sf->df", inner_low, preact_grad, preferred_element_type=f32).astype(
        bf16
    )
    (inner_mean,) = reduce([inner_grad], share)
    (conv_mean,) = reduce([conv_grad], share)
    inner_bias_grad = jnp.sum(preact_grad.astype(f32), axis=0)
    inner_norm_grad = jnp.einsum("sf,df->sd", preact_grad, inner_w, preferred_element_type=f32)
    second_gain_grad = jnp.sum(inner_norm_grad * scaled_two, axis=0)
    second_shift_grad = jnp.sum(inner_norm_grad, axis=0)
    hidden_grad = grad_wide + norm_back(inner_norm_grad, scaled_two, spread_two, gain_two)

    hidden_low = hidden_grad.astype(bf16)
    output_grad = jnp.einsum("sd,se->de", mixed, hidden_low, preferred_element_type=f32).astype(bf16)
    mixed_grad = jnp.einsum("se,de->sd", hidden_low, output_w, preferred_element_type=f32).astype(
        bf16
    )
    query_low, keys_t, values_t, relative_t, sums = attn_bwd(
        query_u, query_v, keys, values, relative, prob_low, mixed_grad
    )
    position_grad = jnp.einsum("ld,el->de", pos_low, relative_t, preferred_element_type=f32).astype(
        bf16
    )
    query_grad = jnp.einsum("sd,se->de", own_rows, query_low, preferred_element_type=f32).astype(
        bf16
    )
    key_grad = jnp.einsum("sd,es->de", normed_low, keys_t, preferred_element_type=f32).astype(bf16)
    value_grad = jnp.einsum("sd,es->de", normed_low, values_t, preferred_element_type=f32).astype(
        bf16
    )
    normed_grad = jnp.einsum("es,de->sd", keys_t, key_w, preferred_element_type=f32)
    normed_grad = normed_grad + jnp.einsum(
        "es,de->sd", values_t, value_w, preferred_element_type=f32
    )
    own_grad = jnp.einsum("se,de->sd", query_low, query_w, preferred_element_type=f32)
    normed_grad = normed_grad + jnp.pad(own_grad, ((total - seg_rows, 0), (0, 0)))
    first_gain_grad = jnp.sum(normed_grad * scaled_one, axis=0)
    first_shift_grad = jnp.sum(normed_grad, axis=0)
    own = slice(total - seg_rows, None)
    token_gradient = hidden_grad + norm_back(
        normed_grad[own], scaled_one[own], spread_one[own], gain_one
    )
    vector_grads = (
        first_gain_grad,
        first_shift_grad,
        sums[0],
        sums[1],
        second_gain_grad,
        second_shift_grad,
        inner_bias_grad,
        outer_bias_grad,
        conv_bias_grad,
    )
    packed = pack_vectors([v.astype(bf16) for v in vector_grads], shards)
    (output_mean,) = reduce([output_grad], share)
    query_mean, key_mean, value_mean, position_mean, table_mean = reduce(
        [query_grad, key_grad, value_grad, position_grad, packed], share
    )
    (
        first_gain_mean,
        first_shift_mean,
        content_mean,
        posbias_mean,
        second_gain_mean,
        second_shift_mean,
        inner_bias_mean,
        outer_bias_mean,
        conv_bias_mean,
    ) = unpack_vectors(table_mean, 1, sizes)
    return (
        result.astype(bf16)[None],
        token_gradient[None],
        made.astype(bf16)[None],
        first_gain_mean,
        first_shift_mean,
        query_mean,
        key_mean,
        value_mean,
        position_mean,
        content_mean,
        posbias_mean,
        output_mean,
        second_gain_mean,
        second_shift_mean,
        inner_mean,
        inner_bias_mean,
        outer_mean,
        outer_bias_mean,
        conv_mean,
        conv_bias_mean,
    )


def per_device_direct(
    tokens,
    memory,
    compressed,
    mem_fill,
    cmem_fill,
    pad_mask,
    first_gain,
    first_shift,
    query_weight,
    key_weight,
    value_weight,
    position_weight,
    content_bias,
    position_bias,
    output_weight,
    second_gain,
    second_shift,
    inner_weight,
    inner_bias,
    outer_weight,
    outer_bias,
    conv_weight,
    conv_bias,
    out_grad,
    comp_grad,
):
    streams, seg_rows, width = tokens.shape
    mem_rows = memory.shape[1]
    cmem_rows = compressed.shape[1]
    total = cmem_rows + mem_rows + seg_rows
    old = total - seg_rows
    shards = lax.axis_size("fsdp")
    share = 1.0 / (streams * lax.axis_size("dp") * shards)
    lanes = 128
    vectors = (
        first_gain,
        first_shift,
        content_bias,
        position_bias,
        second_gain,
        second_shift,
        outer_bias,
        conv_bias,
        inner_bias,
    )
    sizes = [v.shape[0] for v in vectors]
    lines = [v.reshape(-1, lanes) for v in vectors]
    table = jnp.zeros((32, lanes), bf16)
    row, line = jnp.arange(32, dtype=jnp.int32)[:, None], 0
    for v in lines:
        for n in range(v.shape[0]):
            table = jnp.where(row == line, v[n][None], table)
            line += 1
    pos_low = positions_low(total, width)
    (
        scaled_one,
        normed_low,
        query_u,
        query_v,
        keys,
        values,
        relative,
        table,
        key_w,
        value_w,
        query_w,
        position_w,
        output_w,
        inner_w,
    ) = head_stage(
        (compressed[0], memory[0], tokens[0]),
        (table, key_weight, value_weight, query_weight, position_weight, output_weight, inner_weight),
        pos_low,
    )
    normed_low, keys, values, relative = (
        v.reshape(total, width) for v in (normed_low, keys, values, relative)
    )
    own_rows = normed_low[old:]
    blocks = table.reshape(shards, 32, lanes)
    gain_one, shift_one = blocks[:, 0].reshape(width), blocks[:, 1].reshape(width)
    gain_two, shift_two, outer_b, conv_b = (blocks[:, n].reshape(width) for n in (4, 5, 6, 7))
    inner_b = blocks[:, 8 : 8 + sizes[-1] // lanes].reshape(shards * sizes[-1])

    valid = jnp.concatenate(
        [
            jnp.arange(cmem_rows, dtype=jnp.int32) >= cmem_rows - cmem_fill[0],
            jnp.arange(mem_rows, dtype=jnp.int32) >= mem_rows - mem_fill[0],
            pad_mask[0] == 1,
        ]
    )
    bias = jnp.where(valid, 0.0, NEG).astype(f32)[None]
    groups = mem_rows // RATE
    start = mem_rows - RATE * groups
    mem_valid = (jnp.arange(mem_rows, dtype=jnp.int32) >= mem_rows - mem_fill[0]).astype(bf16)
    taps = (memory[0] * mem_valid[:, None])[start:, :].reshape(groups, RATE * width)
    group_valid = (
        start + RATE * jnp.arange(groups, dtype=jnp.int32) + RATE - 1 >= mem_rows - mem_fill[0]
    )[:, None]
    made_grad = comp_grad[0] * group_valid.astype(bf16)
    conv_grad = jnp.einsum("nk,nd->kd", taps, made_grad, preferred_element_type=f32).astype(bf16)
    conv_bias_grad = jnp.sum(made_grad.astype(f32), axis=0)

    conv_grad, taps, query_u = cut(conv_grad, taps, query_u)
    outer_weight, query_u = cut(outer_weight, query_u)
    outer_w = lax.all_gather(outer_weight, "fsdp", axis=0, tiled=True)
    mixed, prob_low = attn_fwd(query_u, query_v, keys, values, relative, bias)
    hidden = tokens[0].astype(f32) + jnp.dot(mixed, output_w, preferred_element_type=f32)
    inner_norm, scaled_two, spread_two = norm_parts(hidden, gain_two, shift_two)
    inner_low = inner_norm.astype(bf16)
    preact = jnp.dot(inner_low, inner_w, preferred_element_type=f32) + inner_b.astype(f32)
    active = smooth_gate(preact).astype(bf16)
    grad = out_grad[0]
    grad_wide = grad.astype(f32)
    active, preact = cut(active, preact)
    outer_grad = jnp.einsum("sf,sd->fd", active, grad, preferred_element_type=f32).astype(bf16)
    outer_bias_grad = jnp.sum(grad_wide, axis=0)

    outer_w, outer_grad, conv_grad = cut(outer_w, outer_grad, conv_grad)
    conv_part = lax.psum_scatter(conv_grad, "fsdp", scatter_dimension=0, tiled=True)
    outer_part = lax.psum_scatter(outer_grad, "fsdp", scatter_dimension=0, tiled=True)
    active_grad = jnp.einsum("sd,fd->sf", grad, outer_w, preferred_element_type=f32)
    gate_pull = jax.vjp(smooth_gate, preact)[1]
    preact_grad = gate_pull(active_grad)[0].astype(bf16)
    inner_bias_grad = jnp.sum(preact_grad.astype(f32), axis=0)
    inner_grad = jnp.einsum("sd,sf->df", inner_low, preact_grad, preferred_element_type=f32).astype(
        bf16
    )
    inner_norm_grad = jnp.einsum("sf,df->sd", preact_grad, inner_w, preferred_element_type=f32)
    second_gain_grad = jnp.sum(inner_norm_grad * scaled_two, axis=0)
    second_shift_grad = jnp.sum(inner_norm_grad, axis=0)
    hidden_grad = grad_wide + norm_back(inner_norm_grad, scaled_two, spread_two, gain_two)
    hidden_low = hidden_grad.astype(bf16)
    mixed_grad = jnp.einsum("se,de->sd", hidden_low, output_w, preferred_element_type=f32).astype(
        bf16
    )
    query_g, keys_g, values_g, relative_g, sums = attn_bwd(
        query_u, query_v, keys, values, relative, prob_low, mixed_grad
    )
    conv_part, query_g, conv_weight = cut(conv_part, query_g, conv_weight)
    conv_end = inward_hop(conv_part)
    conv_w = lax.all_gather(conv_weight, "fsdp", axis=0, tiled=True)
    key_grad = jnp.einsum("sd,es->de", normed_low, keys_g, preferred_element_type=f32).astype(bf16)
    value_grad = jnp.einsum("sd,es->de", normed_low, values_g, preferred_element_type=f32).astype(bf16)
    position_grad = jnp.einsum("ld,el->de", pos_low, relative_g, preferred_element_type=f32).astype(
        bf16
    )
    key_grad, value_grad, position_grad, conv_end, query_g = cut(
        key_grad, value_grad, position_grad, conv_end, query_g
    )
    conv_pair = add(conv_part, conv_end)
    conv_mid = middle_hop(conv_pair)
    query_grad = jnp.einsum("sd,se->de", own_rows, query_g, preferred_element_type=f32).astype(bf16)
    columns = (
        (query_w, jnp.sum(query_g.astype(f32), axis=0)),
        (key_w, jnp.sum(keys_g.astype(f32), axis=1)),
        (value_w, jnp.sum(values_g.astype(f32), axis=1)),
    )
    first_shift_grad = sum(jnp.sum(w.astype(f32) * column[None, :], axis=1) for w, column in columns)
    own_grad = jnp.einsum("se,de->sd", query_g, query_w, preferred_element_type=f32)
    own_grad = own_grad + jnp.einsum(
        "es,de->sd", keys_g[:, old:], key_w, preferred_element_type=f32
    )
    own_grad = own_grad + jnp.einsum(
        "es,de->sd", values_g[:, old:], value_w, preferred_element_type=f32
    )
    inner = own_grad * gain_one.astype(f32)
    own = tokens[0].astype(f32)
    spread_own = lax.rsqrt(
        jnp.mean((own - jnp.mean(own, axis=-1, keepdims=True)) ** 2, axis=-1, keepdims=True) + EPSILON
    )
    token_gradient = hidden_grad + spread_own * (
        inner
        - jnp.mean(inner, axis=-1, keepdims=True)
        - scaled_one * jnp.mean(inner * scaled_one, axis=-1, keepdims=True)
    )
    conv_mid, own_grad, active, hidden_low = cut(conv_mid, own_grad, active, hidden_low)
    conv_sum = add(conv_pair, conv_mid)
    conv_last = outward_hop(conv_sum)
    output_grad = jnp.einsum("sd,se->de", mixed, hidden_low, preferred_element_type=f32).astype(bf16)
    vector_grads = (
        first_shift_grad,
        sums[0],
        sums[1],
        second_gain_grad,
        second_shift_grad,
        outer_bias_grad,
        conv_bias_grad,
        inner_bias_grad,
    )
    packed = jnp.concatenate([v.reshape(shards, -1, lanes) for v in vector_grads], axis=1)
    packed = jnp.pad(packed, ((0, 0), (0, 32 - packed.shape[1]), (0, 0))).astype(bf16)
    result = (
        hidden + jnp.dot(active, outer_w, preferred_element_type=f32) + outer_b.astype(f32)
    ).astype(bf16)
    made = (
        (jnp.dot(taps, conv_w, preferred_element_type=f32) + conv_b.astype(f32))
        * group_valid.astype(f32)
    ).astype(bf16)
    (
        output_mean,
        query_mean,
        key_mean,
        value_mean,
        position_mean,
        inner_mean,
        table_mean,
        outer_mean,
    ) = reduce_tail(
        [(g, 2) for g in (output_grad, query_grad, key_grad, value_grad, position_grad)]
        + [(inner_grad, 4)]
        + [(packed.reshape(shards * 32, lanes), 1)],
        [(outer_part, 4)],
        share,
        1,
    )
    conv_last, query_mean = cut(conv_last, query_mean)
    conv_mean = finish(conv_sum, conv_last, share)
    (
        first_shift_mean,
        content_mean,
        posbias_mean,
        second_gain_mean,
        second_shift_mean,
        outer_bias_mean,
        conv_bias_mean,
    ) = (table_mean[n] for n in range(7))
    inner_bias_mean = table_mean[7 : 7 + sizes[-1] // lanes].reshape(sizes[-1])
    with_normed = sum(
        jnp.sum(w.astype(f32) * mean, axis=1)
        for w, mean in ((query_weight, query_mean), (key_weight, key_mean), (value_weight, value_mean))
    )
    first_gain_mean = (with_normed - first_shift.astype(f32) * first_shift_mean) / first_gain.astype(f32)
    return (
        result[None],
        token_gradient[None],
        made[None],
        first_gain_mean,
        first_shift_mean,
        query_mean,
        key_mean,
        value_mean,
        position_mean,
        content_mean,
        posbias_mean,
        output_mean,
        second_gain_mean,
        second_shift_mean,
        inner_mean,
        inner_bias_mean,
        outer_mean,
        outer_bias_mean,
        conv_mean,
        conv_bias_mean,
    )


def per_device(*arguments):
    if lax.axis_size("dp") == 4 and lax.axis_size("fsdp") == 8:
        return per_device_direct(*arguments)
    return per_device_plain(*arguments)


def solution(mesh):
    in_specs = (
        P(("dp", "fsdp"), None, None),
        P(("dp", "fsdp"), None, None),
        P(("dp", "fsdp"), None, None),
        P(("dp", "fsdp")),
        P(("dp", "fsdp")),
        P(("dp", "fsdp"), None),
        P("fsdp"),
        P("fsdp"),
        P("fsdp", None),
        P("fsdp", None),
        P("fsdp", None),
        P("fsdp", None),
        P("fsdp"),
        P("fsdp"),
        P("fsdp", None),
        P("fsdp"),
        P("fsdp"),
        P("fsdp", None),
        P("fsdp"),
        P("fsdp", None),
        P("fsdp"),
        P("fsdp", None),
        P("fsdp"),
        P(("dp", "fsdp"), None, None),
        P(("dp", "fsdp"), None, None),
    )
    out_specs = (
        P(("dp", "fsdp"), None, None),
        P(("dp", "fsdp"), None, None),
        P(("dp", "fsdp"), None, None),
        P("fsdp"),
        P("fsdp"),
        P("fsdp", None),
        P("fsdp", None),
        P("fsdp", None),
        P("fsdp", None),
        P("fsdp"),
        P("fsdp"),
        P("fsdp", None),
        P("fsdp"),
        P("fsdp"),
        P("fsdp", None),
        P("fsdp"),
        P("fsdp", None),
        P("fsdp"),
        P("fsdp", None),
        P("fsdp"),
    )
    return jax.shard_map(
        per_device, mesh=mesh, in_specs=in_specs, out_specs=out_specs, check_vma=False
    )
```

time: 563 us -> 475 us (0.84)
  local copies, waits for them, and re-layouts: 95.3 us -> 16.2 us
  Pallas kernels: 210 us -> 277 us
  waiting for transfers between devices: 53.7 us -> 16.5 us
  starting transfers between devices: 21.9 us -> 6.64 us
  other arithmetic: 48.8 us -> 36.7 us
  matrix products: 107 us -> 97.7 us
    unnamed x250 -> x108, local copies, waits for them, and re-layouts: 81.1 us -> 6.21 us
    pallas_call x10 -> x4, Pallas kernels: 210 us -> 277 us  [the longest x1 137 us: reduce_tail(): pl.pallas_call(functools.partial(tail_kernel, plan, sources, len(arrays))...]
    dot_general x6 -> x2, matrix products: 29.7 us -> 5.23 us  [the longest x1 2.62 us: per_device_direct(): jnp.einsum('es,de->sd', keys_g[:, old:], key_w, preferred_element_type=f32)]
    reduce_scatter x1, waiting for transfers between devices: 21.7 us -> 0.01 us  [per_device_direct(): lax.psum_scatter(outer_grad, 'fsdp', scatter_dimension=0, tiled=True)]
    ppermute x35 -> x3, waiting for transfers between devices: 31.9 us -> 12.1 us  [hop(): return lax.ppermute(value, ('dp', 'fsdp'), pairs)]
    ppermute x35 -> x3, starting transfers between devices: 21.7 us -> 6.02 us  [hop(): return lax.ppermute(value, ('dp', 'fsdp'), pairs)]
    another operation x3 -> x1, other arithmetic: 11.9 us -> 0.92 us
    dot_general x1, matrix products: 4.55 us -> 14.7 us  [per_device_direct(): jnp.einsum('sd,fd->sf', grad, outer_w, preferred_element_type=f32)]
  transfers between devices with their start and end apart: 38 -> 7, of which waited for: 9 -> 2; matrix products, arithmetic and copies ran while one was open for 31% -> 27% of each run, Pallas kernels for 16% -> 44%
where the time goes in v3:
time: 475 us; the launch traced here: 467 us
  Pallas kernels  277 us (58%)
  matrix products  97.7 us (21%)
  other arithmetic  36.7 us (8%)
  waiting for transfers between devices  16.5 us (3%)
  local copies, waits for them, and re-layouts  16.2 us (3%)
  between operations  16 us (3%)
  starting transfers between devices  6.64 us (1%)
    pallas_call x1, Pallas kernels, reduce_tail(): pl.pallas_call(functools.partial(tail_kernel, plan, sources, len(arrays))...  137 us
    pallas_call x1, Pallas kernels, head_stage(): pl.pallas_call(head_kernel, in_specs=[pl.BlockSpec(memory_space=pltpu.VME...  71.1 us
    pallas_call x1, Pallas kernels, attn_bwd(): pl.pallas_call(attn_bwd_kernel, grid=(HEADS,), in_specs=in_specs, out_spe...  42.5 us
    pallas_call x1, Pallas kernels, attn_fwd(): pl.pallas_call(attn_fwd_kernel, grid=(HEADS,), in_specs=in_specs, out_spe...  26.3 us
    dot_general x1, matrix products, per_device_direct(): jnp.einsum('sd,fd->sf', grad, outer_w, preferred_element_type=f32)  14.7 us
    ppermute x3, waiting for transfers between devices, hop(): return lax.ppermute(value, ('dp', 'fsdp'), pairs)  12.1 us
    dot_general x1, matrix products, per_device_direct(): jnp.einsum('sd,sf->df', inner_low, preact_grad, preferred_element_type=f32)  9.7 us
  transfers between devices with their start and end apart: 7, of which 2 were waited for; matrix products, arithmetic and copies ran while one was open for 27% of the time, Pallas kernels for 44%

profile of v3, /device:TPU:0, one launch (start us, length us, event | category | flops | bytes accessed | tf_op | source)
XLA Modules:
  0.0 467.1 jit_solution(6826284467933678417)
XLA Ops:
  8.0 1.0 multiply_sine_fusion
  10.4 1.6 slice_multiply_fusion
  12.5 4.5 convolution_convert_fusion.2
  17.0 2.6 add_convert_fusion
  20.4 71.1 %head_stage.1 = (f32[512,1024]{1,0:T(8,128)}, bf16[3,512,1024]{2,1,0:T(8,128)(2,1)}, bf16[512,1024]{1,0:T(8,128)(2,1)}, bf16[512,1024]{1,0:T(8,128)(2,1)}, bf16[...) custom-call(bf16[512,1024]{1,0:T(8,128)(2,1)} %bitcast.144, ...), custom_call_target="tpu_custom_call" | custom-call | tf_op jit(solution)/shard_map/head_stage/pallas_call | solution.py:838
  94.0 26.3 %attn_fwd.1 = (bf16[512,1024]{1,0:T(8,128)(2,1)}, bf16[8,512,1536]{2,1,0:T(8,128)(2,1)}) custom-call(bf16[512,1024]{1,0:T(8,128)(2,1)} %get-tuple-element.81.qu_ref, bf16[512,1024]{1,0:T(8,128)(2,1)} %get-tuple-element.82.qv_ref, bf16[1536,1024]{1,0:T(8,128)(2,1)} %bitcast.172, bf16[1536,1024]{1,0:T(8,128)(2,1)} %bitcast.174, bf16[1536,1024]{1,0:T(8,128)(2,1)} %bitcast.176, ...), custom_call_target="tpu_custom_call" | custom-call | flops 4831838208 | bytes 25165824 | tf_op jit(solution)/shard_map/attn_fwd/pallas_call | solution.py:138
  120.4 3.0 fusion.48
  124.7 9.1 %fusion.14 = (bf16[512,4096]{1,0:T(8,128)(2,1)S(1)}, f32[512,4096]{1,0:T(8,128)}) fusion(f32[4096]{0:T(1024)S(1)} %convert.50, bf16[1024,4096]{1,0:T(8,128)(2,1)S(1)} %copy-done.43, f32[512,1024]{1,0:T(8,128)S(1)} %get-tuple-element.166, f32[1024]{0:T(1024)S(1)} %bitcast.164, f32[1024]{0:T(1024)S(1)} %bitcast.153, f32[512]{0:T(512)S(1)} %add_rsqrt_fusion.1, ...), kind=kOutput, calls=%fused_computation.17 | convolution fusion | flops 4318560256 | bytes 23097344 | tf_op jit(solution)/shard_map/dot_general | solution.py:1195
  133.8 2.0 copy-done.48
  135.8 6.8 %convolution_convert_fusion.1 = bf16[4096,1024]{1,0:T(8,128)(2,1)} fusion(bf16[512,4096]{1,0:T(8,128)(2,1)S(1)} %get-tuple-element.109, bf16[1,512,1024]{2,1,0:T(8,128)(2,1)S(1)} %copy-done.9), kind=kOutput, calls=%fused_computation.24 | convolution fusion | flops 4299161600 | bytes 13631488 | tf_op jit(solution)/shard_map/sf,sd->fd/dot_general | solution.py:1200
  142.7 3.7 all-gather.3.cloned.1.call-done
  147.1 2.3 copy.49
  149.4 2.3 copy.50
  151.9 1.4 reduce
  154.5 14.7 %fusion.49 = (bf16[4096]{0:T(1024)(128)(2,1)S(1)}, bf16[512,4096]{1,0:T(8,128)(2,1)S(1)}) fusion(f32[512,4096]{1,0:T(8,128)} %get-tuple-element.96, bf16[4096,1024]{1,0:T(8,128)(2,1)} %all-gather.3.cloned.1.call-done, bf16[1,512,1024]{2,1,0:T(8,128)(2,1)S(1)} %copy-done.10), kind=kOutput, calls=%fused_computation.155 | convolution fusion | flops 4339003392 | bytes 22028288 | tf_op jit(solution)/shard_map/sd,fd->sf/dot_general | solution.py:1206
  169.2 5.1 %multiply_reduce_fusion.3 = (bf16[1024]{0:T(1024)(128)(2,1)S(1)}, f32[512]{0:T(512)S(1)}, f32[512]{0:T(512)S(1)}, bf16[1024]{0:T(1024)(128)(2,1)S(1)}, f32[512,1024]{1,0:T(8,128)S(1)}) fusion(f32[512,1024]{1,0:T(8,128)S(1)} %get-tuple-element.166, f32[512]{0:T(512)S(1)} %add_rsqrt_fusion.1, f32[512]{0:T(512)S(1)} %broadcast_multiply_fusion.5, ...), kind=kOutput, calls=%fused_computation.40 | convolution fusion | flops 4299682816 | bytes 16793600 | tf_op jit(solution)/shard_map/sf,df->sd/dot_general | solution.py:1213
  174.3 2.1 fusion.46
  176.5 1.0 copy-done.20
  177.4 1.3 convolution_convert_fusion.8
  178.7 1.3 copy.52.g_ref
  180.1 42.5 %attn_bwd.1 = (bf16[512,1024]{1,0:T(8,128)(2,1)}, bf16[1024,1536]{1,0:T(8,128)(2,1)}, bf16[1024,1536]{1,0:T(8,128)(2,1)}, bf16[1024,1536]{1,0:T(8,128)(2,1)}, f32[8,1024]{1,0:T(8,128)}) custom-call(bf16[512,1024]{1,0:T(8,128)(2,1)} %get-tuple-element.81.qu_ref, bf16[512,1024]{1,0:T(8,128)(2,1)} %get-tuple-element.82.qv_ref, bf16[1024,512]{1,0:T(8,128)(2,1)} %bitcast.145, ...), custom_call_target="tpu_custom_call" | custom-call | flops 12884901888 | bytes 36700160 | tf_op jit(solution)/shard_map/attn_bwd/pallas_call | solution.py:249
  223.5 3.3 convert_reduce_fusion.1
  228.4 1.0 copy-done.16
  230.7 2.6 fusion.31
  233.4 2.6 fusion.29
  236.0 4.7 %convolution_convert_fusion.6 = bf16[1024,1024]{1,0:T(8,128)(2,1)} fusion(bf16[1536,1024]{1,0:T(8,128)(2,1)S(1)} %bitcast.170, bf16[1024,1536]{1,0:T(8,128)(2,1)S(1)} %copy-done.13), kind=kOutput, calls=%fused_computation.54 | convolution fusion | flops 3222274048 | bytes 8388608 | tf_op jit(solution)/shard_map/sd,es->de/dot_general | solution.py:1228
  240.7 4.8 %convolution_convert_fusion.7 = bf16[1024,1024]{1,0:T(8,128)(2,1)} fusion(bf16[1536,1024]{1,0:T(8,128)(2,1)S(1)} %bitcast.171, bf16[1024,1536]{1,0:T(8,128)(2,1)S(1)} %copy-done.12), kind=kOutput, calls=%fused_computation.55 | convolution fusion | flops 3222274048 | bytes 8388608 | tf_op jit(solution)/shard_map/sd,es->de/dot_general | solution.py:1227
  245.6 9.7 %convolution_convert_fusion = bf16[1024,4096]{1,0:T(8,128)(2,1)} fusion(bf16[512,4096]{1,0:T(8,128)(2,1)} %copy-done.50, f32[512,1024]{1,0:T(8,128)S(1)} %get-tuple-element.166, f32[1024]{0:T(1024)S(1)} %bitcast.165, f32[1024]{0:T(1024)S(1)} %bitcast.156, f32[512]{0:T(512)S(1)} %add_rsqrt_fusion.1, f32[512]{0:T(512)S(1)} %broadcast_multiply_fusion.5), kind=kOutput, calls=%fused_computation.23 | convolution fusion | flops 4301783040 | bytes 14692352 | tf_op jit(solution)/shard_map/sd,sf->df/dot_general | solution.py:1210
  255.3 3.2 collective-permute-start
  258.5 5.1 %convolution_convert_fusion.5 = bf16[1024,1024]{1,0:T(8,128)(2,1)} fusion(bf16[1536,1024]{1,0:T(8,128)(2,1)S(1)} %bitcast.134, bf16[1024,1536]{1,0:T(8,128)(2,1)S(1)} %copy-done.51), kind=kOutput, calls=%fused_computation.53 | convolution fusion | flops 3222274048 | bytes 8388608 | tf_op jit(solution)/shard_map/ld,el->de/dot_general | solution.py:1229
  263.6 12.1 %collective-permute-done = bf16[384,1024]{1,0:T(8,128)(2,1)S(1)} collective-permute-done((bf16[384,1024]{1,0:T(8,128)(2,1)S(1)}, bf16[384,1024]{1,0:T(8,128)(2,1)S(1)}, u32[]{:S(2)}, u32[]{:S(2)}) %collective-permute-start) | collective-permute-done | bytes 786464 | tf_op jit(solution)/shard_map/ppermute | solution.py:306
  275.7 1.2 add_convert_fusion.4
  276.9 1.5 collective-permute-start.1
  278.7 2.9 multiply_reduce_fusion.7
  282.9 4.1 convolution_convert_fusion.3
  287.0 1.8 add_bitcast_fusion
  288.8 1.8 add_convert_fusion.3
  290.7 1.3 collective-permute-start.2
  292.0 9.3 %fusion.20 = bf16[1,512,1024]{2,1,0:T(8,128)(2,1)} fusion(f32[512,1024]{1,0:T(8,128)S(1)} %get-tuple-element.166, bf16[512,4096]{1,0:T(8,128)(2,1)S(1)} %copy-done.49, bf16[4096,1024]{1,0:T(8,128)(2,1)} %all-gather.3.cloned.1.call-done, f32[1024]{0:T(1024)S(1)} %bitcast.163), kind=kOutput, calls=%fused_computation.62 | convolution fusion | flops 4296540160 | bytes 15732736 | tf_op jit(solution)/shard_map/dot_general | solution.py:1278
  301.3 2.6 convolution_convert_fusion.4
  303.9 137.4 %reduce_tail.1 = (bf16[128,1024]{1,0:T(8,128)(2,1)}, bf16[128,1024]{1,0:T(8,128)(2,1)}, bf16[128,1024]{1,0:T(8,128)(2,1)}, bf16[128,1024]{1,0:T(8,128)(2,1)}, bf...) custom-call(bf16[8,128,1024]{2,1,0:T(8,128)(2,1)} %bitcast.143, ...), custom_call_target="tpu_custom_call" | custom-call | tf_op jit(solution)/shard_map/reduce_tail/pallas_call | solution.py:607
  441.4 1.1 convert_multiply_fusion.7
  442.7 1.0 convert_multiply_fusion.8
  444.8 1.8 multiply_reduce_fusion.10
  449.7 1.6 convert_multiply_fusion
  451.3 2.6 convert_multiply_fusion.2
  453.9 1.5 convert_multiply_fusion.1
  455.5 4.9 %fusion.23 = bf16[1,170,1024]{2,1,0:T(8,128)(2,1)} fusion(bf16[170,3072]{1,0:T(8,128)(2,1)S(1)} %copy-done.8, bf16[3072,1024]{1,0:T(8,128)(2,1)} %all-gather.5.cloned.1.call-done, f32[170]{0:T(256)S(1)} %fusion.43, f32[1024]{0:T(1024)S(1)} %bitcast.162), kind=kOutput, calls=%fused_computation.66 | convolution fusion | flops 1070069760 | bytes 7688872 | tf_op jit(solution)/shard_map/dot_general | solution.py:1281
  (180 shorter events, 18.0 us)
Async XLA Ops:
  7.2 139.1 %all-gather.3.cloned.1.call-start = ((), (), s32[]{:S(2)}) async-start(), calls=%async_computation.2 | async-start | bytes 9437184 | tf_op jit(solution)/shard_map/all_gather | solution.py:1190
  12.5 4.5 copy-start.7
  16.9 2.6 copy-start.33
  16.9 2.6 copy-start.35
  16.9 2.6 copy-start.37
  16.9 2.6 copy-start.38
  20.4 73.1 %copy-start.32 = (s32[1,512]{1,0:T(1,128)S(1)}, s32[1,512]{1,0:T(1,128)}, u32[]{:S(2)}) copy-start(s32[1,512]{1,0:T(1,128)} %param.30) | copy-start | bytes 6148
  91.5 154.0 %reduce-scatter.3.cloned.1.call-start = ((), (), s32[]{:S(2)}) async-start(), calls=%async_computation.3 | async-start | bytes 7077888 | tf_op jit(solution)/shard_map/reduce_scatter | solution.py:1204
  94.0 26.3 %copy-start.1 = (bf16[1,512,1024]{2,1,0:T(8,128)(2,1)S(1)}, bf16[1,512,1024]{2,1,0:T(8,128)(2,1)}, u32[]{:S(2)}) copy-start(bf16[1,512,1024]{2,1,0:T(8,128)(2,1)} %param.25) | copy-start | bytes 3145732
  94.0 26.3 %copy-start.45 = (bf16[1024,1024]{1,0:T(8,128)(2,1)S(1)}, bf16[1024,1024]{1,0:T(8,128)(2,1)}, u32[]{:S(2)}) copy-start(bf16[1024,1024]{1,0:T(8,128)(2,1)} %get-tuple-element.87) | copy-start | bytes 6291460
  120.4 4.4 copy-start.43
  124.7 11.1 %copy-start.9 = (bf16[1,512,1024]{2,1,0:T(8,128)(2,1)S(1)}, bf16[1,512,1024]{2,1,0:T(8,128)(2,1)}, u32[]{:S(2)}) copy-start(bf16[1,512,1024]{2,1,0:T(8,128)(2,1)} %param.48) | copy-start | bytes 3145732
  146.4 157.5 %reduce-scatter.5.cloned.1.call-start = ((), (), s32[]{:S(2)}) async-start(), calls=%async_computation.5 | async-start | bytes 9437184 | tf_op jit(solution)/shard_map/reduce_scatter | solution.py:1205
  147.1 308.4 %all-gather.5.cloned.1.call-start = ((), (), s32[]{:S(2)}) async-start(), calls=%async_computation.4 | async-start | bytes 7077888 | tf_op jit(solution)/shard_map/all_gather | solution.py:1226
  153.3 15.9 %slice-start = ((s8[8388608]{0:T(1024)(128)(4,1)}), s8[4194304]{0:T(1024)(128)(4,1)S(1)}, s32[]{:S(2)}) async-start(s8[8388608]{0:T(1024)(128)(4,1)} %bitcast.168), calls=%async_computation.6 | async-start | bytes 8388608
  154.5 14.7 %slice-start.1 = ((s8[8388608]{0:T(1024)(128)(4,1)}), s8[4194304]{0:T(1024)(128)(4,1)S(1)}, s32[]{:S(2)}) async-start(s8[8388608]{0:T(1024)(128)(4,1)} %bitcast.168), calls=%async_computation.7 | async-start | bytes 8388608
  169.2 5.1 %copy-start.50 = (bf16[512,4096]{1,0:T(8,128)(2,1)}, bf16[512,4096]{1,0:T(8,128)(2,1)S(1)}, u32[]{:S(2)}) copy-start(bf16[512,4096]{1,0:T(8,128)(2,1)S(1)} %get-tuple-element.172) | copy-start | bytes 12582916
  174.3 3.1 copy-start.46
  222.6 4.2 copy-start.17
  223.5 4.4 copy-start.13
  227.9 2.8 copy-start.12
  245.5 9.7 %copy-start.28 = (bf16[384,1024]{1,0:T(8,128)(2,1)S(1)}, bf16[384,1024]{1,0:T(8,128)(2,1)}, u32[]{:S(2)}) copy-start(bf16[384,1024]{1,0:T(8,128)(2,1)} %reduce-scatter.3.cloned.1.call-done) | copy-start | bytes 2359300
  245.6 12.9 %copy-start = (bf16[24,64,1024]{2,1,0:T(8,128)(2,1)S(1)}, bf16[24,64,1024]{2,1,0:T(8,128)(2,1)}, u32[]{:S(2)}) copy-start(bf16[24,64,1024]{2,1,0:T(8,128)(2,1)} %add_convert_fusion) | copy-start | bytes 9437188
  245.6 12.9 %copy-start.51 = (bf16[1024,1536]{1,0:T(8,128)(2,1)S(1)}, bf16[1024,1536]{1,0:T(8,128)(2,1)}, u32[]{:S(2)}) copy-start(bf16[1024,1536]{1,0:T(8,128)(2,1)} %get-tuple-element.102) | copy-start | bytes 9437188
  255.3 20.4 %collective-permute-start = (bf16[384,1024]{1,0:T(8,128)(2,1)S(1)}, bf16[384,1024]{1,0:T(8,128)(2,1)S(1)}, u32[]{:S(2)}, u32[]{:S(2)}) collective-permute-start(bf16[384,1024]{1,0:T(8,128)(2,1)S(1)} %copy-done.28), channel_id=1, source_target_pairs={{0,8},{1,9},{2,10},{3,11},{4,12},{5,13},{6,14},{7,15},{24,16},{25,... | collective-permute-start | bytes 2359304 | tf_op jit(solution)/shard_map/ppermute | solution.py:306
  258.5 20.0 %copy-start.11 = (bf16[512,1024]{1,0:T(8,128)(2,1)S(1)}, bf16[512,1024]{1,0:T(8,128)(2,1)}, u32[]{:S(2)}) copy-start(bf16[512,1024]{1,0:T(8,128)(2,1)} %get-tuple-element.105) | copy-start | bytes 3145732
  258.5 20.1 %copy-start.3 = (f32[512,1024]{1,0:T(8,128)S(1)}, f32[512,1024]{1,0:T(8,128)}, u32[]{:S(2)}) copy-start(f32[512,1024]{1,0:T(8,128)} %get-tuple-element.110) | copy-start | bytes 6291460
  258.5 20.1 %copy-start.14 = (f32[512,1024]{1,0:T(8,128)S(1)}, f32[512,1024]{1,0:T(8,128)}, u32[]{:S(2)}) copy-start(f32[512,1024]{1,0:T(8,128)} %fusion.31) | copy-start | bytes 6291460
  258.5 20.1 %copy-start.15 = (f32[512,1024]{1,0:T(8,128)S(1)}, f32[512,1024]{1,0:T(8,128)}, u32[]{:S(2)}) copy-start(f32[512,1024]{1,0:T(8,128)} %fusion.29) | copy-start | bytes 6291460
  263.6 15.0 %copy-start.2 = (bf16[1024,1024]{1,0:T(8,128)(2,1)S(1)}, bf16[1024,1024]{1,0:T(8,128)(2,1)}, u32[]{:S(2)}) copy-start(bf16[1024,1024]{1,0:T(8,128)(2,1)} %get-tuple-element.106) | copy-start | bytes 6291460
  276.9 11.9 %collective-permute-start.1 = (bf16[384,1024]{1,0:T(8,128)(2,1)}, bf16[384,1024]{1,0:T(8,128)(2,1)}, u32[]{:S(2)}, u32[]{:S(2)}) collective-permute-start(bf16[384,1024]{1,0:T(8,128)(2,1)} %add_convert_fusion.4), channel_id=1, source_target_pairs={{8,16},{9,17},{10,18},{11,19},{12,20},{13,21},{14,22},{15,23},{16,... | collective-permute-start | bytes 2359304 | tf_op jit(solution)/shard_map/ppermute | solution.py:306
  282.9 4.1 copy-start.4
  282.9 4.1 copy-start.5
  282.9 4.1 copy-start.6
  287.0 5.0 %copy-start.49 = (bf16[512,4096]{1,0:T(8,128)(2,1)S(1)}, bf16[512,4096]{1,0:T(8,128)(2,1)}, u32[]{:S(2)}) copy-start(bf16[512,4096]{1,0:T(8,128)(2,1)} %copy-done.48) | copy-start | bytes 12582916
  290.7 151.8 %collective-permute-start.2 = (bf16[384,1024]{1,0:T(8,128)(2,1)S(1)}, bf16[384,1024]{1,0:T(8,128)(2,1)}, u32[]{:S(2)}, u32[]{:S(2)}) collective-permute-start(bf16[384,1024]{1,0:T(8,128)(2,1)S(1)} %add_convert_fusion.3), channel_id=1, source_target_pairs={{8,0},{9,1},{10,2},{11,3},{12,4},{13,5},{14,6},{15,7},{16,24},{17,... | collective-permute-start | bytes 2359304 | tf_op jit(solution)/shard_map/ppermute | solution.py:306
  292.0 9.3 %copy-start.21 = (bf16[512,1024]{1,0:T(8,128)(2,1)S(1)}, bf16[512,1024]{1,0:T(8,128)(2,1)}, u32[]{:S(2)}) copy-start(bf16[512,1024]{1,0:T(8,128)(2,1)} %copy-done.20) | copy-start | bytes 3145732
  292.0 9.3 %copy-start.47 = (bf16[512,1024]{1,0:T(8,128)(2,1)S(1)}, bf16[512,1024]{1,0:T(8,128)(2,1)}, u32[]{:S(2)}) copy-start(bf16[512,1024]{1,0:T(8,128)(2,1)} %get-tuple-element.86) | copy-start | bytes 3145732
  303.9 138.6 %copy-start.25 = (bf16[128,1024]{1,0:T(8,128)(2,1)S(1)}, bf16[128,1024]{1,0:T(8,128)(2,1)}, u32[]{:S(2)}) copy-start(bf16[128,1024]{1,0:T(8,128)(2,1)} %refs_6_.1) | copy-start | bytes 786436
  303.9 140.9 %copy-start.26 = (bf16[128,1024]{1,0:T(8,128)(2,1)S(1)}, bf16[128,1024]{1,0:T(8,128)(2,1)}, u32[]{:S(2)}) copy-start(bf16[128,1024]{1,0:T(8,128)(2,1)} %refs_4_.1) | copy-start | bytes 786436
  441.3 5.3 %copy-start.27 = (bf16[128,1024]{1,0:T(8,128)(2,1)S(1)}, bf16[128,1024]{1,0:T(8,128)(2,1)}, u32[]{:S(2)}) copy-start(bf16[128,1024]{1,0:T(8,128)(2,1)} %refs_5_.1) | copy-start | bytes 786436
  441.4 5.3 %copy-start.31 = (bf16[128,1024]{1,0:T(8,128)(2,1)S(1)}, bf16[128,1024]{1,0:T(8,128)(2,1)}, u32[]{:S(2)}) copy-start(bf16[128,1024]{1,0:T(8,128)(2,1)} %get-tuple-element.123) | copy-start | bytes 786436
  441.4 6.1 %copy-start.34 = (bf16[128]{0:T(256)(128)(2,1)S(1)}, bf16[128]{0:T(256)(128)(2,1)}, u32[]{:S(2)}) copy-start(bf16[128]{0:T(256)(128)(2,1)} %param.31) | copy-start | bytes 772
  441.4 6.1 %copy-start.36 = (bf16[128]{0:T(256)(128)(2,1)S(1)}, bf16[128]{0:T(256)(128)(2,1)}, u32[]{:S(2)}) copy-start(bf16[128]{0:T(256)(128)(2,1)} %param.32) | copy-start | bytes 772
  441.4 6.6 %copy-start.30 = (bf16[128,1024]{1,0:T(8,128)(2,1)S(1)}, bf16[128,1024]{1,0:T(8,128)(2,1)}, u32[]{:S(2)}) copy-start(bf16[128,1024]{1,0:T(8,128)(2,1)} %get-tuple-element.126) | copy-start | bytes 786436
  441.4 7.5 %copy-start.29 = (bf16[128,1024]{1,0:T(8,128)(2,1)S(1)}, bf16[128,1024]{1,0:T(8,128)(2,1)}, u32[]{:S(2)}) copy-start(bf16[128,1024]{1,0:T(8,128)(2,1)} %get-tuple-element.125) | copy-start | bytes 786436
  442.5 7.2 %copy-start.18 = (f32[128,1024]{1,0:T(8,128)}, f32[128,1024]{1,0:T(8,128)S(1)}, u32[]{:S(2)}) copy-start(f32[128,1024]{1,0:T(8,128)S(1)} %convert_multiply_fusion.7) | copy-start | bytes 1572868
  442.5 7.2 %copy-start.23 = (bf16[512,1024]{1,0:T(8,128)(2,1)S(1)}, bf16[512,1024]{1,0:T(8,128)(2,1)}, u32[]{:S(2)}) copy-start(bf16[512,1024]{1,0:T(8,128)(2,1)} %get-tuple-element.128) | copy-start | bytes 3145732
  (13 other events, 27.0 us)
Sparse Core Ops, SparseCore 0:
  91.6 54.6 all-gather.2
  149.7 61.7 reduce-scatter.2
  215.3 71.2 reduce-scatter.4
  288.4 57.8 all-gather.4

commit v4 on v3

--- a/solution.py
+++ b/solution.py
@@ -1174,18 +1174,6 @@
         ]
     )
     bias = jnp.where(valid, 0.0, NEG).astype(f32)[None]
-    groups = mem_rows // RATE
-    start = mem_rows - RATE * groups
-    mem_valid = (jnp.arange(mem_rows, dtype=jnp.int32) >= mem_rows - mem_fill[0]).astype(bf16)
-    taps = (memory[0] * mem_valid[:, None])[start:, :].reshape(groups, RATE * width)
-    group_valid = (
-        start + RATE * jnp.arange(groups, dtype=jnp.int32) + RATE - 1 >= mem_rows - mem_fill[0]
-    )[:, None]
-    made_grad = comp_grad[0] * group_valid.astype(bf16)
-    conv_grad = jnp.einsum("nk,nd->kd", taps, made_grad, preferred_element_type=f32).astype(bf16)
-    conv_bias_grad = jnp.sum(made_grad.astype(f32), axis=0)
-
-    conv_grad, taps, query_u = cut(conv_grad, taps, query_u)
     outer_weight, query_u = cut(outer_weight, query_u)
     outer_w = lax.all_gather(outer_weight, "fsdp", axis=0, tiled=True)
     mixed, prob_low = attn_fwd(query_u, query_v, keys, values, relative, bias)
@@ -1200,6 +1188,18 @@
     outer_grad = jnp.einsum("sf,sd->fd", active, grad, preferred_element_type=f32).astype(bf16)
     outer_bias_grad = jnp.sum(grad_wide, axis=0)
 
+    groups = mem_rows // RATE
+    start = mem_rows - RATE * groups
+    mem_valid = (jnp.arange(mem_rows, dtype=jnp.int32) >= mem_rows - mem_fill[0]).astype(bf16)
+    taps = (memory[0] * mem_valid[:, None])[start:, :].reshape(groups, RATE * width)
+    group_valid = (
+        start + RATE * jnp.arange(groups, dtype=jnp.int32) + RATE - 1 >= mem_rows - mem_fill[0]
+    )[:, None]
+    made_grad = comp_grad[0] * group_valid.astype(bf16)
+    made_grad, active = cut(made_grad, active)
+    conv_grad = jnp.einsum("nk,nd->kd", taps, made_grad, preferred_element_type=f32).astype(bf16)
+    conv_bias_grad = jnp.sum(made_grad.astype(f32), axis=0)
+
     outer_w, outer_grad, conv_grad = cut(outer_w, outer_grad, conv_grad)
     conv_part = lax.psum_scatter(conv_grad, "fsdp", scatter_dimension=0, tiled=True)
     outer_part = lax.psum_scatter(outer_grad, "fsdp", scatter_dimension=0, tiled=True)
@@ -1235,12 +1235,16 @@
     conv_pair = add(conv_part, conv_end)
     conv_mid = middle_hop(conv_pair)
     query_grad = jnp.einsum("sd,se->de", own_rows, query_g, preferred_element_type=f32).astype(bf16)
-    columns = (
-        (query_w, jnp.sum(query_g.astype(f32), axis=0)),
-        (key_w, jnp.sum(keys_g.astype(f32), axis=1)),
-        (value_w, jnp.sum(values_g.astype(f32), axis=1)),
-    )
-    first_shift_grad = sum(jnp.sum(w.astype(f32) * column[None, :], axis=1) for w, column in columns)
+    trio = (
+        (query_w, query_grad, jnp.sum(query_g.astype(f32), axis=0)),
+        (key_w, key_grad, jnp.sum(keys_g.astype(f32), axis=1)),
+        (value_w, value_grad, jnp.sum(values_g.astype(f32), axis=1)),
+    )
+    first_shift_grad = sum(
+        jnp.sum(w.astype(f32) * column[None, :], axis=1) for w, _, column in trio
+    )
+    with_normed = sum(jnp.sum(w.astype(f32) * g.astype(f32), axis=1) for w, g, _ in trio)
+    first_gain_grad = (with_normed - shift_one.astype(f32) * first_shift_grad) / gain_one.astype(f32)
     own_grad = jnp.einsum("se,de->sd", query_g, query_w, preferred_element_type=f32)
     own_grad = own_grad + jnp.einsum(
         "es,de->sd", keys_g[:, old:], key_w, preferred_element_type=f32
@@ -1263,6 +1267,7 @@
     conv_last = outward_hop(conv_sum)
     output_grad = jnp.einsum("sd,se->de", mixed, hidden_low, preferred_element_type=f32).astype(bf16)
     vector_grads = (
+        first_gain_grad,
         first_shift_grad,
         sums[0],
         sums[1],
@@ -1301,6 +1306,7 @@
     conv_last, query_mean = cut(conv_last, query_mean)
     conv_mean = finish(conv_sum, conv_last, share)
     (
+        first_gain_mean,
         first_shift_mean,
         content_mean,
         posbias_mean,
@@ -1308,13 +1314,8 @@
         second_shift_mean,
         outer_bias_mean,
         conv_bias_mean,
-    ) = (table_mean[n] for n in range(7))
-    inner_bias_mean = table_mean[7 : 7 + sizes[-1] // lanes].reshape(sizes[-1])
-    with_normed = sum(
-        jnp.sum(w.astype(f32) * mean, axis=1)
-        for w, mean in ((query_weight, query_mean), (key_weight, key_mean), (value_weight, value_mean))
-    )
-    first_gain_mean = (with_normed - first_shift.astype(f32) * first_shift_mean) / first_gain.astype(f32)
+    ) = (table_mean[n] for n in range(8))
+    inner_bias_mean = table_mean[8 : 8 + sizes[-1] // lanes].reshape(sizes[-1])
     return (
         result[None],
         token_gradient[None],

time: 475 us -> 473 us (level)
  matrix products: 97.7 us -> 107 us
  Pallas kernels: 277 us -> 268 us
    pallas_call x1, Pallas kernels: 137 us -> 128 us  [reduce_tail(): pl.pallas_call(functools.partial(tail_kernel, plan, sources, len(arrays))...]
    mul x6 -> x8, other arithmetic: 6.89 us -> 11 us  [reduce_tail(): return [total.astype(f32) * share for total in totals]]
  transfers between devices with their start and end apart: 7 -> 7, of which waited for: 2 -> 1; matrix products, arithmetic and copies ran while one was open for 27% -> 32% of each run, Pallas kernels for 44% -> 42%
where the time goes in v4:
time: 473 us; the launch traced here: 466 us
  Pallas kernels  268 us (57%)
  matrix products  107 us (23%)
  other arithmetic  38.3 us (8%)
  local copies, waits for them, and re-layouts  16.6 us (4%)
  between operations  16.3 us (3%)
  waiting for transfers between devices  13.2 us (3%)
  starting transfers between devices  7.15 us (2%)
    pallas_call x1, Pallas kernels, reduce_tail(): pl.pallas_call(functools.partial(tail_kernel, plan, sources, len(arrays))...  128 us
    pallas_call x1, Pallas kernels, head_stage(): pl.pallas_call(head_kernel, in_specs=[pl.BlockSpec(memory_space=pltpu.VME...  71.1 us
    pallas_call x1, Pallas kernels, attn_bwd(): pl.pallas_call(attn_bwd_kernel, grid=(HEADS,), in_specs=in_specs, out_spe...  42.5 us
    pallas_call x1, Pallas kernels, attn_fwd(): pl.pallas_call(attn_fwd_kernel, grid=(HEADS,), in_specs=in_specs, out_spe...  26.3 us
    dot_general x1, matrix products, per_device_direct(): jnp.einsum('sd,fd->sf', grad, outer_w, preferred_element_type=f32)  14 us
    ppermute x3, waiting for transfers between devices, hop(): return lax.ppermute(value, ('dp', 'fsdp'), pairs)  12.5 us
    mul x8, other arithmetic, reduce_tail(): return [total.astype(f32) * share for total in totals]  11 us
    dot_general x1, matrix products, per_device_direct(): jnp.einsum('sf,sd->fd', active, grad, preferred_element_type=f32)  10.3 us
  transfers between devices with their start and end apart: 7, of which 1 were waited for; matrix products, arithmetic and copies ran while one was open for 32% of the time, Pallas kernels for 42%

profile of v4, /device:TPU:0, one launch (start us, length us, event | category | flops | bytes accessed | tf_op | source)
XLA Modules:
  0.0 466.4 jit_solution(5117314705932718781)
XLA Ops:
  9.7 2.6 add_convert_fusion
  13.1 71.1 %head_stage.1 = (f32[512,1024]{1,0:T(8,128)}, bf16[3,512,1024]{2,1,0:T(8,128)(2,1)}, bf16[512,1024]{1,0:T(8,128)(2,1)}, bf16[512,1024]{1,0:T(8,128)(2,1)}, bf16[...) custom-call(bf16[512,1024]{1,0:T(8,128)(2,1)} %bitcast.143, ...), custom_call_target="tpu_custom_call" | custom-call | tf_op jit(solution)/shard_map/head_stage/pallas_call | solution.py:838
  87.2 26.3 %attn_fwd.1 = (bf16[512,1024]{1,0:T(8,128)(2,1)}, bf16[8,512,1536]{2,1,0:T(8,128)(2,1)}) custom-call(bf16[512,1024]{1,0:T(8,128)(2,1)} %get-tuple-element.79.qu_ref, bf16[512,1024]{1,0:T(8,128)(2,1)} %get-tuple-element.80.qv_ref, bf16[1536,1024]{1,0:T(8,128)(2,1)} %bitcast.173, bf16[1536,1024]{1,0:T(8,128)(2,1)} %bitcast.175, bf16[1536,1024]{1,0:T(8,128)(2,1)} %bitcast.177, ...), custom_call_target="tpu_custom_call" | custom-call | flops 4831838208 | bytes 25165824 | tf_op jit(solution)/shard_map/attn_fwd/pallas_call | solution.py:138
  113.5 2.8 fusion.53
  116.7 1.6 slice_convert_fusion.1
  118.3 9.8 %fusion.14 = (bf16[512,4096]{1,0:T(8,128)(2,1)}, f32[512,4096]{1,0:T(8,128)}) fusion(f32[4096]{0:T(1024)S(1)} %convert.53, bf16[1024,4096]{1,0:T(8,128)(2,1)S(1)} %copy-done.38, f32[512,1024]{1,0:T(8,128)S(1)} %get-tuple-element.166, f32[1024]{0:T(1024)S(1)} %bitcast.167, f32[1024]{0:T(1024)S(1)} %bitcast.157, f32[512]{0:T(512)S(1)} %add_rsqrt_fusion.1, ...), kind=kOutput, calls=%fused_computation.17 | convolution fusion | flops 4318560256 | bytes 23097344 | tf_op jit(solution)/shard_map/dot_general | solution.py:1183
  128.3 1.3 slice_multiply_fusion
  129.6 2.6 reshape.540
  132.2 5.7 %convolution_convert_fusion.2 = bf16[3072,1024]{1,0:T(8,128)(2,1)} fusion(bf16[170,3072]{1,0:T(8,128)(2,1)} %reshape.540, bf16[170,1024]{1,0:T(8,128)(2,1)S(1)} %bitcast_multiply_fusion.2), kind=kOutput, calls=%fused_computation.29 | convolution fusion | flops 1072693248 | bytes 7684096 | tf_op jit(solution)/shard_map/nk,nd->kd/dot_general | solution.py:1200
  137.9 10.3 %convolution_convert_fusion.1 = bf16[4096,1024]{1,0:T(8,128)(2,1)} fusion(bf16[512,4096]{1,0:T(8,128)(2,1)} %get-tuple-element.108, bf16[1,512,1024]{2,1,0:T(8,128)(2,1)} %param.48), kind=kOutput, calls=%fused_computation.24 | convolution fusion | flops 4299161600 | bytes 13631488 | tf_op jit(solution)/shard_map/sf,sd->fd/dot_general | solution.py:1188
  149.0 2.7 copy.49
  151.8 2.3 copy.50
  154.1 1.6 reduce
  157.0 14.0 %fusion.54 = (bf16[4096]{0:T(1024)(128)(2,1)S(1)}, bf16[512,4096]{1,0:T(8,128)(2,1)S(1)}) fusion(f32[512,4096]{1,0:T(8,128)} %get-tuple-element.94, bf16[4096,1024]{1,0:T(8,128)(2,1)} %all-gather.3.cloned.1.call-done, bf16[1,512,1024]{2,1,0:T(8,128)(2,1)S(1)} %copy-done.10), kind=kOutput, calls=%fused_computation.162 | convolution fusion | flops 4339003392 | bytes 22028288 | tf_op jit(solution)/shard_map/sd,fd->sf/dot_general | solution.py:1206
  171.0 9.6 %multiply_reduce_fusion = (bf16[1024]{0:T(1024)(128)(2,1)S(1)}, f32[512]{0:T(512)S(1)}, f32[512]{0:T(512)S(1)}, bf16[1024]{0:T(1024)(128)(2,1)S(1)}, f32[512,1024]{1,0:T(8,128)S(1)}) fusion(f32[512,1024]{1,0:T(8,128)S(1)} %get-tuple-element.166, f32[512]{0:T(512)S(1)} %add_rsqrt_fusion.1, f32[512]{0:T(512)S(1)} %broadcast_multiply_fusion.5, ...), kind=kOutput, calls=%fused_computation.49 | convolution fusion | flops 4299682816 | bytes 16793600 | tf_op jit(solution)/shard_map/sf,df->sd/dot_general | solution.py:1213
  180.7 2.1 fusion.51
  183.8 1.3 convolution_convert_fusion.8
  185.1 1.3 copy.52.g_ref
  186.4 42.5 %attn_bwd.1 = (bf16[512,1024]{1,0:T(8,128)(2,1)}, bf16[1024,1536]{1,0:T(8,128)(2,1)}, bf16[1024,1536]{1,0:T(8,128)(2,1)}, bf16[1024,1536]{1,0:T(8,128)(2,1)}, f32[8,1024]{1,0:T(8,128)}) custom-call(bf16[512,1024]{1,0:T(8,128)(2,1)} %get-tuple-element.79.qu_ref, bf16[512,1024]{1,0:T(8,128)(2,1)} %get-tuple-element.80.qv_ref, bf16[1024,512]{1,0:T(8,128)(2,1)} %bitcast.144, ...), custom_call_target="tpu_custom_call" | custom-call | flops 12884901888 | bytes 36700160 | tf_op jit(solution)/shard_map/attn_bwd/pallas_call | solution.py:249
  229.9 2.9 convert_reduce_fusion.1
  233.4 1.4 copy-done.14
  234.7 2.7 fusion.37
  237.4 3.7 convolution_convert_fusion.6
  241.1 4.8 %convolution_convert_fusion.7 = bf16[1024,1024]{1,0:T(8,128)(2,1)} fusion(bf16[1536,1024]{1,0:T(8,128)(2,1)S(1)} %bitcast.172, bf16[1024,1536]{1,0:T(8,128)(2,1)S(1)} %copy-done.14), kind=kOutput, calls=%fused_computation.64 | convolution fusion | flops 3222274048 | bytes 8388608 | tf_op jit(solution)/shard_map/sd,es->de/dot_general | solution.py:1227
  246.0 7.4 %convolution_convert_fusion = bf16[1024,4096]{1,0:T(8,128)(2,1)} fusion(bf16[512,4096]{1,0:T(8,128)(2,1)S(1)} %copy-done.45, f32[512,1024]{1,0:T(8,128)S(1)} %copy-done.5, f32[1024]{0:T(1024)S(1)} %bitcast.168, f32[1024]{0:T(1024)S(1)} %bitcast.160, f32[512]{0:T(512)S(1)} %add_rsqrt_fusion.1, f32[512]{0:T(512)S(1)} %broadcast_multiply_fusion.5), kind=kOutput, calls=%fused_computation.23 | convolution fusion | flops 4301783040 | bytes 14692352 | tf_op jit(solution)/shard_map/sd,sf->df/dot_general | solution.py:1210
  253.4 4.8 %fusion.35 = f32[512,1024]{1,0:T(8,128)} fusion(bf16[1024,1024]{1,0:T(8,128)(2,1)} %get-tuple-element.106, bf16[1024,1536]{1,0:T(8,128)(2,1)} %get-tuple-element.99), kind=kOutput, calls=%fused_computation.82 | convolution fusion | flops 1073741824 | bytes 5242880 | tf_op jit(solution)/shard_map/es,de->sd/dot_general | solution.py:1252
  258.2 3.8 collective-permute-start
  262.0 4.7 %convolution_convert_fusion.5 = bf16[1024,1024]{1,0:T(8,128)(2,1)} fusion(bf16[1536,1024]{1,0:T(8,128)(2,1)S(1)} %bitcast.133, bf16[1024,1536]{1,0:T(8,128)(2,1)S(1)} %copy-done.46), kind=kOutput, calls=%fused_computation.62 | convolution fusion | flops 3222274048 | bytes 8388608 | tf_op jit(solution)/shard_map/ld,el->de/dot_general | solution.py:1229
  266.7 12.5 %collective-permute-done = bf16[384,1024]{1,0:T(8,128)(2,1)S(1)} collective-permute-done((bf16[384,1024]{1,0:T(8,128)(2,1)S(1)}, bf16[384,1024]{1,0:T(8,128)(2,1)S(1)}, u32[]{:S(2)}, u32[]{:S(2)}) %collective-permute-start) | collective-permute-done | bytes 786464 | tf_op jit(solution)/shard_map/ppermute | solution.py:306
  279.2 1.2 add_convert_fusion.4
  280.4 1.7 collective-permute-start.1
  282.3 1.2 fusion.21
  283.9 1.1 fusion.23
  285.5 4.5 fusion.19
  291.6 4.7 %multiply_reduce_fusion.4 = (f32[512]{0:T(512)S(1)}, f32[512]{0:T(512)S(1)}, f32[512,1024]{1,0:T(8,128)S(1)}) fusion(f32[1024]{0:T(1024)S(1)} %bitcast.149, f32[512,1024]{1,0:T(8,128)S(1)} %copy-done.7, f32[512,1024]{1,0:T(8,128)} %fusion.35, f32[512,1024]{1,0:T(8,128)} %fusion.37, bf16[512,1024]{1,0:T(8,128)(2,1)S(1)} %copy-done.11, ...), kind=kOutput, calls=%fused_computation.65 | convolution fusion | flops 1076886528 | bytes 11542528 | tf_op jit(solution)/shard_map/se,de->sd/dot_general | solution.py:1248
  296.3 1.8 add_bitcast_fusion
  298.1 2.0 add_convert_fusion.3
  300.2 1.3 collective-permute-start.2
  301.5 9.1 %fusion.26 = bf16[1,512,1024]{2,1,0:T(8,128)(2,1)} fusion(f32[512,1024]{1,0:T(8,128)S(1)} %copy-done.6, bf16[512,4096]{1,0:T(8,128)(2,1)S(1)} %copy-done.43, bf16[4096,1024]{1,0:T(8,128)(2,1)} %all-gather.3.cloned.1.call-done, f32[1024]{0:T(1024)S(1)} %bitcast.166), kind=kOutput, calls=%fused_computation.71 | convolution fusion | flops 4296540160 | bytes 15732736 | tf_op jit(solution)/shard_map/dot_general | solution.py:1283
  310.6 2.7 convolution_convert_fusion.4
  313.3 127.6 %reduce_tail.1 = (bf16[128,1024]{1,0:T(8,128)(2,1)}, bf16[128,1024]{1,0:T(8,128)(2,1)}, bf16[128,1024]{1,0:T(8,128)(2,1)}, bf16[128,1024]{1,0:T(8,128)(2,1)}, bf...) custom-call(bf16[8,128,1024]{2,1,0:T(8,128)(2,1)} %bitcast.142, ...), custom_call_target="tpu_custom_call" | custom-call | tf_op jit(solution)/shard_map/reduce_tail/pallas_call | solution.py:607
  441.0 1.9 convert_multiply_fusion.13
  444.7 1.8 convert_multiply_fusion.10
  446.5 1.8 convert_multiply_fusion.11
  450.0 1.6 convert_multiply_fusion.6
  451.6 1.4 convert_multiply_fusion.8
  453.0 1.5 convert_multiply_fusion.7
  454.6 4.8 %fusion.29 = bf16[1,170,1024]{2,1,0:T(8,128)(2,1)} fusion(bf16[170,3072]{1,0:T(8,128)(2,1)S(1)} %copy-done.9, bf16[3072,1024]{1,0:T(8,128)(2,1)} %all-gather.5.cloned.1.call-done, f32[170]{0:T(256)S(1)} %fusion.48, f32[1024]{0:T(1024)S(1)} %bitcast.165), kind=kOutput, calls=%fused_computation.75 | convolution fusion | flops 1070069760 | bytes 7688872 | tf_op jit(solution)/shard_map/dot_general | solution.py:1286
  (165 shorter events, 16.2 us)
Async XLA Ops:
  7.2 141.0 %all-gather.3.cloned.1.call-start = ((), (), s32[]{:S(2)}) async-start(), calls=%async_computation.2 | async-start | bytes 9437184 | tf_op jit(solution)/shard_map/all_gather | solution.py:1178
  8.4 4.0 copy-start.30
  8.4 4.0 copy-start.31
  8.4 3.9 copy-start.32
  8.4 3.9 copy-start.33
  8.4 3.9 copy-start.34
  8.4 3.9 copy-start.35
  8.4 3.9 copy-start.36
  8.4 3.9 copy-start.37
  13.1 73.4 %copy-start.29 = (s32[1,512]{1,0:T(1,128)S(1)}, s32[1,512]{1,0:T(1,128)}, u32[]{:S(2)}) copy-start(s32[1,512]{1,0:T(1,128)} %param.30) | copy-start | bytes 6148
  84.2 169.1 %reduce-scatter.3.cloned.1.call-start = ((), (), s32[]{:S(2)}) async-start(), calls=%async_computation.3 | async-start | bytes 7077888 | tf_op jit(solution)/shard_map/reduce_scatter | solution.py:1204
  87.2 26.3 %copy-start.1 = (bf16[1,512,1024]{2,1,0:T(8,128)(2,1)S(1)}, bf16[1,512,1024]{2,1,0:T(8,128)(2,1)}, u32[]{:S(2)}) copy-start(bf16[1,512,1024]{2,1,0:T(8,128)(2,1)} %param.25) | copy-start | bytes 3145732
  87.2 26.3 %copy-start.40 = (bf16[1024,1024]{1,0:T(8,128)(2,1)S(1)}, bf16[1024,1024]{1,0:T(8,128)(2,1)}, u32[]{:S(2)}) copy-start(bf16[1024,1024]{1,0:T(8,128)(2,1)} %get-tuple-element.85) | copy-start | bytes 6291460
  113.5 4.8 %copy-start.38 = (bf16[1024,4096]{1,0:T(8,128)(2,1)S(1)}, bf16[1024,4096]{1,0:T(8,128)(2,1)}, u32[]{:S(2)}) copy-start(bf16[1024,4096]{1,0:T(8,128)(2,1)} %get-tuple-element.88) | copy-start | bytes 25165828
  116.3 64.4 %copy-start.4 = (f32[512,1024]{1,0:T(8,128)}, f32[512,1024]{1,0:T(8,128)S(1)}, u32[]{:S(2)}) copy-start(f32[512,1024]{1,0:T(8,128)S(1)} %get-tuple-element.166) | copy-start | bytes 6291460
  118.3 9.9 %copy-start.25 = (bf16[1,170,1024]{2,1,0:T(8,128)(2,1)S(1)}, bf16[1,170,1024]{2,1,0:T(8,128)(2,1)}, u32[]{:S(2)}) copy-start(bf16[1,170,1024]{2,1,0:T(8,128)(2,1)} %param.49) | copy-start | bytes 1044484
  118.3 10.0 %copy-start.12 = (bf16[1,512,1024]{2,1,0:T(8,128)(2,1)S(1)}, bf16[1,512,1024]{2,1,0:T(8,128)(2,1)}, u32[]{:S(2)}) copy-start(bf16[1,512,1024]{2,1,0:T(8,128)(2,1)} %param.26) | copy-start | bytes 3145732
  148.2 165.1 %reduce-scatter.5.cloned.1.call-start = ((), (), s32[]{:S(2)}) async-start(), calls=%async_computation.5 | async-start | bytes 9437184 | tf_op jit(solution)/shard_map/reduce_scatter | solution.py:1205
  149.0 305.6 %all-gather.5.cloned.1.call-start = ((), (), s32[]{:S(2)}) async-start(), calls=%async_computation.4 | async-start | bytes 7077888 | tf_op jit(solution)/shard_map/all_gather | solution.py:1226
  171.0 9.7 %copy-start.44 = (bf16[512,4096]{1,0:T(8,128)(2,1)}, bf16[512,4096]{1,0:T(8,128)(2,1)S(1)}, u32[]{:S(2)}) copy-start(bf16[512,4096]{1,0:T(8,128)(2,1)S(1)} %get-tuple-element.173) | copy-start | bytes 12582916
  180.7 3.1 copy-start.41
  186.4 46.9 %copy-start.17 = (bf16[1024,1024]{1,0:T(8,128)(2,1)S(1)}, bf16[1024,1024]{1,0:T(8,128)(2,1)}, u32[]{:S(2)}) copy-start(bf16[1024,1024]{1,0:T(8,128)(2,1)} %get-tuple-element.105) | copy-start | bytes 6291460
  229.0 3.9 copy-start.13
  232.8 1.9 copy-start.14
  234.7 2.7 copy-start.39
  241.1 42.4 %copy-start.2 = (bf16[1024,1024]{1,0:T(8,128)(2,1)}, bf16[1024,1024]{1,0:T(8,128)(2,1)S(1)}, u32[]{:S(2)}) copy-start(bf16[1024,1024]{1,0:T(8,128)(2,1)S(1)} %convolution_convert_fusion.6) | copy-start | bytes 6291460
  241.1 4.8 %copy-start.5 = (f32[512,1024]{1,0:T(8,128)S(1)}, f32[512,1024]{1,0:T(8,128)}, u32[]{:S(2)}) copy-start(f32[512,1024]{1,0:T(8,128)} %copy-done.4) | copy-start | bytes 6291460
  241.1 4.8 %copy-start.45 = (bf16[512,4096]{1,0:T(8,128)(2,1)S(1)}, bf16[512,4096]{1,0:T(8,128)(2,1)}, u32[]{:S(2)}) copy-start(bf16[512,4096]{1,0:T(8,128)(2,1)} %copy-done.44) | copy-start | bytes 12582916
  253.4 4.8 %copy-start.24 = (bf16[384,1024]{1,0:T(8,128)(2,1)S(1)}, bf16[384,1024]{1,0:T(8,128)(2,1)}, u32[]{:S(2)}) copy-start(bf16[384,1024]{1,0:T(8,128)(2,1)} %reduce-scatter.3.cloned.1.call-done) | copy-start | bytes 2359300
  253.4 8.6 %copy-start = (bf16[24,64,1024]{2,1,0:T(8,128)(2,1)S(1)}, bf16[24,64,1024]{2,1,0:T(8,128)(2,1)}, u32[]{:S(2)}) copy-start(bf16[24,64,1024]{2,1,0:T(8,128)(2,1)} %add_convert_fusion) | copy-start | bytes 9437188
  253.4 8.6 %copy-start.46 = (bf16[1024,1536]{1,0:T(8,128)(2,1)S(1)}, bf16[1024,1536]{1,0:T(8,128)(2,1)}, u32[]{:S(2)}) copy-start(bf16[1024,1536]{1,0:T(8,128)(2,1)} %get-tuple-element.100) | copy-start | bytes 9437188
  258.2 21.0 %collective-permute-start = (bf16[384,1024]{1,0:T(8,128)(2,1)S(1)}, bf16[384,1024]{1,0:T(8,128)(2,1)S(1)}, u32[]{:S(2)}, u32[]{:S(2)}) collective-permute-start(bf16[384,1024]{1,0:T(8,128)(2,1)S(1)} %copy-done.24), channel_id=1, source_target_pairs={{0,8},{1,9},{2,10},{3,11},{4,12},{5,13},{6,14},{7,15},{24,16},{25,... | collective-permute-start | bytes 2359304 | tf_op jit(solution)/shard_map/ppermute | solution.py:306
  262.0 20.1 %copy-start.11 = (bf16[512,1024]{1,0:T(8,128)(2,1)S(1)}, bf16[512,1024]{1,0:T(8,128)(2,1)}, u32[]{:S(2)}) copy-start(bf16[512,1024]{1,0:T(8,128)(2,1)} %get-tuple-element.103) | copy-start | bytes 3145732
  262.0 20.2 %copy-start.18 = (bf16[1024,1024]{1,0:T(8,128)(2,1)S(1)}, bf16[1024,1024]{1,0:T(8,128)(2,1)}, u32[]{:S(2)}) copy-start(bf16[1024,1024]{1,0:T(8,128)(2,1)} %get-tuple-element.105) | copy-start | bytes 6291460
  266.7 15.6 %copy-start.3 = (bf16[1024,1024]{1,0:T(8,128)(2,1)S(1)}, bf16[1024,1024]{1,0:T(8,128)(2,1)}, u32[]{:S(2)}) copy-start(bf16[1024,1024]{1,0:T(8,128)(2,1)} %convolution_convert_fusion.7) | copy-start | bytes 6291460
  280.4 17.8 %collective-permute-start.1 = (bf16[384,1024]{1,0:T(8,128)(2,1)}, bf16[384,1024]{1,0:T(8,128)(2,1)}, u32[]{:S(2)}, u32[]{:S(2)}) collective-permute-start(bf16[384,1024]{1,0:T(8,128)(2,1)} %add_convert_fusion.4), channel_id=1, source_target_pairs={{8,16},{9,17},{10,18},{11,19},{12,20},{13,21},{14,22},{15,23},{16,... | collective-permute-start | bytes 2359304 | tf_op jit(solution)/shard_map/ppermute | solution.py:306
  282.3 1.6 copy-start.16
  283.9 1.6 copy-start.15
  285.5 6.1 %copy-start.7 = (f32[512,1024]{1,0:T(8,128)S(1)}, f32[512,1024]{1,0:T(8,128)}, u32[]{:S(2)}) copy-start(f32[512,1024]{1,0:T(8,128)} %get-tuple-element.109) | copy-start | bytes 6291460
  291.6 4.7 %copy-start.8 = (f32[512,1024]{1,0:T(8,128)S(1)}, f32[512,1024]{1,0:T(8,128)}, u32[]{:S(2)}) copy-start(f32[512,1024]{1,0:T(8,128)} %get-tuple-element.141) | copy-start | bytes 6291460
  296.3 5.2 %copy-start.43 = (bf16[512,4096]{1,0:T(8,128)(2,1)S(1)}, bf16[512,4096]{1,0:T(8,128)(2,1)}, u32[]{:S(2)}) copy-start(bf16[512,4096]{1,0:T(8,128)(2,1)} %get-tuple-element.108) | copy-start | bytes 12582916
  298.1 3.4 copy-start.6
  300.2 142.7 %collective-permute-start.2 = (bf16[384,1024]{1,0:T(8,128)(2,1)S(1)}, bf16[384,1024]{1,0:T(8,128)(2,1)S(1)}, u32[]{:S(2)}, u32[]{:S(2)}) collective-permute-start(bf16[384,1024]{1,0:T(8,128)(2,1)S(1)} %add_convert_fusion.3), channel_id=1, source_target_pairs={{8,0},{9,1},{10,2},{11,3},{12,4},{13,5},{14,6},{15,7},{16,24},{17,... | collective-permute-start | bytes 2359304 | tf_op jit(solution)/shard_map/ppermute | solution.py:306
  301.5 9.1 %copy-start.20 = (bf16[512,1024]{1,0:T(8,128)(2,1)S(1)}, bf16[512,1024]{1,0:T(8,128)(2,1)}, u32[]{:S(2)}) copy-start(bf16[512,1024]{1,0:T(8,128)(2,1)} %copy-done.19) | copy-start | bytes 3145732
  301.5 9.1 %copy-start.42 = (bf16[512,1024]{1,0:T(8,128)(2,1)S(1)}, bf16[512,1024]{1,0:T(8,128)(2,1)}, u32[]{:S(2)}) copy-start(bf16[512,1024]{1,0:T(8,128)(2,1)} %get-tuple-element.84) | copy-start | bytes 3145732
  440.9 7.4 %copy-start.27 = (bf16[128,1024]{1,0:T(8,128)(2,1)S(1)}, bf16[128,1024]{1,0:T(8,128)(2,1)}, u32[]{:S(2)}) copy-start(bf16[128,1024]{1,0:T(8,128)(2,1)} %get-tuple-element.121) | copy-start | bytes 786436
  440.9 8.2 %copy-start.26 = (bf16[128,1024]{1,0:T(8,128)(2,1)S(1)}, bf16[128,1024]{1,0:T(8,128)(2,1)}, u32[]{:S(2)}) copy-start(bf16[128,1024]{1,0:T(8,128)(2,1)} %get-tuple-element.124) | copy-start | bytes 786436
  441.0 9.0 %copy-start.22 = (bf16[512,1024]{1,0:T(8,128)(2,1)S(1)}, bf16[512,1024]{1,0:T(8,128)(2,1)}, u32[]{:S(2)}) copy-start(bf16[512,1024]{1,0:T(8,128)(2,1)} %get-tuple-element.126) | copy-start | bytes 3145732
  (6 other events, 8.1 us)
Sparse Core Ops, SparseCore 0:
  84.3 54.6 all-gather.2
  148.4 62.6 reduce-scatter.2
  214.9 71.2 reduce-scatter.4
  288.0 54.5 all-gather.4

commit v5 on v4

--- a/solution.py
+++ b/solution.py
@@ -1296,7 +1296,7 @@
         table_mean,
         outer_mean,
     ) = reduce_tail(
-        [(g, 2) for g in (output_grad, query_grad, key_grad, value_grad, position_grad)]
+        [(g, 1) for g in (output_grad, query_grad, key_grad, value_grad, position_grad)]
         + [(inner_grad, 4)]
         + [(packed.reshape(shards * 32, lanes), 1)],
         [(outer_part, 4)],

time: 473 us -> 475 us (level)
  no operation moved by 1% of the time
where the time goes in v5:
time: 475 us; the launch traced here: 468 us
  Pallas kernels  269 us (57%)
  matrix products  107 us (23%)
  other arithmetic  38.3 us (8%)
  local copies, waits for them, and re-layouts  16.6 us (3%)
  between operations  16.3 us (3%)
  waiting for transfers between devices  13.2 us (3%)
  starting transfers between devices  7.15 us (2%)
    pallas_call x1, Pallas kernels, reduce_tail(): pl.pallas_call(functools.partial(tail_kernel, plan, sources, len(arrays))...  129 us
    pallas_call x1, Pallas kernels, head_stage(): pl.pallas_call(head_kernel, in_specs=[pl.BlockSpec(memory_space=pltpu.VME...  71.1 us
    pallas_call x1, Pallas kernels, attn_bwd(): pl.pallas_call(attn_bwd_kernel, grid=(HEADS,), in_specs=in_specs, out_spe...  42.5 us
    pallas_call x1, Pallas kernels, attn_fwd(): pl.pallas_call(attn_fwd_kernel, grid=(HEADS,), in_specs=in_specs, out_spe...  26.3 us
    dot_general x1, matrix products, per_device_direct(): jnp.einsum('sd,fd->sf', grad, outer_w, preferred_element_type=f32)  14 us
    ppermute x3, waiting for transfers between devices, hop(): return lax.ppermute(value, ('dp', 'fsdp'), pairs)  12.5 us
    mul x8, other arithmetic, reduce_tail(): return [total.astype(f32) * share for total in totals]  11 us
    dot_general x1, matrix products, per_device_direct(): jnp.einsum('sf,sd->fd', active, grad, preferred_element_type=f32)  10.3 us
  transfers between devices with their start and end apart: 7, of which 1 were waited for; matrix products, arithmetic and copies ran while one was open for 32% of the time, Pallas kernels for 42%

profile of v5, /device:TPU:0, one launch (start us, length us, event | category | flops | bytes accessed | tf_op | source)
XLA Modules:
  0.0 468.0 jit_solution(16941896102642872333)
XLA Ops:
  9.7 2.6 add_convert_fusion
  13.1 71.1 %head_stage.1 = (f32[512,1024]{1,0:T(8,128)}, bf16[3,512,1024]{2,1,0:T(8,128)(2,1)}, bf16[512,1024]{1,0:T(8,128)(2,1)}, bf16[512,1024]{1,0:T(8,128)(2,1)}, bf16[...) custom-call(bf16[512,1024]{1,0:T(8,128)(2,1)} %bitcast.143, ...), custom_call_target="tpu_custom_call" | custom-call | tf_op jit(solution)/shard_map/head_stage/pallas_call | solution.py:838
  87.2 26.3 %attn_fwd.1 = (bf16[512,1024]{1,0:T(8,128)(2,1)}, bf16[8,512,1536]{2,1,0:T(8,128)(2,1)}) custom-call(bf16[512,1024]{1,0:T(8,128)(2,1)} %get-tuple-element.79.qu_ref, bf16[512,1024]{1,0:T(8,128)(2,1)} %get-tuple-element.80.qv_ref, bf16[1536,1024]{1,0:T(8,128)(2,1)} %bitcast.173, bf16[1536,1024]{1,0:T(8,128)(2,1)} %bitcast.175, bf16[1536,1024]{1,0:T(8,128)(2,1)} %bitcast.177, ...), custom_call_target="tpu_custom_call" | custom-call | flops 4831838208 | bytes 25165824 | tf_op jit(solution)/shard_map/attn_fwd/pallas_call | solution.py:138
  113.5 2.8 fusion.53
  116.7 1.6 slice_convert_fusion.1
  118.3 9.8 %fusion.14 = (bf16[512,4096]{1,0:T(8,128)(2,1)}, f32[512,4096]{1,0:T(8,128)}) fusion(f32[4096]{0:T(1024)S(1)} %convert.53, bf16[1024,4096]{1,0:T(8,128)(2,1)S(1)} %copy-done.38, f32[512,1024]{1,0:T(8,128)S(1)} %get-tuple-element.166, f32[1024]{0:T(1024)S(1)} %bitcast.167, f32[1024]{0:T(1024)S(1)} %bitcast.157, f32[512]{0:T(512)S(1)} %add_rsqrt_fusion.1, ...), kind=kOutput, calls=%fused_computation.17 | convolution fusion | flops 4318560256 | bytes 23097344 | tf_op jit(solution)/shard_map/dot_general | solution.py:1183
  128.3 1.3 slice_multiply_fusion
  129.6 2.6 reshape.540
  132.2 5.7 %convolution_convert_fusion.2 = bf16[3072,1024]{1,0:T(8,128)(2,1)} fusion(bf16[170,3072]{1,0:T(8,128)(2,1)} %reshape.540, bf16[170,1024]{1,0:T(8,128)(2,1)S(1)} %bitcast_multiply_fusion.2), kind=kOutput, calls=%fused_computation.29 | convolution fusion | flops 1072693248 | bytes 7684096 | tf_op jit(solution)/shard_map/nk,nd->kd/dot_general | solution.py:1200
  137.9 10.3 %convolution_convert_fusion.1 = bf16[4096,1024]{1,0:T(8,128)(2,1)} fusion(bf16[512,4096]{1,0:T(8,128)(2,1)} %get-tuple-element.108, bf16[1,512,1024]{2,1,0:T(8,128)(2,1)} %param.48), kind=kOutput, calls=%fused_computation.24 | convolution fusion | flops 4299161600 | bytes 13631488 | tf_op jit(solution)/shard_map/sf,sd->fd/dot_general | solution.py:1188
  149.0 2.7 copy.49
  151.8 2.3 copy.50
  154.1 1.6 reduce
  157.0 14.0 %fusion.54 = (bf16[4096]{0:T(1024)(128)(2,1)S(1)}, bf16[512,4096]{1,0:T(8,128)(2,1)S(1)}) fusion(f32[512,4096]{1,0:T(8,128)} %get-tuple-element.94, bf16[4096,1024]{1,0:T(8,128)(2,1)} %all-gather.3.cloned.1.call-done, bf16[1,512,1024]{2,1,0:T(8,128)(2,1)S(1)} %copy-done.10), kind=kOutput, calls=%fused_computation.162 | convolution fusion | flops 4339003392 | bytes 22028288 | tf_op jit(solution)/shard_map/sd,fd->sf/dot_general | solution.py:1206
  171.0 9.6 %multiply_reduce_fusion = (bf16[1024]{0:T(1024)(128)(2,1)S(1)}, f32[512]{0:T(512)S(1)}, f32[512]{0:T(512)S(1)}, bf16[1024]{0:T(1024)(128)(2,1)S(1)}, f32[512,1024]{1,0:T(8,128)S(1)}) fusion(f32[512,1024]{1,0:T(8,128)S(1)} %get-tuple-element.166, f32[512]{0:T(512)S(1)} %add_rsqrt_fusion.1, f32[512]{0:T(512)S(1)} %broadcast_multiply_fusion.5, ...), kind=kOutput, calls=%fused_computation.49 | convolution fusion | flops 4299682816 | bytes 16793600 | tf_op jit(solution)/shard_map/sf,df->sd/dot_general | solution.py:1213
  180.7 2.1 fusion.51
  183.8 1.3 convolution_convert_fusion.8
  185.1 1.3 copy.52.g_ref
  186.4 42.5 %attn_bwd.1 = (bf16[512,1024]{1,0:T(8,128)(2,1)}, bf16[1024,1536]{1,0:T(8,128)(2,1)}, bf16[1024,1536]{1,0:T(8,128)(2,1)}, bf16[1024,1536]{1,0:T(8,128)(2,1)}, f32[8,1024]{1,0:T(8,128)}) custom-call(bf16[512,1024]{1,0:T(8,128)(2,1)} %get-tuple-element.79.qu_ref, bf16[512,1024]{1,0:T(8,128)(2,1)} %get-tuple-element.80.qv_ref, bf16[1024,512]{1,0:T(8,128)(2,1)} %bitcast.144, ...), custom_call_target="tpu_custom_call" | custom-call | flops 12884901888 | bytes 36700160 | tf_op jit(solution)/shard_map/attn_bwd/pallas_call | solution.py:249
  229.9 2.9 convert_reduce_fusion.1
  233.4 1.4 copy-done.14
  234.7 2.7 fusion.37
  237.4 3.7 convolution_convert_fusion.6
  241.1 4.8 %convolution_convert_fusion.7 = bf16[1024,1024]{1,0:T(8,128)(2,1)} fusion(bf16[1536,1024]{1,0:T(8,128)(2,1)S(1)} %bitcast.172, bf16[1024,1536]{1,0:T(8,128)(2,1)S(1)} %copy-done.14), kind=kOutput, calls=%fused_computation.64 | convolution fusion | flops 3222274048 | bytes 8388608 | tf_op jit(solution)/shard_map/sd,es->de/dot_general | solution.py:1227
  246.0 7.4 %convolution_convert_fusion = bf16[1024,4096]{1,0:T(8,128)(2,1)} fusion(bf16[512,4096]{1,0:T(8,128)(2,1)S(1)} %copy-done.45, f32[512,1024]{1,0:T(8,128)S(1)} %copy-done.5, f32[1024]{0:T(1024)S(1)} %bitcast.168, f32[1024]{0:T(1024)S(1)} %bitcast.160, f32[512]{0:T(512)S(1)} %add_rsqrt_fusion.1, f32[512]{0:T(512)S(1)} %broadcast_multiply_fusion.5), kind=kOutput, calls=%fused_computation.23 | convolution fusion | flops 4301783040 | bytes 14692352 | tf_op jit(solution)/shard_map/sd,sf->df/dot_general | solution.py:1210
  253.4 4.8 %fusion.35 = f32[512,1024]{1,0:T(8,128)} fusion(bf16[1024,1024]{1,0:T(8,128)(2,1)} %get-tuple-element.106, bf16[1024,1536]{1,0:T(8,128)(2,1)} %get-tuple-element.99), kind=kOutput, calls=%fused_computation.82 | convolution fusion | flops 1073741824 | bytes 5242880 | tf_op jit(solution)/shard_map/es,de->sd/dot_general | solution.py:1252
  258.2 3.8 collective-permute-start
  262.0 4.7 convolution_convert_fusion.5
  266.7 12.5 %collective-permute-done = bf16[384,1024]{1,0:T(8,128)(2,1)S(1)} collective-permute-done((bf16[384,1024]{1,0:T(8,128)(2,1)S(1)}, bf16[384,1024]{1,0:T(8,128)(2,1)S(1)}, u32[]{:S(2)}, u32[]{:S(2)}) %collective-permute-start) | collective-permute-done | bytes 786464 | tf_op jit(solution)/shard_map/ppermute | solution.py:306
  279.2 1.2 add_convert_fusion.4
  280.4 1.7 collective-permute-start.1
  282.3 1.2 fusion.21
  283.9 1.1 fusion.23
  285.5 4.5 fusion.19
  291.6 4.7 %multiply_reduce_fusion.4 = (f32[512]{0:T(512)S(1)}, f32[512]{0:T(512)S(1)}, f32[512,1024]{1,0:T(8,128)S(1)}) fusion(f32[1024]{0:T(1024)S(1)} %bitcast.149, f32[512,1024]{1,0:T(8,128)S(1)} %copy-done.7, f32[512,1024]{1,0:T(8,128)} %fusion.35, f32[512,1024]{1,0:T(8,128)} %fusion.37, bf16[512,1024]{1,0:T(8,128)(2,1)S(1)} %copy-done.11, ...), kind=kOutput, calls=%fused_computation.65 | convolution fusion | flops 1076886528 | bytes 11542528 | tf_op jit(solution)/shard_map/se,de->sd/dot_general | solution.py:1248
  296.3 1.8 add_bitcast_fusion
  298.1 2.0 add_convert_fusion.3
  300.2 1.3 collective-permute-start.2
  301.5 9.1 %fusion.26 = bf16[1,512,1024]{2,1,0:T(8,128)(2,1)} fusion(f32[512,1024]{1,0:T(8,128)S(1)} %copy-done.6, bf16[512,4096]{1,0:T(8,128)(2,1)S(1)} %copy-done.43, bf16[4096,1024]{1,0:T(8,128)(2,1)} %all-gather.3.cloned.1.call-done, f32[1024]{0:T(1024)S(1)} %bitcast.166), kind=kOutput, calls=%fused_computation.71 | convolution fusion | flops 4296540160 | bytes 15732736 | tf_op jit(solution)/shard_map/dot_general | solution.py:1283
  310.6 2.7 convolution_convert_fusion.4
  313.3 129.3 %reduce_tail.1 = (bf16[128,1024]{1,0:T(8,128)(2,1)}, bf16[128,1024]{1,0:T(8,128)(2,1)}, bf16[128,1024]{1,0:T(8,128)(2,1)}, bf16[128,1024]{1,0:T(8,128)(2,1)}, bf...) custom-call(bf16[8,128,1024]{2,1,0:T(8,128)(2,1)} %bitcast.142, ...), custom_call_target="tpu_custom_call" | custom-call | tf_op jit(solution)/shard_map/reduce_tail/pallas_call | solution.py:607
  442.6 1.9 convert_multiply_fusion.13
  446.4 1.8 convert_multiply_fusion.10
  448.2 1.8 convert_multiply_fusion.11
  451.7 1.6 convert_multiply_fusion.6
  453.3 1.4 convert_multiply_fusion.8
  454.7 1.5 convert_multiply_fusion.7
  456.3 4.8 %fusion.29 = bf16[1,170,1024]{2,1,0:T(8,128)(2,1)} fusion(bf16[170,3072]{1,0:T(8,128)(2,1)S(1)} %copy-done.9, bf16[3072,1024]{1,0:T(8,128)(2,1)} %all-gather.5.cloned.1.call-done, f32[170]{0:T(256)S(1)} %fusion.48, f32[1024]{0:T(1024)S(1)} %bitcast.165), kind=kOutput, calls=%fused_computation.75 | convolution fusion | flops 1070069760 | bytes 7688872 | tf_op jit(solution)/shard_map/dot_general | solution.py:1286
  (165 shorter events, 16.2 us)
Async XLA Ops:
  7.2 141.0 %all-gather.3.cloned.1.call-start = ((), (), s32[]{:S(2)}) async-start(), calls=%async_computation.2 | async-start | bytes 9437184 | tf_op jit(solution)/shard_map/all_gather | solution.py:1178
  8.4 4.0 copy-start.30
  8.4 4.0 copy-start.31
  8.4 3.9 copy-start.32
  8.4 3.9 copy-start.33
  8.4 3.9 copy-start.34
  8.4 3.9 copy-start.35
  8.4 3.9 copy-start.36
  8.4 3.9 copy-start.37
  13.1 73.4 %copy-start.29 = (s32[1,512]{1,0:T(1,128)S(1)}, s32[1,512]{1,0:T(1,128)}, u32[]{:S(2)}) copy-start(s32[1,512]{1,0:T(1,128)} %param.30) | copy-start | bytes 6148
  84.2 169.1 %reduce-scatter.3.cloned.1.call-start = ((), (), s32[]{:S(2)}) async-start(), calls=%async_computation.3 | async-start | bytes 7077888 | tf_op jit(solution)/shard_map/reduce_scatter | solution.py:1204
  87.2 26.3 %copy-start.1 = (bf16[1,512,1024]{2,1,0:T(8,128)(2,1)S(1)}, bf16[1,512,1024]{2,1,0:T(8,128)(2,1)}, u32[]{:S(2)}) copy-start(bf16[1,512,1024]{2,1,0:T(8,128)(2,1)} %param.25) | copy-start | bytes 3145732
  87.2 26.3 %copy-start.40 = (bf16[1024,1024]{1,0:T(8,128)(2,1)S(1)}, bf16[1024,1024]{1,0:T(8,128)(2,1)}, u32[]{:S(2)}) copy-start(bf16[1024,1024]{1,0:T(8,128)(2,1)} %get-tuple-element.85) | copy-start | bytes 6291460
  113.5 4.8 %copy-start.38 = (bf16[1024,4096]{1,0:T(8,128)(2,1)S(1)}, bf16[1024,4096]{1,0:T(8,128)(2,1)}, u32[]{:S(2)}) copy-start(bf16[1024,4096]{1,0:T(8,128)(2,1)} %get-tuple-element.88) | copy-start | bytes 25165828
  116.3 64.4 %copy-start.4 = (f32[512,1024]{1,0:T(8,128)}, f32[512,1024]{1,0:T(8,128)S(1)}, u32[]{:S(2)}) copy-start(f32[512,1024]{1,0:T(8,128)S(1)} %get-tuple-element.166) | copy-start | bytes 6291460
  118.3 9.9 %copy-start.25 = (bf16[1,170,1024]{2,1,0:T(8,128)(2,1)S(1)}, bf16[1,170,1024]{2,1,0:T(8,128)(2,1)}, u32[]{:S(2)}) copy-start(bf16[1,170,1024]{2,1,0:T(8,128)(2,1)} %param.49) | copy-start | bytes 1044484
  118.3 10.0 %copy-start.12 = (bf16[1,512,1024]{2,1,0:T(8,128)(2,1)S(1)}, bf16[1,512,1024]{2,1,0:T(8,128)(2,1)}, u32[]{:S(2)}) copy-start(bf16[1,512,1024]{2,1,0:T(8,128)(2,1)} %param.26) | copy-start | bytes 3145732
  148.2 165.1 %reduce-scatter.5.cloned.1.call-start = ((), (), s32[]{:S(2)}) async-start(), calls=%async_computation.5 | async-start | bytes 9437184 | tf_op jit(solution)/shard_map/reduce_scatter | solution.py:1205
  149.0 307.3 %all-gather.5.cloned.1.call-start = ((), (), s32[]{:S(2)}) async-start(), calls=%async_computation.4 | async-start | bytes 7077888 | tf_op jit(solution)/shard_map/all_gather | solution.py:1226
  171.0 9.7 %copy-start.44 = (bf16[512,4096]{1,0:T(8,128)(2,1)}, bf16[512,4096]{1,0:T(8,128)(2,1)S(1)}, u32[]{:S(2)}) copy-start(bf16[512,4096]{1,0:T(8,128)(2,1)S(1)} %get-tuple-element.173) | copy-start | bytes 12582916
  180.7 3.1 copy-start.41
  186.4 46.9 %copy-start.17 = (bf16[1024,1024]{1,0:T(8,128)(2,1)S(1)}, bf16[1024,1024]{1,0:T(8,128)(2,1)}, u32[]{:S(2)}) copy-start(bf16[1024,1024]{1,0:T(8,128)(2,1)} %get-tuple-element.105) | copy-start | bytes 6291460
  229.0 3.9 copy-start.13
  232.8 1.9 copy-start.14
  234.7 2.7 copy-start.39
  241.1 42.4 %copy-start.2 = (bf16[1024,1024]{1,0:T(8,128)(2,1)}, bf16[1024,1024]{1,0:T(8,128)(2,1)S(1)}, u32[]{:S(2)}) copy-start(bf16[1024,1024]{1,0:T(8,128)(2,1)S(1)} %convolution_convert_fusion.6) | copy-start | bytes 6291460
  241.1 4.8 %copy-start.5 = (f32[512,1024]{1,0:T(8,128)S(1)}, f32[512,1024]{1,0:T(8,128)}, u32[]{:S(2)}) copy-start(f32[512,1024]{1,0:T(8,128)} %copy-done.4) | copy-start | bytes 6291460
  241.1 4.8 %copy-start.45 = (bf16[512,4096]{1,0:T(8,128)(2,1)S(1)}, bf16[512,4096]{1,0:T(8,128)(2,1)}, u32[]{:S(2)}) copy-start(bf16[512,4096]{1,0:T(8,128)(2,1)} %copy-done.44) | copy-start | bytes 12582916
  253.4 4.8 %copy-start.24 = (bf16[384,1024]{1,0:T(8,128)(2,1)S(1)}, bf16[384,1024]{1,0:T(8,128)(2,1)}, u32[]{:S(2)}) copy-start(bf16[384,1024]{1,0:T(8,128)(2,1)} %reduce-scatter.3.cloned.1.call-done) | copy-start | bytes 2359300
  253.4 8.6 %copy-start = (bf16[24,64,1024]{2,1,0:T(8,128)(2,1)S(1)}, bf16[24,64,1024]{2,1,0:T(8,128)(2,1)}, u32[]{:S(2)}) copy-start(bf16[24,64,1024]{2,1,0:T(8,128)(2,1)} %add_convert_fusion) | copy-start | bytes 9437188
  253.4 8.6 %copy-start.46 = (bf16[1024,1536]{1,0:T(8,128)(2,1)S(1)}, bf16[1024,1536]{1,0:T(8,128)(2,1)}, u32[]{:S(2)}) copy-start(bf16[1024,1536]{1,0:T(8,128)(2,1)} %get-tuple-element.100) | copy-start | bytes 9437188
  258.2 21.0 %collective-permute-start = (bf16[384,1024]{1,0:T(8,128)(2,1)S(1)}, bf16[384,1024]{1,0:T(8,128)(2,1)S(1)}, u32[]{:S(2)}, u32[]{:S(2)}) collective-permute-start(bf16[384,1024]{1,0:T(8,128)(2,1)S(1)} %copy-done.24), channel_id=1, source_target_pairs={{0,8},{1,9},{2,10},{3,11},{4,12},{5,13},{6,14},{7,15},{24,16},{25,... | collective-permute-start | bytes 2359304 | tf_op jit(solution)/shard_map/ppermute | solution.py:306
  262.0 20.1 %copy-start.11 = (bf16[512,1024]{1,0:T(8,128)(2,1)S(1)}, bf16[512,1024]{1,0:T(8,128)(2,1)}, u32[]{:S(2)}) copy-start(bf16[512,1024]{1,0:T(8,128)(2,1)} %get-tuple-element.103) | copy-start | bytes 3145732
  262.0 20.2 %copy-start.18 = (bf16[1024,1024]{1,0:T(8,128)(2,1)S(1)}, bf16[1024,1024]{1,0:T(8,128)(2,1)}, u32[]{:S(2)}) copy-start(bf16[1024,1024]{1,0:T(8,128)(2,1)} %get-tuple-element.105) | copy-start | bytes 6291460
  266.7 15.6 %copy-start.3 = (bf16[1024,1024]{1,0:T(8,128)(2,1)S(1)}, bf16[1024,1024]{1,0:T(8,128)(2,1)}, u32[]{:S(2)}) copy-start(bf16[1024,1024]{1,0:T(8,128)(2,1)} %convolution_convert_fusion.7) | copy-start | bytes 6291460
  280.4 17.8 %collective-permute-start.1 = (bf16[384,1024]{1,0:T(8,128)(2,1)}, bf16[384,1024]{1,0:T(8,128)(2,1)}, u32[]{:S(2)}, u32[]{:S(2)}) collective-permute-start(bf16[384,1024]{1,0:T(8,128)(2,1)} %add_convert_fusion.4), channel_id=1, source_target_pairs={{8,16},{9,17},{10,18},{11,19},{12,20},{13,21},{14,22},{15,23},{16,... | collective-permute-start | bytes 2359304 | tf_op jit(solution)/shard_map/ppermute | solution.py:306
  282.3 1.6 copy-start.16
  283.9 1.6 copy-start.15
  285.5 6.1 %copy-start.7 = (f32[512,1024]{1,0:T(8,128)S(1)}, f32[512,1024]{1,0:T(8,128)}, u32[]{:S(2)}) copy-start(f32[512,1024]{1,0:T(8,128)} %get-tuple-element.109) | copy-start | bytes 6291460
  291.6 4.7 %copy-start.8 = (f32[512,1024]{1,0:T(8,128)S(1)}, f32[512,1024]{1,0:T(8,128)}, u32[]{:S(2)}) copy-start(f32[512,1024]{1,0:T(8,128)} %get-tuple-element.141) | copy-start | bytes 6291460
  296.3 5.2 %copy-start.43 = (bf16[512,4096]{1,0:T(8,128)(2,1)S(1)}, bf16[512,4096]{1,0:T(8,128)(2,1)}, u32[]{:S(2)}) copy-start(bf16[512,4096]{1,0:T(8,128)(2,1)} %get-tuple-element.108) | copy-start | bytes 12582916
  298.1 3.4 copy-start.6
  300.2 144.4 %collective-permute-start.2 = (bf16[384,1024]{1,0:T(8,128)(2,1)S(1)}, bf16[384,1024]{1,0:T(8,128)(2,1)S(1)}, u32[]{:S(2)}, u32[]{:S(2)}) collective-permute-start(bf16[384,1024]{1,0:T(8,128)(2,1)S(1)} %add_convert_fusion.3), channel_id=1, source_target_pairs={{8,0},{9,1},{10,2},{11,3},{12,4},{13,5},{14,6},{15,7},{16,24},{17,... | collective-permute-start | bytes 2359304 | tf_op jit(solution)/shard_map/ppermute | solution.py:306
  301.5 9.1 %copy-start.20 = (bf16[512,1024]{1,0:T(8,128)(2,1)S(1)}, bf16[512,1024]{1,0:T(8,128)(2,1)}, u32[]{:S(2)}) copy-start(bf16[512,1024]{1,0:T(8,128)(2,1)} %copy-done.19) | copy-start | bytes 3145732
  301.5 9.1 %copy-start.42 = (bf16[512,1024]{1,0:T(8,128)(2,1)S(1)}, bf16[512,1024]{1,0:T(8,128)(2,1)}, u32[]{:S(2)}) copy-start(bf16[512,1024]{1,0:T(8,128)(2,1)} %get-tuple-element.84) | copy-start | bytes 3145732
  442.6 7.4 %copy-start.27 = (bf16[128,1024]{1,0:T(8,128)(2,1)S(1)}, bf16[128,1024]{1,0:T(8,128)(2,1)}, u32[]{:S(2)}) copy-start(bf16[128,1024]{1,0:T(8,128)(2,1)} %get-tuple-element.121) | copy-start | bytes 786436
  442.6 8.2 %copy-start.26 = (bf16[128,1024]{1,0:T(8,128)(2,1)S(1)}, bf16[128,1024]{1,0:T(8,128)(2,1)}, u32[]{:S(2)}) copy-start(bf16[128,1024]{1,0:T(8,128)(2,1)} %get-tuple-element.124) | copy-start | bytes 786436
  442.6 9.0 %copy-start.22 = (bf16[512,1024]{1,0:T(8,128)(2,1)S(1)}, bf16[512,1024]{1,0:T(8,128)(2,1)}, u32[]{:S(2)}) copy-start(bf16[512,1024]{1,0:T(8,128)(2,1)} %get-tuple-element.126) | copy-start | bytes 3145732
  (6 other events, 8.1 us)
Sparse Core Ops, SparseCore 0:
  84.3 54.6 all-gather.2
  148.4 62.6 reduce-scatter.2
  214.9 71.2 reduce-scatter.4
  288.0 54.3 all-gather.4
